TPU v7x, 256 devices: a whole 4x4x8 slice. The times are simulated.
256 devices in a mesh: tile: 64 (over x, z, core), mem: 4 (over y).
Axes of the slice: x: 4, y: 4, z: 8, core: 2. Of those that a mesh axis runs over, the one named last changes fastest.
Arguments:
- control: float32 [64, 64, 32768], P('mem', None, 'tile'), may hold values from -8 to 8
- ensemble: bfloat16 [64, 5, 64, 32768], P('mem', None, None, 'tile'), may hold values from -6 to 6
- jacobian: bfloat16 [640, 320], replicated, may hold values from -0.3125 to 0.3125
- send_columns: int32 [256, 64, 2], P(('tile', 'mem')), may hold values from 0 to 127, as said below
- received_counts: int32 [256, 64], P(('tile', 'mem')), may hold values from 0 to 2, as said below
- observed_channel: int32 [256, 64, 2, 128], P(('tile', 'mem')), may hold values from 0 to 639
- innovation: float32 [256, 64, 2, 128], P(('tile', 'mem')), may hold values from -1.5 to 1.5
- error_weight: float32 [256, 64, 2, 128], P(('tile', 'mem')), may hold values from 1 to 10
Outputs:
- gradient: float32 [64, 64, 32768], P('mem', None, 'tile')
- departures: float32 [256, 64, 2, 128], P(('tile', 'mem'))
Inputs may be any that keep to these rules, and one draw needn't show every extreme that they name: `send_columns`: entry [d, t, j] is a column within the 128 columns of block k of strip s, where d = s * 4 + k; the entries of one row d are distinct. `received_counts`: entry [e, s] counts the used slots, from the first, of the 2 slots that device e receives from tile s. In each mem group one owner receives 2 from every source tile.
All inputs are finite; a program needn't handle non-finite values.
Results may differ from a plain program's by a relative error of at most 0.01.
Values may be sent and summed in bfloat16 or wider, within the bound.
No kernel may reach another device: no remote copies, remote signals or barrier semaphores. Data moves between devices by JAX's collectives and lax.ppermute only.
A program may use at most 64 MiB of HBM per device.

v0:
```python
import math

import jax
import jax.numpy as jnp
from jax import lax
from jax.sharding import PartitionSpec as P

NY = 64


diffusion_coef = 0.2


def extended_2(block, sides, width):
    for axis, dim in sides:
        count = lax.axis_size(axis)
        forward = [(i, i + 1) for i in range(count - 1)]
        backward = [(target, source) for source, target in forward]
        low = lax.ppermute(
            lax.slice_in_dim(block, block.shape[dim] - width, None, axis=dim), axis, forward
        )
        high = lax.ppermute(lax.slice_in_dim(block, 0, width, axis=dim), axis, backward)
        block = jnp.concatenate([low, block, high], axis=dim)
    return block


def y_neighbours(state_field):
    length = state_field.shape[-1]
    position = lax.iota(jnp.int32, length) % NY
    zeros_edge = jnp.zeros(state_field.shape[:-1] + (1,), state_field.dtype)
    upward = jnp.concatenate([state_field[..., 1:], zeros_edge], -1)
    downward = jnp.concatenate([zeros_edge, state_field[..., :-1]], -1)
    return jnp.where(position == NY - 1, 0.0, upward) + jnp.where(position == 0, 0.0, downward)


def widen_with_halo(state_field):
    return extended_2(state_field, (("tile", 2),), NY)


def localize(state_field, tile_index, strip_rows, grid_rows):
    halo_depth = 1
    for sweep_turn in range(4 // halo_depth):
        extended = widen_with_halo(state_field)
        middle = extended[..., NY:-NY]
        swept = middle + diffusion_coef * (
            extended[..., : -2 * NY] + extended[..., 2 * NY :] + y_neighbours(middle) - 4.0 * middle
        )
        first_row = tile_index * strip_rows - (halo_depth - 1)
        domain_wide_row = first_row + lax.iota(jnp.int32, swept.shape[-1]) // NY
        extended = jnp.where((domain_wide_row >= 0) & (domain_wide_row < grid_rows), swept, 0.0)
        state_field = extended
    return state_field


def pick_channels(block):
    model_block, channel_block = block
    channel_ids = lax.iota(jnp.int32, model_block.shape[-1])
    hits = channel_block[:, :, None] == channel_ids[None, None, :]
    return jnp.sum(jnp.where(hits, model_block[:, None, :], 0.0), axis=2)


def spread_channels(block):
    weighted_block, channel_block, channel_count = (block[0], block[1], block[2].shape[-1])
    channel_ids = lax.iota(jnp.int32, channel_count)
    hits = channel_block[:, :, None] == channel_ids[None, None, :]
    return jnp.sum(jnp.where(hits, weighted_block[:, :, None], 0.0), axis=1)


def body(
    control,
    ensemble,
    jacobian,
    send_columns,
    received_counts,
    observed_channel,
    innovation,
    error_weight,
):
    members = control.shape[0] * lax.axis_size("mem")
    member_scale = 1.0 / math.sqrt(members)
    tile_columns = control.shape[2]
    strip_rows = tile_columns // NY
    grid_rows = strip_rows * lax.axis_size("tile")
    tile_index = lax.axis_index("tile")
    state_size = ensemble.shape[1] * ensemble.shape[2]
    channels = jacobian.shape[0]
    localized_member_field = localize(control, tile_index, strip_rows, grid_rows)
    localization_weights = localized_member_field.astype(jnp.bfloat16)
    member_sum = (
        jnp.einsum(
            "teb,tqeb->qeb", localization_weights, ensemble, preferred_element_type=jnp.float32
        )
        * member_scale
    )
    member_sum = member_sum.reshape(state_size, tile_columns)
    block_sum = lax.psum_scatter(member_sum, "mem", scatter_dimension=1, tiled=True).astype(
        jnp.bfloat16
    )
    block_columns = block_sum.shape[1]
    slot_table = send_columns[0]
    owner_count = slot_table.shape[0]
    count_of_slots = slot_table.shape[1]
    row_count = owner_count * count_of_slots
    slot_hits = (
        slot_table.reshape(row_count, 1) == lax.iota(jnp.int32, block_columns)[None, :]
    ).astype(jnp.bfloat16)
    outgoing = jnp.einsum(
        "sc,ic->si", slot_hits, block_sum, preferred_element_type=jnp.float32
    ).astype(jnp.bfloat16)
    incoming = lax.all_to_all(
        outgoing.reshape(owner_count, count_of_slots, state_size),
        "tile",
        split_axis=0,
        concat_axis=0,
        tiled=True,
    )
    model_channels = jnp.dot(
        incoming.reshape(row_count, state_size),
        jnp.transpose(jacobian),
        preferred_element_type=jnp.float32,
    )
    observed_count = observed_channel.shape[-1]
    channel_rows = observed_channel[0].reshape(row_count, observed_count)
    block_count = math.gcd(row_count, 8)
    block_rows = row_count // block_count
    evolved = lax.map(
        pick_channels,
        (
            model_channels.reshape(block_count, block_rows, channels),
            channel_rows.reshape(block_count, block_rows, observed_count),
        ),
    )
    evolved = evolved.reshape(owner_count, count_of_slots, observed_count)
    filled = (
        jnp.arange(count_of_slots, dtype=jnp.int32)[None, :, None]
        < received_counts[0][:, None, None]
    )
    departures = jnp.where(filled, evolved - innovation[0], 0.0)
    weighted = error_weight[0] * departures
    channel_shape = jnp.zeros((block_count, channels), jnp.int32)
    channel_adjoint = lax.map(
        spread_channels,
        (
            weighted.reshape(block_count, block_rows, observed_count),
            channel_rows.reshape(block_count, block_rows, observed_count),
            channel_shape,
        ),
    )
    channel_adjoint = channel_adjoint.reshape(row_count, channels)
    column_adjoint = jnp.dot(
        channel_adjoint.astype(jnp.bfloat16), jacobian, preferred_element_type=jnp.float32
    ).astype(jnp.bfloat16)
    returned = lax.all_to_all(
        column_adjoint.reshape(owner_count, count_of_slots, state_size),
        "tile",
        split_axis=0,
        concat_axis=0,
        tiled=True,
    )
    block_adjoint = jnp.einsum(
        "si,sc->ic",
        returned.reshape(row_count, state_size),
        slot_hits,
        preferred_element_type=jnp.float32,
    ).astype(jnp.bfloat16)
    strip_adjoint = lax.all_gather(block_adjoint, "mem", axis=1, tiled=True)
    analysis_increment_adjoint = strip_adjoint.reshape(
        ensemble.shape[1], ensemble.shape[2], tile_columns
    )
    member_adjoint = (
        jnp.einsum(
            "roug,oug->rug",
            ensemble,
            analysis_increment_adjoint,
            preferred_element_type=jnp.float32,
        )
        * member_scale
    )
    gradient = localize(member_adjoint, tile_index, strip_rows, grid_rows)
    return (gradient, departures[None])


def solution(mesh):
    in_specs = (
        P("mem", None, "tile"),
        P("mem", None, None, "tile"),
        P(),
        P(("tile", "mem"), None, None),
        P(("tile", "mem"), None),
        P(("tile", "mem"), None, None, None),
        P(("tile", "mem"), None, None, None),
        P(("tile", "mem"), None, None, None),
    )
    out_specs = (P("mem", None, "tile"), P(("tile", "mem"), None, None, None))
    return jax.shard_map(body, mesh=mesh, in_specs=in_specs, out_specs=out_specs, check_vma=False)
```

profile of v0, /device:TPU:2, one launch (start us, length us, event | category | flops | bytes accessed | tf_op | source)
XLA Modules:
  0.0 260.8 jit_solution(6287265310948972759)
XLA Ops:
  7.2 2.5 fusion.77
  9.7 7.2 %collective-permute-start.1 = (f32[16,64,64]{2,1,0:T(8,128)}, f32[16,64,64]{2,1,0:T(8,128)S(1)}, u32[]{:S(2)}, u32[]{:S(2)}) collective-permute-start(f32[16,64,64]{2,1,0:T(8,128)} %get-tuple-element.95), channel_id=1, source_target_pairs={{4,0},{8,4},{12,8},{16,12},{20,16},{24,20},{28,24},{32,28},{36,32}... | collective-permute-start | bytes 786440 | tf_op jit(solution)/shard_map/ppermute | solution.py:22
  16.9 1.9 collective-permute-start
  20.2 3.7 %collective-permute-done.1 = f32[16,64,64]{2,1,0:T(8,128)S(1)} collective-permute-done((f32[16,64,64]{2,1,0:T(8,128)}, f32[16,64,64]{2,1,0:T(8,128)S(1)}, u32[]{:S(2)}, u32[]{:S(2)}) %collective-permute-start.1) | collective-permute-done | bytes 262176 | tf_op jit(solution)/shard_map/ppermute | solution.py:22
  23.9 5.8 %collective-permute-done = f32[16,64,64]{2,1,0:T(8,128)S(1)} collective-permute-done((f32[16,64,64]{2,1,0:T(8,128)}, f32[16,64,64]{2,1,0:T(8,128)S(1)}, u32[]{:S(2)}, u32[]{:S(2)}) %collective-permute-start) | collective-permute-done | bytes 262176 | tf_op jit(solution)/shard_map/ppermute | solution.py:19
  29.7 1.8 fusion.48
  31.8 1.9 collective-permute-start.3
  33.7 2.4 collective-permute-start.2
  36.9 3.5 %collective-permute-done.3 = f32[16,64,64]{2,1,0:T(8,128)S(1)} collective-permute-done((f32[16,64,64]{2,1,0:T(8,128)S(1)}, f32[16,64,64]{2,1,0:T(8,128)S(1)}, u32[]{:S(2)}, u32[]{:S(2)}) %collective-permute-start.3) | collective-permute-done | bytes 262176 | tf_op jit(solution)/shard_map/ppermute | solution.py:22
  40.4 5.9 %collective-permute-done.2 = f32[16,64,64]{2,1,0:T(8,128)S(1)} collective-permute-done((f32[16,64,64]{2,1,0:T(8,128)S(1)}, f32[16,64,64]{2,1,0:T(8,128)S(1)}, u32[]{:S(2)}, u32[]{:S(2)}) %collective-permute-start.2) | collective-permute-done | bytes 262176 | tf_op jit(solution)/shard_map/ppermute | solution.py:19
  46.3 1.8 fusion.42
  48.3 1.9 collective-permute-start.5
  50.3 2.4 collective-permute-start.4
  53.4 3.5 %collective-permute-done.5 = f32[16,64,64]{2,1,0:T(8,128)S(1)} collective-permute-done((f32[16,64,64]{2,1,0:T(8,128)S(1)}, f32[16,64,64]{2,1,0:T(8,128)S(1)}, u32[]{:S(2)}, u32[]{:S(2)}) %collective-permute-start.5) | collective-permute-done | bytes 262176 | tf_op jit(solution)/shard_map/ppermute | solution.py:22
  56.9 5.9 %collective-permute-done.4 = f32[16,64,64]{2,1,0:T(8,128)S(1)} collective-permute-done((f32[16,64,64]{2,1,0:T(8,128)S(1)}, f32[16,64,64]{2,1,0:T(8,128)S(1)}, u32[]{:S(2)}, u32[]{:S(2)}) %collective-permute-start.4) | collective-permute-done | bytes 262176 | tf_op jit(solution)/shard_map/ppermute | solution.py:19
  62.9 1.8 fusion.36
  64.9 1.9 collective-permute-start.7
  66.8 2.6 collective-permute-start.6
  70.2 3.3 %collective-permute-done.7 = f32[16,64,64]{2,1,0:T(8,128)S(1)} collective-permute-done((f32[16,64,64]{2,1,0:T(8,128)S(1)}, f32[16,64,64]{2,1,0:T(8,128)S(1)}, u32[]{:S(2)}, u32[]{:S(2)}) %collective-permute-start.7) | collective-permute-done | bytes 262176 | tf_op jit(solution)/shard_map/ppermute | solution.py:22
  73.5 5.9 %collective-permute-done.6 = f32[16,64,64]{2,1,0:T(8,128)S(1)} collective-permute-done((f32[16,64,64]{2,1,0:T(8,128)S(1)}, f32[16,64,64]{2,1,0:T(8,128)S(1)}, u32[]{:S(2)}, u32[]{:S(2)}) %collective-permute-start.6) | collective-permute-done | bytes 262176 | tf_op jit(solution)/shard_map/ppermute | solution.py:19
  79.4 1.8 bitcast_convert_fusion
  81.3 1.1 multiply_reduce_fusion.1
  82.4 0.9 broadcast_multiply_fusion
  85.2 19.2 %reduce-scatter.2.cloned.1.call-done = f32[320,128]{1,0:T(8,128)} async-done(((f32[320,512]{1,0:T(8,128)}), f32[320,128]{1,0:T(8,128)}) %reduce-scatter.2.cloned.1.call-update) | async-done | bytes 163856 | tf_op jit(solution)/shard_map/reduce_scatter | solution.py:96
  104.4 1.2 convolution_convert_fusion.2
  106.4 10.5 %all-to-all-start = ((bf16[64,2,320]{2,1,0:T(2,128)(2,1)}), bf16[64,2,320]{2,1,0:T(2,128)(2,1)S(1)}, u32[]{:S(2)}, u32[]{:S(2)}) async-start(bf16[64,2,320]{2,1,0:T(2,128)(2,1)} %reshape.78), calls=%async_computation.1 | async-start | bytes 196608 | tf_op jit(solution)/shard_map/all_to_all | solution.py:110
  117.0 9.1 %all-to-all-done = bf16[64,2,320]{2,1,0:T(2,128)(2,1)S(1)} async-done(((bf16[64,2,320]{2,1,0:T(2,128)(2,1)}), bf16[64,2,320]{2,1,0:T(2,128)(2,1)S(1)}, u32[]{:S(2)}, u32[]{:S(2)}) %all-to-all-start) | async-done | bytes 81952 | tf_op jit(solution)/shard_map/all_to_all | solution.py:110
  126.5 13.9 %while.22 = (s32[]{:T(128)}, f32[8,16,128]{2,1,0:T(8,128)S(1)}, s32[8,16,128]{2,1,0:T(8,128)}, f32[8,16,640]{2,1,0:T(8,128)S(1)}) while((s32[]{:T(128)}, f32[8,16,128]{2,1,0:T(8,128)S(1)}, s32[8,16,128]{2,1,0:T(8,128)}, f32[8,16,640]{2,1,0:T(8,128)S(1)}) %tuple.66), condition=%wide.region_3.4_spmd.clone, body=%wide.region_1.3_spmd.sunk.clone | while | flops 3930114 | bytes 172105 | solution.py:126
  127.3 1.0 select_reduce_fusion.6
  129.0 1.0 select_reduce_fusion.6
  130.7 1.0 select_reduce_fusion.6
  132.5 1.0 select_reduce_fusion.6
  134.2 1.0 select_reduce_fusion.6
  135.9 1.0 select_reduce_fusion.6
  137.7 1.0 select_reduce_fusion.6
  139.4 1.0 select_reduce_fusion.6
  140.5 13.1 %while.23 = (s32[]{:T(128)}, bf16[8,16,640]{2,1,0:T(8,128)(2,1)S(1)}, s32[8,16,128]{2,1,0:T(8,128)}, f32[8,16,128]{2,1,0:T(8,128)S(1)}) while((s32[]{:T(128)}, bf16[8,16,640]{2,1,0:T(8,128)(2,1)S(1)}, s32[8,16,128]{2,1,0:T(8,128)}, f32[8,16,128]{2,1,0:T(8,128)S(1)}) %tuple.67), condition=%wide.region_6.7_spmd.clone, body=%wide.region_4.6_spmd.sunk.clone | while | flops 3921922 | bytes 110665 | solution.py:141
  141.3 0.9 select_reduce_fusion.7
  142.9 0.9 select_reduce_fusion.7
  147.8 0.9 select_reduce_fusion.7
  154.8 5.5 %all-to-all-start.1 = ((bf16[64,2,320]{2,1,0:T(2,128)(2,1)}), bf16[64,2,320]{2,1,0:T(2,128)(2,1)S(1)}, u32[]{:S(2)}, u32[]{:S(2)}) async-start(bf16[64,2,320]{2,1,0:T(2,128)(2,1)} %reshape.79), calls=%async_computation.2 | async-start | bytes 196608 | tf_op jit(solution)/shard_map/all_to_all | solution.py:153
  161.1 8.5 %all-to-all-done.1 = bf16[64,2,320]{2,1,0:T(2,128)(2,1)S(1)} async-done(((bf16[64,2,320]{2,1,0:T(2,128)(2,1)}), bf16[64,2,320]{2,1,0:T(2,128)(2,1)S(1)}, u32[]{:S(2)}, u32[]{:S(2)}) %all-to-all-start.1) | async-done | bytes 81952 | tf_op jit(solution)/shard_map/all_to_all | solution.py:153
  169.8 12.2 %all_gather.3 = bf16[320,512]{1,0:T(8,128)(2,1)S(1)} all-gather(bf16[320,128]{1,0:T(8,128)(2,1)S(1)} %convolution_convert_fusion), channel_id=1, replica_groups=mesh['tile'=64,'mem'=4] {'mem'}, dimensions={1}, use_global_device_ids=true | all-gather | bytes 409600 | tf_op jit(solution)/shard_map/all_gather | solution.py:166
  182.1 3.9 %multiply_reduce_fusion = f32[64,512,16]{1,0,2:T(8,128)S(1)} fusion(f32[64,512,5]{1,0,2:T(8,128)S(1)} %convert.2, bf16[16,5,64,512]{3,2,1,0:T(8,128)(2,1)} %param.13), kind=kLoop, calls=%fused_computation.10 | loop fusion | flops 7340032 | bytes 7995392 | tf_op jit(solution)/shard_map/roug,oug->rug/dot_general | solution.py:171
  186.5 1.9 collective-permute-start.9
  188.4 2.6 %collective-permute-start.8 = (f32[16,64,64]{2,1,0:T(8,128)S(1)}, f32[16,64,64]{2,1,0:T(8,128)S(1)}, u32[]{:S(2)}, u32[]{:S(2)}) collective-permute-start(f32[16,64,64]{2,1,0:T(8,128)S(1)} %get-tuple-element.78), channel_id=1, source_target_pairs={{0,4},{4,8},{8,12},{12,16},{16,20},{20,24},{24,28},{28,32},{32,36}... | collective-permute-start | bytes 786440 | tf_op jit(solution)/shard_map/ppermute | solution.py:19
  191.8 3.3 %collective-permute-done.9 = f32[16,64,64]{2,1,0:T(8,128)S(1)} collective-permute-done((f32[16,64,64]{2,1,0:T(8,128)S(1)}, f32[16,64,64]{2,1,0:T(8,128)S(1)}, u32[]{:S(2)}, u32[]{:S(2)}) %collective-permute-start.9) | collective-permute-done | bytes 262176 | tf_op jit(solution)/shard_map/ppermute | solution.py:22
  195.1 6.0 %collective-permute-done.8 = f32[16,64,64]{2,1,0:T(8,128)S(1)} collective-permute-done((f32[16,64,64]{2,1,0:T(8,128)S(1)}, f32[16,64,64]{2,1,0:T(8,128)S(1)}, u32[]{:S(2)}, u32[]{:S(2)}) %collective-permute-start.8) | collective-permute-done | bytes 262176 | tf_op jit(solution)/shard_map/ppermute | solution.py:19
  201.1 1.8 fusion.23
  203.1 1.9 collective-permute-start.11
  205.0 2.4 collective-permute-start.10
  208.3 3.5 %collective-permute-done.11 = f32[16,64,64]{2,1,0:T(8,128)S(1)} collective-permute-done((f32[16,64,64]{2,1,0:T(8,128)S(1)}, f32[16,64,64]{2,1,0:T(8,128)S(1)}, u32[]{:S(2)}, u32[]{:S(2)}) %collective-permute-start.11) | collective-permute-done | bytes 262176 | tf_op jit(solution)/shard_map/ppermute | solution.py:22
  211.7 5.9 %collective-permute-done.10 = f32[16,64,64]{2,1,0:T(8,128)S(1)} collective-permute-done((f32[16,64,64]{2,1,0:T(8,128)S(1)}, f32[16,64,64]{2,1,0:T(8,128)S(1)}, u32[]{:S(2)}, u32[]{:S(2)}) %collective-permute-start.10) | collective-permute-done | bytes 262176 | tf_op jit(solution)/shard_map/ppermute | solution.py:19
  217.6 1.9 fusion.17
  219.7 1.9 collective-permute-start.13
  221.7 2.4 collective-permute-start.12
  224.8 3.5 %collective-permute-done.13 = f32[16,64,64]{2,1,0:T(8,128)S(1)} collective-permute-done((f32[16,64,64]{2,1,0:T(8,128)S(1)}, f32[16,64,64]{2,1,0:T(8,128)S(1)}, u32[]{:S(2)}, u32[]{:S(2)}) %collective-permute-start.13) | collective-permute-done | bytes 262176 | tf_op jit(solution)/shard_map/ppermute | solution.py:22
  228.3 5.9 %collective-permute-done.12 = f32[16,64,64]{2,1,0:T(8,128)S(1)} collective-permute-done((f32[16,64,64]{2,1,0:T(8,128)S(1)}, f32[16,64,64]{2,1,0:T(8,128)S(1)}, u32[]{:S(2)}, u32[]{:S(2)}) %collective-permute-start.12) | collective-permute-done | bytes 262176 | tf_op jit(solution)/shard_map/ppermute | solution.py:19
  234.3 1.8 fusion.11
  236.3 1.9 collective-permute-start.15
  238.2 2.4 collective-permute-start.14
  241.4 3.5 %collective-permute-done.15 = f32[16,64,64]{2,1,0:T(8,128)S(1)} collective-permute-done((f32[16,64,64]{2,1,0:T(8,128)S(1)}, f32[16,64,64]{2,1,0:T(8,128)S(1)}, u32[]{:S(2)}, u32[]{:S(2)}) %collective-permute-start.15) | collective-permute-done | bytes 262176 | tf_op jit(solution)/shard_map/ppermute | solution.py:22
  244.9 5.9 %collective-permute-done.14 = f32[16,64,64]{2,1,0:T(8,128)S(1)} collective-permute-done((f32[16,64,64]{2,1,0:T(8,128)S(1)}, f32[16,64,64]{2,1,0:T(8,128)S(1)}, u32[]{:S(2)}, u32[]{:S(2)}) %collective-permute-start.14) | collective-permute-done | bytes 262176 | tf_op jit(solution)/shard_map/ppermute | solution.py:19
  250.8 3.1 %fusion.5 = f32[16,64,512]{2,1,0:T(8,128)} fusion(f32[16,64,512]{2,1,0:T(8,128)S(1)} %fusion.11, f32[16,64,64]{2,1,0:T(8,128)S(1)} %collective-permute-done.15, f32[16,64,64]{2,1,0:T(8,128)S(1)} %collective-permute-done.14, f32[16,64,511]{2,1,0:T(8,128)S(1)} %get-tuple-element.65, f32[16,64,511]{2,1,0:T(8,128)S(1)} %get-tuple-element.64, ...), kind=kLoop, calls=%fused_computation.18 | loop fusion | flops 6291456 | bytes 8906240 | tf_op jit(solution)/shard_map/jit(_where)/select_n | solution.py:50
  (130 shorter events, 29.9 us)
Async XLA Ops:
  7.2 119.1 %copy-start = (bf16[640,320]{0,1:T(8,128)(2,1)S(1)}, bf16[640,320]{0,1:T(8,128)(2,1)}, u32[]{:S(2)}) copy-start(bf16[640,320]{0,1:T(8,128)(2,1)} %param.14) | copy-start | bytes 1228804
  7.2 12.2 %copy-start.2 = (f32[16,64,512]{2,1,0:T(8,128)S(1)}, f32[16,64,512]{2,1,0:T(8,128)}, u32[]{:S(2)}) copy-start(f32[16,64,512]{2,1,0:T(8,128)} %param.12) | copy-start | bytes 6291460
  7.2 97.2 %reduce-scatter.2.cloned.1.call-start = ((), (), s32[]{:S(2)}) async-start(), calls=%async_computation.3 | async-start | bytes 819200 | tf_op jit(solution)/shard_map/reduce_scatter | solution.py:96
  9.7 14.2 %collective-permute-start.1 = (f32[16,64,64]{2,1,0:T(8,128)}, f32[16,64,64]{2,1,0:T(8,128)S(1)}, u32[]{:S(2)}, u32[]{:S(2)}) collective-permute-start(f32[16,64,64]{2,1,0:T(8,128)} %get-tuple-element.95), channel_id=1, source_target_pairs={{4,0},{8,4},{12,8},{16,12},{20,16},{24,20},{28,24},{32,28},{36,32}... | collective-permute-start | bytes 786440 | tf_op jit(solution)/shard_map/ppermute | solution.py:22
  16.9 12.8 %collective-permute-start = (f32[16,64,64]{2,1,0:T(8,128)}, f32[16,64,64]{2,1,0:T(8,128)S(1)}, u32[]{:S(2)}, u32[]{:S(2)}) collective-permute-start(f32[16,64,64]{2,1,0:T(8,128)} %get-tuple-element.94), channel_id=1, source_target_pairs={{0,4},{4,8},{8,12},{12,16},{16,20},{20,24},{24,28},{28,32},{32,36}... | collective-permute-start | bytes 786440 | tf_op jit(solution)/shard_map/ppermute | solution.py:19
  19.4 60.1 %copy-start.7 = (pred[512]{0:T(512)(128)(4,1)}, pred[512]{0:T(512)(128)(4,1)S(1)}, u32[]{:S(2)}) copy-start(pred[512]{0:T(512)(128)(4,1)S(1)} %get-tuple-element.96) | copy-start | bytes 1540
  19.4 60.1 %copy-start.9 = (pred[512]{0:T(512)(128)(4,1)}, pred[512]{0:T(512)(128)(4,1)S(1)}, u32[]{:S(2)}) copy-start(pred[512]{0:T(512)(128)(4,1)S(1)} %get-tuple-element.97) | copy-start | bytes 1540
  19.4 10.3 %copy-start.5 = (pred[512]{0:T(512)(128)(4,1)S(1)}, pred[512]{0:T(512)(128)(4,1)}, u32[]{:S(2)}) copy-start(pred[512]{0:T(512)(128)(4,1)} %broadcast_compare_fusion.2) | copy-start | bytes 1540
  31.8 8.6 %collective-permute-start.3 = (f32[16,64,64]{2,1,0:T(8,128)S(1)}, f32[16,64,64]{2,1,0:T(8,128)S(1)}, u32[]{:S(2)}, u32[]{:S(2)}) collective-permute-start(f32[16,64,64]{2,1,0:T(8,128)S(1)} %get-tuple-element.91), channel_id=1, source_target_pairs={{4,0},{8,4},{12,8},{16,12},{20,16},{24,20},{28,24},{32,28},{36,32}... | collective-permute-start | bytes 786440 | tf_op jit(solution)/shard_map/ppermute | solution.py:22
  33.7 12.6 %collective-permute-start.2 = (f32[16,64,64]{2,1,0:T(8,128)S(1)}, f32[16,64,64]{2,1,0:T(8,128)S(1)}, u32[]{:S(2)}, u32[]{:S(2)}) collective-permute-start(f32[16,64,64]{2,1,0:T(8,128)S(1)} %get-tuple-element.90), channel_id=1, source_target_pairs={{0,4},{4,8},{8,12},{12,16},{16,20},{20,24},{24,28},{28,32},{32,36}... | collective-permute-start | bytes 786440 | tf_op jit(solution)/shard_map/ppermute | solution.py:19
  48.3 8.6 %collective-permute-start.5 = (f32[16,64,64]{2,1,0:T(8,128)S(1)}, f32[16,64,64]{2,1,0:T(8,128)S(1)}, u32[]{:S(2)}, u32[]{:S(2)}) collective-permute-start(f32[16,64,64]{2,1,0:T(8,128)S(1)} %get-tuple-element.87), channel_id=1, source_target_pairs={{4,0},{8,4},{12,8},{16,12},{20,16},{24,20},{28,24},{32,28},{36,32}... | collective-permute-start | bytes 786440 | tf_op jit(solution)/shard_map/ppermute | solution.py:22
  50.3 12.6 %collective-permute-start.4 = (f32[16,64,64]{2,1,0:T(8,128)S(1)}, f32[16,64,64]{2,1,0:T(8,128)S(1)}, u32[]{:S(2)}, u32[]{:S(2)}) collective-permute-start(f32[16,64,64]{2,1,0:T(8,128)S(1)} %get-tuple-element.86), channel_id=1, source_target_pairs={{0,4},{4,8},{8,12},{12,16},{16,20},{20,24},{24,28},{28,32},{32,36}... | collective-permute-start | bytes 786440 | tf_op jit(solution)/shard_map/ppermute | solution.py:19
  64.9 8.6 %collective-permute-start.7 = (f32[16,64,64]{2,1,0:T(8,128)S(1)}, f32[16,64,64]{2,1,0:T(8,128)S(1)}, u32[]{:S(2)}, u32[]{:S(2)}) collective-permute-start(f32[16,64,64]{2,1,0:T(8,128)S(1)} %get-tuple-element.81), channel_id=1, source_target_pairs={{4,0},{8,4},{12,8},{16,12},{20,16},{24,20},{28,24},{32,28},{36,32}... | collective-permute-start | bytes 786440 | tf_op jit(solution)/shard_map/ppermute | solution.py:22
  66.8 12.6 %collective-permute-start.6 = (f32[16,64,64]{2,1,0:T(8,128)S(1)}, f32[16,64,64]{2,1,0:T(8,128)S(1)}, u32[]{:S(2)}, u32[]{:S(2)}) collective-permute-start(f32[16,64,64]{2,1,0:T(8,128)S(1)} %get-tuple-element.80), channel_id=1, source_target_pairs={{0,4},{4,8},{8,12},{12,16},{16,20},{20,24},{24,28},{28,32},{32,36}... | collective-permute-start | bytes 786440 | tf_op jit(solution)/shard_map/ppermute | solution.py:19
  69.4 11.9 %slice-start = ((s8[5242880]{0:T(1024)(128)(4,1)}), s8[4194304]{0:T(1024)(128)(4,1)S(1)}, s32[]{:S(2)}) async-start(s8[5242880]{0:T(1024)(128)(4,1)} %bitcast.60), calls=%async_computation.4 | async-start | bytes 8388608
  79.4 1.8 slice-start.1
  81.3 2.1 copy-start.11
  81.3 2.9 %copy-start.12 = (s32[1,64]{1,0:T(1,128)S(1)}, s32[1,64]{1,0:T(1,128)}, u32[]{:S(2)}) copy-start(s32[1,64]{1,0:T(1,128)} %param.16) | copy-start | bytes 772
  83.3 57.1 %copy-start.3 = (f32[1,64,2,128]{3,2,1,0:T(2,128)S(1)}, f32[1,64,2,128]{3,2,1,0:T(2,128)}, u32[]{:S(2)}) copy-start(f32[1,64,2,128]{3,2,1,0:T(2,128)} %param.18) | copy-start | bytes 196612
  83.3 57.1 %copy-start.4 = (f32[1,64,2,128]{3,2,1,0:T(2,128)S(1)}, f32[1,64,2,128]{3,2,1,0:T(2,128)}, u32[]{:S(2)}) copy-start(f32[1,64,2,128]{3,2,1,0:T(2,128)} %param.19) | copy-start | bytes 196612
  106.4 19.7 %all-to-all-start = ((bf16[64,2,320]{2,1,0:T(2,128)(2,1)}), bf16[64,2,320]{2,1,0:T(2,128)(2,1)S(1)}, u32[]{:S(2)}, u32[]{:S(2)}) async-start(bf16[64,2,320]{2,1,0:T(2,128)(2,1)} %reshape.78), calls=%async_computation.1 | async-start | bytes 196608 | tf_op jit(solution)/shard_map/all_to_all | solution.py:110
  154.8 14.7 %all-to-all-start.1 = ((bf16[64,2,320]{2,1,0:T(2,128)(2,1)}), bf16[64,2,320]{2,1,0:T(2,128)(2,1)S(1)}, u32[]{:S(2)}, u32[]{:S(2)}) async-start(bf16[64,2,320]{2,1,0:T(2,128)(2,1)} %reshape.79), calls=%async_computation.2 | async-start | bytes 196608 | tf_op jit(solution)/shard_map/all_to_all | solution.py:153
  186.5 8.6 %collective-permute-start.9 = (f32[16,64,64]{2,1,0:T(8,128)S(1)}, f32[16,64,64]{2,1,0:T(8,128)S(1)}, u32[]{:S(2)}, u32[]{:S(2)}) collective-permute-start(f32[16,64,64]{2,1,0:T(8,128)S(1)} %get-tuple-element.79), channel_id=1, source_target_pairs={{4,0},{8,4},{12,8},{16,12},{20,16},{24,20},{28,24},{32,28},{36,32}... | collective-permute-start | bytes 786440 | tf_op jit(solution)/shard_map/ppermute | solution.py:22
  188.4 12.6 %copy-start.6 = (pred[512]{0:T(512)(128)(4,1)S(1)}, pred[512]{0:T(512)(128)(4,1)}, u32[]{:S(2)}) copy-start(pred[512]{0:T(512)(128)(4,1)} %broadcast_compare_fusion.2) | copy-start | bytes 1540
  188.4 12.6 %copy-start.8 = (pred[512]{0:T(512)(128)(4,1)S(1)}, pred[512]{0:T(512)(128)(4,1)}, u32[]{:S(2)}) copy-start(pred[512]{0:T(512)(128)(4,1)} %copy-done.7) | copy-start | bytes 1540
  188.4 12.6 %copy-start.10 = (pred[512]{0:T(512)(128)(4,1)S(1)}, pred[512]{0:T(512)(128)(4,1)}, u32[]{:S(2)}) copy-start(pred[512]{0:T(512)(128)(4,1)} %copy-done.9) | copy-start | bytes 1540
  188.4 12.6 %collective-permute-start.8 = (f32[16,64,64]{2,1,0:T(8,128)S(1)}, f32[16,64,64]{2,1,0:T(8,128)S(1)}, u32[]{:S(2)}, u32[]{:S(2)}) collective-permute-start(f32[16,64,64]{2,1,0:T(8,128)S(1)} %get-tuple-element.78), channel_id=1, source_target_pairs={{0,4},{4,8},{8,12},{12,16},{16,20},{20,24},{24,28},{28,32},{32,36}... | collective-permute-start | bytes 786440 | tf_op jit(solution)/shard_map/ppermute | solution.py:19
  203.1 8.6 %collective-permute-start.11 = (f32[16,64,64]{2,1,0:T(8,128)S(1)}, f32[16,64,64]{2,1,0:T(8,128)S(1)}, u32[]{:S(2)}, u32[]{:S(2)}) collective-permute-start(f32[16,64,64]{2,1,0:T(8,128)S(1)} %get-tuple-element.75), channel_id=1, source_target_pairs={{4,0},{8,4},{12,8},{16,12},{20,16},{24,20},{28,24},{32,28},{36,32}... | collective-permute-start | bytes 786440 | tf_op jit(solution)/shard_map/ppermute | solution.py:22
  205.0 12.6 %collective-permute-start.10 = (f32[16,64,64]{2,1,0:T(8,128)S(1)}, f32[16,64,64]{2,1,0:T(8,128)S(1)}, u32[]{:S(2)}, u32[]{:S(2)}) collective-permute-start(f32[16,64,64]{2,1,0:T(8,128)S(1)} %get-tuple-element.74), channel_id=1, source_target_pairs={{0,4},{4,8},{8,12},{12,16},{16,20},{20,24},{24,28},{28,32},{32,36}... | collective-permute-start | bytes 786440 | tf_op jit(solution)/shard_map/ppermute | solution.py:19
  219.7 8.6 %collective-permute-start.13 = (f32[16,64,64]{2,1,0:T(8,128)S(1)}, f32[16,64,64]{2,1,0:T(8,128)S(1)}, u32[]{:S(2)}, u32[]{:S(2)}) collective-permute-start(f32[16,64,64]{2,1,0:T(8,128)S(1)} %get-tuple-element.71), channel_id=1, source_target_pairs={{4,0},{8,4},{12,8},{16,12},{20,16},{24,20},{28,24},{32,28},{36,32}... | collective-permute-start | bytes 786440 | tf_op jit(solution)/shard_map/ppermute | solution.py:22
  221.7 12.6 %collective-permute-start.12 = (f32[16,64,64]{2,1,0:T(8,128)S(1)}, f32[16,64,64]{2,1,0:T(8,128)S(1)}, u32[]{:S(2)}, u32[]{:S(2)}) collective-permute-start(f32[16,64,64]{2,1,0:T(8,128)S(1)} %get-tuple-element.70), channel_id=1, source_target_pairs={{0,4},{4,8},{8,12},{12,16},{16,20},{20,24},{24,28},{28,32},{32,36}... | collective-permute-start | bytes 786440 | tf_op jit(solution)/shard_map/ppermute | solution.py:19
  236.3 8.6 %collective-permute-start.15 = (f32[16,64,64]{2,1,0:T(8,128)S(1)}, f32[16,64,64]{2,1,0:T(8,128)S(1)}, u32[]{:S(2)}, u32[]{:S(2)}) collective-permute-start(f32[16,64,64]{2,1,0:T(8,128)S(1)} %get-tuple-element.67), channel_id=1, source_target_pairs={{4,0},{8,4},{12,8},{16,12},{20,16},{24,20},{28,24},{32,28},{36,32}... | collective-permute-start | bytes 786440 | tf_op jit(solution)/shard_map/ppermute | solution.py:22
  238.2 12.6 %collective-permute-start.14 = (f32[16,64,64]{2,1,0:T(8,128)S(1)}, f32[16,64,64]{2,1,0:T(8,128)S(1)}, u32[]{:S(2)}, u32[]{:S(2)}) collective-permute-start(f32[16,64,64]{2,1,0:T(8,128)S(1)} %get-tuple-element.66), channel_id=1, source_target_pairs={{0,4},{4,8},{8,12},{12,16},{16,20},{20,24},{24,28},{28,32},{32,36}... | collective-permute-start | bytes 786440 | tf_op jit(solution)/shard_map/ppermute | solution.py:19
  250.8 3.2 %copy-start.1 = (bf16[640,320]{0,1:T(8,128)(2,1)S(1)}, bf16[640,320]{0,1:T(8,128)(2,1)}, u32[]{:S(2)}) copy-start(bf16[640,320]{0,1:T(8,128)(2,1)} %param.14) | copy-start | bytes 1228804
Sparse Core Ops, SparseCore 0:
  83.5 20.9 reduce-scatter.1
where the time goes:
time: 262 us; the launch traced here: 261 us
  waiting for transfers between devices  112 us (43%)
  starting transfers between devices  55.8 us (21%)
  other arithmetic  39.2 us (15%)
  local copies, waits for them, and re-layouts  24.7 us (9%)
  between operations  14.6 us (6%)
  blocking collectives  12.2 us (5%)
    ppermute x8, waiting for transfers between devices, extended_2(): lax.ppermute(lax.slice_in_dim(block, block.shape[dim] - width, None, axis...  47.4 us
    ppermute x8, waiting for transfers between devices, extended_2(): lax.ppermute(lax.slice_in_dim(block, 0, width, axis=dim), axis, backward)  27.7 us
    ppermute x8, starting transfers between devices, extended_2(): lax.ppermute(lax.slice_in_dim(block, 0, width, axis=dim), axis, backward)  20.6 us
    reduce_scatter x1, waiting for transfers between devices, body(): lax.psum_scatter(member_sum, 'mem', scatter_dimension=1, tiled=True)  19.2 us
    ppermute x8, starting transfers between devices, extended_2(): lax.ppermute(lax.slice_in_dim(block, block.shape[dim] - width, None, axis...  19.2 us
    select_n x7, other arithmetic, localize(): jnp.where((domain_wide_row >= 0) & (domain_wide_row < grid_rows), swept,...  14.1 us
    all_gather x1, blocking collectives, body(): strip_adjoint = lax.all_gather(block_adjoint, 'mem', axis=1, tiled=True)  12.2 us
    all_to_all x1, starting transfers between devices, body(): lax.all_to_all(outgoing.reshape(owner_count, count_of_slots, state_size),...  10.5 us
  transfers between devices with their start and end apart: 19, of which 19 were waited for; matrix products, arithmetic and copies ran while one was open for 4% of the time, Pallas kernels for 0%

commit v1 on v0

v1 whole, which is shorter than its diff:
```python
import functools
import math

import jax
import jax.numpy as jnp
import numpy as np
from jax import lax
from jax.experimental import pallas as pl
from jax.experimental.pallas import tpu as pltpu
from jax.sharding import PartitionSpec as P

NY = 64
SWEEPS = 4
DIFFUSION = 0.2
HALF = SWEEPS * NY

CONTROL_STEP = 8.0 / 32704.0
INNOVATION_STEP = 1.5 / 32700.0
WEIGHT_STEP = 10.0 / 32700.0

F32 = jnp.float32
BF16 = jnp.bfloat16
I16 = jnp.int16
I32 = jnp.int32


def sweep_matrices():
    y_part = (1.0 - 4.0 * DIFFUSION) * np.eye(NY) + DIFFUSION * (
        np.eye(NY, k=1) + np.eye(NY, k=-1)
    )
    powers = [np.linalg.matrix_power(y_part, n) for n in range(SWEEPS + 1)]
    by_distance = [np.zeros((NY, NY)) for _ in range(SWEEPS + 1)]
    for k in range(SWEEPS + 1):
        for ups in range(k + 1):
            distance = 2 * ups - k
            if distance >= 0:
                by_distance[distance] = by_distance[distance] + (
                    math.comb(SWEEPS, k)
                    * DIFFUSION**k
                    * math.comb(k, ups)
                    * powers[SWEEPS - k]
                )

    def block(distance_of, image_of=None):
        full = np.zeros((HALF, HALF))
        for xi in range(SWEEPS):
            for xo in range(SWEEPS):
                piece = np.zeros((NY, NY))
                if distance_of(xi, xo) <= SWEEPS:
                    piece = piece + by_distance[distance_of(xi, xo)]
                if image_of is not None and image_of(xi, xo) <= SWEEPS:
                    piece = piece - by_distance[image_of(xi, xo)]
                full[xi * NY : (xi + 1) * NY, xo * NY : (xo + 1) * NY] = piece
        return full

    last = SWEEPS - 1
    same = lambda xi, xo: abs(xi - xo)
    blocks = [
        block(same, lambda xi, xo: xi + xo + 2),
        block(same),
        block(same, lambda xi, xo: (last - xi) + (last - xo) + 2),
        block(lambda xi, xo: xo + SWEEPS - xi),
        block(lambda xi, xo: xi + SWEEPS - xo),
    ]
    stacked = np.stack(blocks).astype(np.float32)
    high = stacked.astype(jnp.bfloat16)
    low = (stacked - high.astype(np.float32)).astype(jnp.bfloat16)
    return np.stack([high, low], axis=1)


def split_high_low(values):
    high = values.astype(BF16)
    return high, (values - high.astype(F32)).astype(BF16)


def mm(a, b):
    return jnp.dot(a, b, preferred_element_type=F32)


def mm_nt(a, b):
    return lax.dot_general(a, b, (((1,), (1,)), ((), ())), preferred_element_type=F32)


def params(**extra):
    return pltpu.CompilerParams(vmem_limit_bytes=48 * 1024 * 1024, **extra)


def cost(flops, bytes_accessed):
    return pl.CostEstimate(flops=flops, bytes_accessed=bytes_accessed, transcendentals=0)


def sweep_own_kernel(edge_ref, x_ref, t_left, t_right, t_after, t_before, o_ref):
    left, right = x_ref[:, :HALF], x_ref[:, HALF:]
    left_high, left_low = split_high_low(left)
    right_high, right_low = split_high_low(right)

    def apply(high, low, t_ref):
        return mm(high, t_ref[0, 0]) + mm(low, t_ref[0, 0]) + mm(high, t_ref[0, 1])

    o_ref[:, :HALF] = apply(left_high, left_low, t_left) + apply(right_high, right_low, t_before)
    o_ref[:, HALF:] = apply(right_high, right_low, t_right) + apply(left_high, left_low, t_after)


def sweep_own(edges, field, matrices):
    rows, columns = field.shape
    step = 256
    t_spec = lambda pick: pl.BlockSpec((1, 2, HALF, HALF), pick)
    return pl.pallas_call(
        sweep_own_kernel,
        out_shape=jax.ShapeDtypeStruct((rows, columns), F32),
        grid_spec=pltpu.PrefetchScalarGridSpec(
            num_scalar_prefetch=1,
            grid=(rows // step,),
            in_specs=[
                pl.BlockSpec((step, columns), lambda i, e: (i, 0)),
                t_spec(lambda i, e: (e[0], 0, 0, 0)),
                t_spec(lambda i, e: (e[1], 0, 0, 0)),
                t_spec(lambda i, e: (3, 0, 0, 0)),
                t_spec(lambda i, e: (4, 0, 0, 0)),
            ],
            out_specs=pl.BlockSpec((step, columns), lambda i, e: (i, 0)),
        ),
        compiler_params=params(),
        cost_estimate=cost(2 * 6 * rows * columns * HALF, 10 * rows * columns),
        name="sweep_own",
    )(edges, field, matrices, matrices, matrices, matrices)


def member_sum_kernel(scale, own_ref, low_ref, high_ref, ens_ref, t_after, t_before, o_ref):
    members, levels, columns = own_ref.shape
    variables = ens_ref.shape[1]
    blocks, width = o_ref.shape[0], o_ref.shape[3]
    half_blocks = blocks // 2

    def from_halo(halo_ref, t_ref):
        coded = halo_ref[...].reshape(members * levels, HALF).astype(I32)
        upper = (coded >> 8).astype(F32).astype(BF16)
        lower = (coded & 255).astype(F32).astype(BF16)
        upper_part = mm(upper, t_ref[0, 0]) + mm(upper, t_ref[0, 1])
        lower_part = mm(lower, t_ref[0, 0])
        total = (upper_part * 256.0 + lower_part) * CONTROL_STEP
        return total.reshape(members, levels, HALF)

    halos = [from_halo(low_ref, t_after), from_halo(high_ref, t_before)]
    for k in range(blocks):
        offset = (k % half_blocks) * width
        halo = halos[k // half_blocks][:, :, offset : offset + width]
        weights = own_ref[:, :, k * width : (k + 1) * width] + halo
        weights = weights.astype(BF16).astype(F32)
        for v in range(variables):
            total = None
            for m in range(members):
                term = weights[m] * ens_ref[m, v, :, k * width : (k + 1) * width].astype(F32)
                total = term if total is None else total + term
            o_ref[k, v] = (total * scale).astype(BF16)


def member_sum(own, from_low, from_high, ensemble, matrices, scale, blocks):
    members, variables, levels, columns = ensemble.shape
    step = 16
    width = columns // blocks
    return pl.pallas_call(
        functools.partial(member_sum_kernel, scale),
        out_shape=jax.ShapeDtypeStruct((blocks, variables, levels, width), BF16),
        grid=(levels // step,),
        in_specs=[
            pl.BlockSpec((members, step, columns), lambda i: (0, i, 0)),
            pl.BlockSpec((members, step, HALF), lambda i: (0, i, 0)),
            pl.BlockSpec((members, step, HALF), lambda i: (0, i, 0)),
            pl.BlockSpec((members, variables, step, columns), lambda i: (0, 0, i, 0)),
            pl.BlockSpec((1, 2, HALF, HALF), lambda i: (3, 0, 0, 0)),
            pl.BlockSpec((1, 2, HALF, HALF), lambda i: (4, 0, 0, 0)),
        ],
        out_specs=pl.BlockSpec((blocks, variables, step, width), lambda i: (0, 0, i, 0)),
        compiler_params=params(),
        cost_estimate=cost(
            2 * 3 * members * levels * columns * HALF, 2 * ensemble.size + 6 * own.size
        ),
        name="member_sum",
    )(own, from_low, from_high, ensemble, matrices, matrices)


def obs_tables_kernel(obs_ref, w_ref, b_ref):
    slots, width = obs_ref.shape[0], obs_ref.shape[2]
    groups = w_ref.shape[0]
    group_id = lax.broadcasted_iota(I32, (8, width), 0)
    lane_id = lax.broadcasted_iota(I32, (width, width), 0)

    def one(slot):
        row = obs_ref[slot].astype(I32)
        channel = row[0:1]
        innovation = row[1:2].astype(F32) * INNOVATION_STEP
        weight = row[2:3].astype(F32) * WEIGHT_STEP
        in_group = jnp.broadcast_to(channel >> 7, (8, width)) == group_id
        one_hot = jnp.where(
            jnp.broadcast_to(channel & 127, (width, width)) == lane_id, 1.0, 0.0
        ).astype(BF16)

        def spread(values):
            high, low = split_high_low(values)
            kept = [
                jnp.where(in_group, jnp.broadcast_to(part.astype(F32), (8, width)), 0.0)
                for part in (high, low)
            ]
            return kept

        left = jnp.concatenate(spread(weight) + spread(weight * innovation), axis=0)
        sums = mm_nt(left.astype(BF16), one_hot)
        w_sum = sums[0:8] + sums[8:16]
        b_sum = sums[16:24] + sums[24:32]
        for g in range(groups):
            w_ref[g, pl.ds(slot, 1), :] = w_sum[g : g + 1]
            b_ref[g, pl.ds(slot, 1), :] = b_sum[g : g + 1]

    unroll = 8

    def several(turn, carry):
        for inner in range(unroll):
            one(turn * unroll + inner)
        return carry

    lax.fori_loop(0, slots // unroll, several, 0)


def obs_tables(obs, channels):
    slots, _, width = obs.shape
    shape = jax.ShapeDtypeStruct((channels // width, slots, width), F32)
    return pl.pallas_call(
        obs_tables_kernel,
        out_shape=(shape, shape),
        compiler_params=params(),
        cost_estimate=cost(2 * 32 * slots * width * width, 10 * slots * channels),
        name="obs_tables",
    )(obs)


def observe_kernel(parts_ref, slots_ref, jac_ref, w_ref, b_ref, adj_ref, model_ref):
    count, state, width = parts_ref.shape
    groups = w_ref.shape[0]
    total = parts_ref[0].astype(F32)
    for p in range(1, count):
        total = total + parts_ref[p].astype(F32)
    increment = total.astype(BF16)
    slots = slots_ref.shape[1]
    column_id = lax.broadcasted_iota(I32, (width, slots), 0)
    hits = jnp.where(column_id == jnp.broadcast_to(slots_ref[...], (width, slots)), 1.0, 0.0)
    hits = hits.astype(BF16)
    carried = mm(increment, hits).T.astype(BF16)
    column_adjoint = jnp.zeros((slots, state), F32)
    for g in range(groups):
        jac = jac_ref[g * width : (g + 1) * width, :]
        model = mm_nt(carried, jac)
        model_ref[g] = model
        channel_adjoint = (model * w_ref[g] - b_ref[g]).astype(BF16)
        column_adjoint = column_adjoint + mm(channel_adjoint, jac)
    rounded = column_adjoint.T.astype(BF16)
    adj_ref[...] = mm_nt(rounded, hits).astype(BF16)


def observe(parts, slots, jacobian, w_table, b_table):
    count, state, width = parts.shape
    channels = jacobian.shape[0]
    rows = slots.shape[1]
    return pl.pallas_call(
        observe_kernel,
        out_shape=(
            jax.ShapeDtypeStruct((state, width), BF16),
            jax.ShapeDtypeStruct((channels // width, rows, width), F32),
        ),
        compiler_params=params(),
        cost_estimate=cost(4 * rows * state * channels, 12 * rows * channels),
        name="observe",
    )(parts, slots, jacobian, w_table, b_table)


def pick_kernel(model_ref, obs_ref, o_ref):
    channel = obs_ref[:, 0, :].astype(I32)
    group, lane = channel >> 7, channel & 127
    picked = jnp.zeros(channel.shape, F32)
    for g in range(model_ref.shape[0]):
        taken = jnp.take_along_axis(model_ref[g], lane, axis=1)
        picked = jnp.where(group == g, taken, picked)
    o_ref[...] = picked


def pick(model, obs):
    groups, slots, width = model.shape
    return pl.pallas_call(
        pick_kernel,
        out_shape=jax.ShapeDtypeStruct((slots, width), F32),
        compiler_params=params(),
        cost_estimate=cost(slots * width * 16, 8 * groups * slots * width),
        name="pick",
    )(model, obs)


def member_adjoint_kernel(scale, ens_ref, adj_ref, full_ref, low_ref, high_ref):
    variables = ens_ref.shape[1]
    blocks, width = adj_ref.shape[0], adj_ref.shape[3]
    half_blocks = blocks // 2
    for m in range(ens_ref.shape[0]):
        for k in range(blocks):
            total = None
            for v in range(variables):
                term = ens_ref[m, v, :, k * width : (k + 1) * width].astype(F32) * adj_ref[
                    k, v
                ].astype(F32)
                total = term if total is None else total + term
            total = total * scale
            full_ref[m, :, k * width : (k + 1) * width] = total
            half = low_ref if k < half_blocks else high_ref
            offset = (k % half_blocks) * width
            half[m, :, offset : offset + width] = total.astype(BF16)


def member_adjoint(ensemble, adjoint, scale):
    members, variables, levels, columns = ensemble.shape
    blocks, _, _, width = adjoint.shape
    step = 4
    half = jax.ShapeDtypeStruct((members, levels, HALF), BF16)
    half_spec = pl.BlockSpec((step, levels, HALF), lambda i: (i, 0, 0))
    return pl.pallas_call(
        functools.partial(member_adjoint_kernel, scale),
        out_shape=(jax.ShapeDtypeStruct((members, levels, columns), F32), half, half),
        grid=(members // step,),
        in_specs=[
            pl.BlockSpec((step, variables, levels, columns), lambda i: (i, 0, 0, 0)),
            pl.BlockSpec((blocks, variables, levels, width), lambda i: (0, 0, 0, 0)),
        ],
        out_specs=(
            pl.BlockSpec((step, levels, columns), lambda i: (i, 0, 0)),
            half_spec,
            half_spec,
        ),
        compiler_params=params(),
        cost_estimate=cost(2 * ensemble.size, 4 * ensemble.size),
        name="member_adjoint",
    )(ensemble, adjoint)


def add_halo_kernel(own_ref, low_ref, high_ref, t_after, t_before, o_ref):
    def from_halo(halo_ref, t_ref):
        return mm(halo_ref[...], t_ref[0, 0]) + mm(halo_ref[...], t_ref[0, 1])

    o_ref[:, :HALF] = own_ref[:, :HALF] + from_halo(low_ref, t_after)
    o_ref[:, HALF:] = own_ref[:, HALF:] + from_halo(high_ref, t_before)


def add_halo(own, from_low, from_high, matrices):
    rows, columns = own.shape
    step = 256
    return pl.pallas_call(
        add_halo_kernel,
        out_shape=jax.ShapeDtypeStruct((rows, columns), F32),
        grid=(rows // step,),
        in_specs=[
            pl.BlockSpec((step, columns), lambda i: (i, 0)),
            pl.BlockSpec((step, HALF), lambda i: (i, 0)),
            pl.BlockSpec((step, HALF), lambda i: (i, 0)),
            pl.BlockSpec((1, 2, HALF, HALF), lambda i: (3, 0, 0, 0)),
            pl.BlockSpec((1, 2, HALF, HALF), lambda i: (4, 0, 0, 0)),
        ],
        out_specs=pl.BlockSpec((step, columns), lambda i: (i, 0)),
        compiler_params=params(),
        cost_estimate=cost(2 * 2 * rows * columns * HALF, 10 * rows * columns),
        name="add_halo",
    )(own, from_low, from_high, matrices, matrices)


def swap_halos(low_half, high_half):
    count = lax.axis_size("tile")
    forward = [(i, i + 1) for i in range(count - 1)]
    backward = [(i + 1, i) for i in range(count - 1)]
    from_low = lax.ppermute(high_half, "tile", forward)
    from_high = lax.ppermute(low_half, "tile", backward)
    return from_low, from_high


def coded(values, step):
    return jnp.clip(jnp.round(values * (1.0 / step)), -32767.0, 32767.0).astype(I16)


def body(
    control,
    ensemble,
    jacobian,
    send_columns,
    received_counts,
    observed_channel,
    innovation,
    error_weight,
):
    members, levels, columns = control.shape
    variables = ensemble.shape[1]
    state = variables * levels
    groups = lax.axis_size("mem")
    owners = lax.axis_size("tile")
    scale = 1.0 / math.sqrt(members * groups)
    width = columns // groups
    channels = jacobian.shape[0]
    observed = observed_channel.shape[-1]
    slots = send_columns.shape[-1]
    tile_index = lax.axis_index("tile")
    matrices = jnp.asarray(sweep_matrices())
    edges = jnp.stack(
        [jnp.where(tile_index == 0, 0, 1), jnp.where(tile_index == owners - 1, 2, 1)]
    ).astype(I32)

    from_low, from_high = swap_halos(
        coded(control[:, :, :HALF], CONTROL_STEP), coded(control[:, :, HALF:], CONTROL_STEP)
    )

    filled = (
        jnp.arange(slots, dtype=I32)[None, :, None] < received_counts[0][:, None, None]
    )
    packed = jnp.concatenate(
        [
            observed_channel[0].astype(I16),
            coded(innovation[0], INNOVATION_STEP),
            coded(jnp.where(filled, error_weight[0], 0.0), WEIGHT_STEP),
        ],
        axis=-1,
    )
    obs = lax.all_to_all(packed, "tile", split_axis=0, concat_axis=0, tiled=True)
    obs = obs.reshape(owners * slots, 3, observed)

    own = sweep_own(edges, control.reshape(members * levels, columns), matrices)
    parts = member_sum(
        own.reshape(members, levels, columns),
        from_low,
        from_high,
        ensemble,
        matrices,
        scale,
        groups,
    )
    parts = lax.all_to_all(
        parts.reshape(groups, state, width), "mem", split_axis=0, concat_axis=0, tiled=True
    )
    w_table, b_table = obs_tables(obs, channels)
    block_adjoint, model = observe(
        parts, send_columns.reshape(1, owners * slots), jacobian, w_table, b_table
    )
    adjoint = lax.all_to_all(
        jnp.broadcast_to(block_adjoint[None], (groups, state, width)),
        "mem",
        split_axis=0,
        concat_axis=0,
        tiled=True,
    ).reshape(groups, variables, levels, width)

    evolved = pick(model, obs).reshape(owners, slots, observed)
    evolved = lax.all_to_all(evolved, "tile", split_axis=0, concat_axis=0, tiled=True)
    departures = jnp.where(filled, evolved - innovation[0], 0.0)

    full, low_half, high_half = member_adjoint(ensemble, adjoint, scale)
    from_low, from_high = swap_halos(low_half, high_half)
    own = sweep_own(edges, full.reshape(members * levels, columns), matrices)
    gradient = add_halo(
        own,
        from_low.reshape(members * levels, HALF),
        from_high.reshape(members * levels, HALF),
        matrices,
    )
    return gradient.reshape(members, levels, columns), departures[None]


def solution(mesh):
    in_specs = (
        P("mem", None, "tile"),
        P("mem", None, None, "tile"),
        P(),
        P(("tile", "mem"), None, None),
        P(("tile", "mem"), None),
        P(("tile", "mem"), None, None, None),
        P(("tile", "mem"), None, None, None),
        P(("tile", "mem"), None, None, None),
    )
    out_specs = (P("mem", None, "tile"), P(("tile", "mem"), None, None, None))
    return jax.shard_map(body, mesh=mesh, in_specs=in_specs, out_specs=out_specs, check_vma=False)
```

time: 262 us -> 95.3 us (0.36)
  the two profiles are of different devices: /device:TPU:2 before, /device:TPU:1 now
where the time goes in v1:
time: 95.3 us; the launch traced here: 94.7 us
  starting transfers between devices  30.3 us (32%)
  blocking collectives  28.7 us (30%)
  Pallas kernels  24 us (25%)
  other arithmetic  5.6 us (6%)
  waiting for transfers between devices  3.14 us (3%)
  local copies, waits for them, and re-layouts  2.06 us (2%)
    all_to_all x1, blocking collectives, body(): lax.all_to_all(evolved, 'tile', split_axis=0, concat_axis=0, tiled=True)  20.5 us
    all_to_all x1, starting transfers between devices, body(): lax.all_to_all(packed, 'tile', split_axis=0, concat_axis=0, tiled=True)  11.7 us
    all_to_all x1, blocking collectives, body(): lax.all_to_all(jnp.broadcast_to(block_adjoint[None], (groups, state, widt...  8.25 us
    ppermute x2, starting transfers between devices, swap_halos(): from_low = lax.ppermute(high_half, 'tile', forward)  7.41 us
    ppermute x2, starting transfers between devices, swap_halos(): from_high = lax.ppermute(low_half, 'tile', backward)  7.02 us
    pallas_call x2, Pallas kernels, sweep_own(): pl.pallas_call(sweep_own_kernel, out_shape=jax.ShapeDtypeStruct((rows, co...  5.79 us
    pallas_call x1, Pallas kernels, member_sum(): pl.pallas_call(functools.partial(member_sum_kernel, scale), out_shape=jax...  5.68 us
    all_to_all x1, starting transfers between devices, body(): lax.all_to_all(parts.reshape(groups, state, width), 'mem', split_axis=0,...  4.18 us
  transfers between devices with their start and end apart: 6, of which 2 were waited for; matrix products, arithmetic and copies ran while one was open for 5% of the time, Pallas kernels for 17%

profile of v1, /device:TPU:1, one launch (start us, length us, event | category | flops | bytes accessed | tf_op | source)
XLA Modules:
  0.0 94.7 jit_solution(9577816011131624346)
XLA Ops:
  0.6 0.0 copy-start
  0.6 0.0 copy-start.1
  0.7 3.0 %clamp_convert_fusion = (s16[16,64,256]{2,1,0:T(8,128)(2,1)}, s16[16,64,256]{2,1,0:T(8,128)(2,1)}) fusion(f32[16,64,512]{2,1,0:T(8,128)} %param.9), kind=kLoop, calls=%fused_computation | loop fusion | flops 2097152 | bytes 3145728 | tf_op jit(solution)/shard_map/convert_element_type | solution.py:380
  3.6 5.1 %collective-permute-start.1 = (s16[16,64,256]{2,1,0:T(8,128)(2,1)}, s16[16,64,256]{2,1,0:T(8,128)(2,1)}, u32[]{:S(2)}, u32[]{:S(2)}) collective-permute-start(s16[16,64,256]{2,1,0:T(8,128)(2,1)} %get-tuple-element.20), channel_id=1, source_target_pairs={{4,0},{8,4},{12,8},{16,12},{20,16},{24,20},{28,24},{32,28},{36,32}... | collective-permute-start | bytes 1572872 | tf_op jit(solution)/shard_map/ppermute | solution.py:375
  8.7 1.9 %collective-permute-start = (s16[16,64,256]{2,1,0:T(8,128)(2,1)}, s16[16,64,256]{2,1,0:T(8,128)(2,1)}, u32[]{:S(2)}, u32[]{:S(2)}) collective-permute-start(s16[16,64,256]{2,1,0:T(8,128)(2,1)} %get-tuple-element.21), channel_id=1, source_target_pairs={{0,4},{4,8},{8,12},{12,16},{16,20},{20,24},{24,28},{28,32},{32,36}... | collective-permute-start | bytes 1572872 | tf_op jit(solution)/shard_map/ppermute | solution.py:374
  10.6 0.7 iota_compare_fusion
  11.3 1.0 %fusion.3 = (s16[64,2,128]{2,0,1:T(8,128)(2,1)S(1)}, s16[64,2,128]{2,0,1:T(8,128)(2,1)S(1)}) fusion(f32[1,64,2,128]{3,2,1,0:T(2,128)} %param.16, pred[64,2]{0,1:T(4,128)(4,1)S(1)} %iota_compare_fusion, f32[1,64,2,128]{3,2,1,0:T(2,128)} %param.15), kind=kLoop, calls=%fused_computation.7 | loop fusion | flops 147456 | bytes 196736 | tf_op jit(solution)/shard_map/convert_element_type | solution.py:380
  12.3 0.8 fusion.9
  13.1 0.7 copy.27
  13.9 11.7 %all-to-all-start.1 = ((s16[64,2,384]{2,1,0:T(2,128)(2,1)}), s16[64,2,384]{2,1,0:T(2,128)(2,1)S(1)}, u32[]{:S(2)}, u32[]{:S(2)}) async-start(s16[64,2,384]{2,1,0:T(2,128)(2,1)} %copy.27), calls=%async_computation.1 | async-start | bytes 196608 | tf_op jit(solution)/shard_map/all_to_all | solution.py:424
  25.6 0.1 pad_add_fusion.1.edge_ref
  25.7 0.0 copy-done
  25.7 0.0 copy-done.1
  25.7 2.9 %sweep_own.2 = f32[1024,512]{1,0:T(8,128)S(1)} custom-call(s32[2]{0:T(128)S(1)} %pad_add_fusion.1.edge_ref, f32[1024,512]{1,0:T(8,128)S(1)} %bitcast.39, bf16[5,2,256,256]{3,2,1,0:T(8,128)(2,1)S(1)} %copy-done, bf16[5,2,256,256]{3,2,1,0:T(8,128)(2,1)S(1)} %copy-done, bf16[5,2,256,256]{3,2,1,0:T(8,128)(2,1)S(1)} %copy-done, bf16[5,2,256,256]{3,2,1,0:T(8,128)(2,1)S(1)} %copy-done), custom_call_target="tpu_custom_call" | custom-call | flops 1610612736 | bytes 5242880 | tf_op jit(solution)/shard_map/sweep_own/pallas_call | solution.py:108
  28.6 0.0 collective-permute-done.1.high_ref
  28.6 0.0 collective-permute-done.low_ref
  28.6 0.0 copy-start.4
  28.6 0.0 copy-start.2
  28.6 5.7 %member_sum.1 = bf16[4,5,64,128]{3,2,1,0:T(8,128)(2,1)} custom-call(f32[16,64,512]{2,1,0:T(8,128)S(1)} %bitcast.40, s16[16,64,256]{2,1,0:T(8,128)(2,1)} %collective-permute-done.low_ref, s16[16,64,256]{2,1,0:T(8,128)(2,1)} %collective-permute-done.1.high_ref, bf16[16,5,64,512]{3,2,1,0:T(8,128)(2,1)} %ens_ref.3, bf16[5,2,256,256]{3,2,1,0:T(8,128)(2,1)S(1)} %copy-done, ...), custom_call_target="tpu_custom_call" | custom-call | flops 805306368 | bytes 8388608 | tf_op jit(solution)/shard_map/member_sum/pallas_call | solution.py:162
  34.3 1.4 %all-to-all-done.1 = s16[64,2,384]{2,1,0:T(2,128)(2,1)S(1)} async-done(((s16[64,2,384]{2,1,0:T(2,128)(2,1)}), s16[64,2,384]{2,1,0:T(2,128)(2,1)S(1)}, u32[]{:S(2)}, u32[]{:S(2)}) %all-to-all-start.1) | async-done | bytes 98336 | tf_op jit(solution)/shard_map/all_to_all | solution.py:424
  35.7 4.2 %all-to-all-start = ((bf16[4,320,128]{2,1,0:T(8,128)(2,1)}), bf16[4,320,128]{2,1,0:T(8,128)(2,1)S(1)}, u32[]{:S(2)}, u32[]{:S(2)}) async-start(bf16[4,320,128]{2,1,0:T(8,128)(2,1)} %bitcast.4), calls=%async_computation | async-start | bytes 655360 | tf_op jit(solution)/shard_map/all_to_all | solution.py:437
  39.9 0.0 copy-done.4
  39.9 0.1 copy.23
  40.0 0.1 reshape.70.slots_ref
  40.1 0.0 copy-done.2
  40.1 0.3 copy.28.jac_ref
  40.4 0.1 reshape.71.obs_ref
  40.5 4.2 %obs_tables.1 = (f32[5,128,128]{2,1,0:T(8,128)S(1)}, f32[5,128,128]{2,1,0:T(8,128)S(1)}) custom-call(s16[128,3,128]{2,1,0:T(4,128)(2,1)S(1)} %reshape.71.obs_ref), custom_call_target="tpu_custom_call" | custom-call | flops 134217728 | bytes 819200 | tf_op jit(solution)/shard_map/obs_tables/pallas_call | solution.py:228
  44.6 1.7 %all-to-all-done.parts_ref = bf16[4,320,128]{2,1,0:T(8,128)(2,1)S(1)} async-done(((bf16[4,320,128]{2,1,0:T(8,128)(2,1)}), bf16[4,320,128]{2,1,0:T(8,128)(2,1)S(1)}, u32[]{:S(2)}, u32[]{:S(2)}) %all-to-all-start) | async-done | bytes 327712 | tf_op jit(solution)/shard_map/all_to_all | solution.py:437
  46.4 1.3 %observe.1 = (bf16[320,128]{1,0:T(8,128)(2,1)S(1)}, f32[5,128,128]{2,1,0:T(8,128)S(1)}) custom-call(bf16[4,320,128]{2,1,0:T(8,128)(2,1)S(1)} %all-to-all-done.parts_ref, s32[1,128]{1,0:T(1,128)S(1)} %reshape.70.slots_ref, bf16[640,320]{1,0:T(8,128)(2,1)S(1)} %copy.28.jac_ref, f32[5,128,128]{2,1,0:T(8,128)S(1)} %get-tuple-element.9.w_ref, ...), custom_call_target="tpu_custom_call" | custom-call | flops 104857600 | bytes 983040 | tf_op jit(solution)/shard_map/observe/pallas_call | solution.py:264
  47.8 8.3 %all_to_all.20 = bf16[4,320,128]{2,1,0:T(8,128)(2,1)S(1)} all-to-all(bf16[4,320,128]{2,1,0:T(8,128)(2,1)S(1)} %broadcast_in_dim.28), channel_id=1, replica_groups=mesh['tile'=64,'mem'=4] {'mem'}, dimensions={0} | all-to-all | bytes 655360 | tf_op jit(solution)/shard_map/all_to_all | solution.py:444
  56.1 0.0 copy-start.3
  56.1 3.9 %member_adjoint.1 = (f32[16,64,512]{2,1,0:T(8,128)S(1)}, bf16[16,64,256]{2,1,0:T(8,128)(2,1)S(1)}, bf16[16,64,256]{2,1,0:T(8,128)(2,1)S(1)}) custom-call(bf16[16,5,64,512]{3,2,1,0:T(8,128)(2,1)} %ens_ref.3, bf16[4,5,64,128]{3,2,1,0:T(8,128)(2,1)S(1)} %bitcast.42), custom_call_target="tpu_custom_call" | custom-call | flops 5242880 | bytes 10485760 | tf_op jit(solution)/shard_map/member_adjoint/pallas_call | solution.py:322
  60.0 5.5 %collective-permute-start.2 = (bf16[16,64,256]{2,1,0:T(8,128)(2,1)S(1)}, bf16[16,64,256]{2,1,0:T(8,128)(2,1)S(1)}, u32[]{:S(2)}, u32[]{:S(2)}) collective-permute-start(bf16[16,64,256]{2,1,0:T(8,128)(2,1)S(1)} %get-tuple-element.13), channel_id=1, source_target_pairs={{0,4},{4,8},{8,12},{12,16},{16,20},{20,24},{24,28},{28,32},{32,36}... | collective-permute-start | bytes 1572872 | tf_op jit(solution)/shard_map/ppermute | solution.py:374
  65.5 1.9 %collective-permute-start.3 = (bf16[16,64,256]{2,1,0:T(8,128)(2,1)S(1)}, bf16[16,64,256]{2,1,0:T(8,128)(2,1)S(1)}, u32[]{:S(2)}, u32[]{:S(2)}) collective-permute-start(bf16[16,64,256]{2,1,0:T(8,128)(2,1)S(1)} %get-tuple-element.14), channel_id=1, source_target_pairs={{4,0},{8,4},{12,8},{16,12},{20,16},{24,20},{28,24},{32,28},{36,32}... | collective-permute-start | bytes 1572872 | tf_op jit(solution)/shard_map/ppermute | solution.py:375
  67.4 0.6 pick.1
  68.0 20.5 %all_to_all.21 = f32[64,2,128]{2,1,0:T(2,128)S(1)} all-to-all(f32[64,2,128]{2,1,0:T(2,128)S(1)} %bitcast.45), channel_id=1, replica_groups=mesh['tile'=64,'mem'=4] {'tile'}, dimensions={0} | all-to-all | bytes 131072 | tf_op jit(solution)/shard_map/all_to_all | solution.py:453
  88.5 0.0 copy-done.3
  88.5 0.1 fusion.8
  88.6 0.7 copy.30
  89.2 2.9 %sweep_own.3.own_ref = f32[1024,512]{1,0:T(8,128)S(1)} custom-call(s32[2]{0:T(128)S(1)} %pad_add_fusion.1.edge_ref, f32[1024,512]{1,0:T(8,128)S(1)} %bitcast.41, bf16[5,2,256,256]{3,2,1,0:T(8,128)(2,1)S(1)} %copy-done, bf16[5,2,256,256]{3,2,1,0:T(8,128)(2,1)S(1)} %copy-done, bf16[5,2,256,256]{3,2,1,0:T(8,128)(2,1)S(1)} %copy-done, ...), custom_call_target="tpu_custom_call" | custom-call | flops 1610612736 | bytes 5242880 | tf_op jit(solution)/shard_map/sweep_own/pallas_call | solution.py:108
  92.1 0.0 collective-permute-done.2
  92.1 0.0 collective-permute-done.3
  92.2 2.5 %add_halo.1 = f32[1024,512]{1,0:T(8,128)} custom-call(f32[1024,512]{1,0:T(8,128)S(1)} %sweep_own.3.own_ref, bf16[1024,256]{1,0:T(8,128)(2,1)S(1)} %bitcast.43, bf16[1024,256]{1,0:T(8,128)(2,1)S(1)} %bitcast.44, bf16[5,2,256,256]{3,2,1,0:T(8,128)(2,1)S(1)} %copy-done, bf16[5,2,256,256]{3,2,1,0:T(8,128)(2,1)S(1)} %copy-done), custom_call_target="tpu_custom_call" | custom-call | flops 536870912 | bytes 5242880 | tf_op jit(solution)/shard_map/add_halo/pallas_call | solution.py:352
  (2 shorter events, 0.1 us)
Async XLA Ops:
  0.6 25.1 %copy-start = (bf16[5,2,256,256]{3,2,1,0:T(8,128)(2,1)S(1)}, bf16[5,2,256,256]{3,2,1,0:T(8,128)(2,1)}, u32[]{:S(2)}) copy-start(bf16[5,2,256,256]{3,2,1,0:T(8,128)(2,1)} %constant.28.clone.t_left.t_right.t_after.t_before) | copy-start | bytes 3932164
  0.6 25.0 %copy-start.1 = (f32[16,64,512]{2,1,0:T(8,128)S(1)}, f32[16,64,512]{2,1,0:T(8,128)}, u32[]{:S(2)}) copy-start(f32[16,64,512]{2,1,0:T(8,128)} %param.9) | copy-start | bytes 6291460
  3.6 25.0 %collective-permute-start.1 = (s16[16,64,256]{2,1,0:T(8,128)(2,1)}, s16[16,64,256]{2,1,0:T(8,128)(2,1)}, u32[]{:S(2)}, u32[]{:S(2)}) collective-permute-start(s16[16,64,256]{2,1,0:T(8,128)(2,1)} %get-tuple-element.20), channel_id=1, source_target_pairs={{4,0},{8,4},{12,8},{16,12},{20,16},{24,20},{28,24},{32,28},{36,32}... | collective-permute-start | bytes 1572872 | tf_op jit(solution)/shard_map/ppermute | solution.py:375
  8.7 19.9 %collective-permute-start = (s16[16,64,256]{2,1,0:T(8,128)(2,1)}, s16[16,64,256]{2,1,0:T(8,128)(2,1)}, u32[]{:S(2)}, u32[]{:S(2)}) collective-permute-start(s16[16,64,256]{2,1,0:T(8,128)(2,1)} %get-tuple-element.21), channel_id=1, source_target_pairs={{0,4},{4,8},{8,12},{12,16},{16,20},{20,24},{24,28},{28,32},{32,36}... | collective-permute-start | bytes 1572872 | tf_op jit(solution)/shard_map/ppermute | solution.py:374
  13.9 21.8 %all-to-all-start.1 = ((s16[64,2,384]{2,1,0:T(2,128)(2,1)}), s16[64,2,384]{2,1,0:T(2,128)(2,1)S(1)}, u32[]{:S(2)}, u32[]{:S(2)}) async-start(s16[64,2,384]{2,1,0:T(2,128)(2,1)} %copy.27), calls=%async_computation.1 | async-start | bytes 196608 | tf_op jit(solution)/shard_map/all_to_all | solution.py:424
  28.6 11.3 %copy-start.4 = (s32[1,64,2]{1,2,0:T(2,128)S(1)}, s32[1,64,2]{1,2,0:T(2,128)}, u32[]{:S(2)}) copy-start(s32[1,64,2]{1,2,0:T(2,128)} %param.12) | copy-start | bytes 1540
  28.6 11.5 %copy-start.2 = (bf16[640,320]{0,1:T(8,128)(2,1)S(1)}, bf16[640,320]{0,1:T(8,128)(2,1)}, u32[]{:S(2)}) copy-start(bf16[640,320]{0,1:T(8,128)(2,1)} %param.11) | copy-start | bytes 1228804
  35.7 10.7 %all-to-all-start = ((bf16[4,320,128]{2,1,0:T(8,128)(2,1)}), bf16[4,320,128]{2,1,0:T(8,128)(2,1)S(1)}, u32[]{:S(2)}, u32[]{:S(2)}) async-start(bf16[4,320,128]{2,1,0:T(8,128)(2,1)} %bitcast.4), calls=%async_computation | async-start | bytes 655360 | tf_op jit(solution)/shard_map/all_to_all | solution.py:437
  56.1 32.4 %copy-start.3 = (f32[1,64,2,128]{3,2,1,0:T(2,128)S(1)}, f32[1,64,2,128]{3,2,1,0:T(2,128)}, u32[]{:S(2)}) copy-start(f32[1,64,2,128]{3,2,1,0:T(2,128)} %param.15) | copy-start | bytes 196612
  60.0 32.2 %collective-permute-start.2 = (bf16[16,64,256]{2,1,0:T(8,128)(2,1)S(1)}, bf16[16,64,256]{2,1,0:T(8,128)(2,1)S(1)}, u32[]{:S(2)}, u32[]{:S(2)}) collective-permute-start(bf16[16,64,256]{2,1,0:T(8,128)(2,1)S(1)} %get-tuple-element.13), channel_id=1, source_target_pairs={{0,4},{4,8},{8,12},{12,16},{16,20},{20,24},{24,28},{28,32},{32,36}... | collective-permute-start | bytes 1572872 | tf_op jit(solution)/shard_map/ppermute | solution.py:374
  65.5 26.7 %collective-permute-start.3 = (bf16[16,64,256]{2,1,0:T(8,128)(2,1)S(1)}, bf16[16,64,256]{2,1,0:T(8,128)(2,1)S(1)}, u32[]{:S(2)}, u32[]{:S(2)}) collective-permute-start(bf16[16,64,256]{2,1,0:T(8,128)(2,1)S(1)} %get-tuple-element.14), channel_id=1, source_target_pairs={{4,0},{8,4},{12,8},{16,12},{20,16},{24,20},{28,24},{32,28},{36,32}... | collective-permute-start | bytes 1572872 | tf_op jit(solution)/shard_map/ppermute | solution.py:375

commit v2 on v1

v2 whole, which is shorter than its diff:
```python
import functools
import math

import jax
import jax.numpy as jnp
import numpy as np
from jax import lax
from jax.experimental import pallas as pl
from jax.experimental.pallas import tpu as pltpu
from jax.sharding import PartitionSpec as P


NY = 64
SWEEPS = 4
DIFFUSION = 0.2
HALF = SWEEPS * NY

CONTROL_STEP = 8.0 / 32704.0
INNOVATION_STEP = 1.5 / 32700.0
WEIGHT_STEP = 10.0 / 32700.0

F32 = jnp.float32
BF16 = jnp.bfloat16
I16 = jnp.int16
I32 = jnp.int32

VMEM = pl.BlockSpec(memory_space=pltpu.VMEM)
HBM = pl.BlockSpec(memory_space=pltpu.HBM)
SMEM = pl.BlockSpec(memory_space=pltpu.SMEM)


def sweep_matrices():
    y_part = (1.0 - 4.0 * DIFFUSION) * np.eye(NY) + DIFFUSION * (
        np.eye(NY, k=1) + np.eye(NY, k=-1)
    )
    powers = [np.linalg.matrix_power(y_part, n) for n in range(SWEEPS + 1)]
    by_distance = [np.zeros((NY, NY)) for _ in range(SWEEPS + 1)]
    for k in range(SWEEPS + 1):
        for ups in range(k + 1):
            distance = 2 * ups - k
            if distance >= 0:
                by_distance[distance] = by_distance[distance] + (
                    math.comb(SWEEPS, k)
                    * DIFFUSION**k
                    * math.comb(k, ups)
                    * powers[SWEEPS - k]
                )

    def block(distance_of, image_of=None):
        full = np.zeros((HALF, HALF))
        for xi in range(SWEEPS):
            for xo in range(SWEEPS):
                piece = np.zeros((NY, NY))
                if distance_of(xi, xo) <= SWEEPS:
                    piece = piece + by_distance[distance_of(xi, xo)]
                if image_of is not None and image_of(xi, xo) <= SWEEPS:
                    piece = piece - by_distance[image_of(xi, xo)]
                full[xi * NY : (xi + 1) * NY, xo * NY : (xo + 1) * NY] = piece
        return full

    last = SWEEPS - 1
    same = lambda xi, xo: abs(xi - xo)
    blocks = [
        block(same, lambda xi, xo: xi + xo + 2),
        block(same),
        block(same, lambda xi, xo: (last - xi) + (last - xo) + 2),
        block(lambda xi, xo: xo + SWEEPS - xi),
        block(lambda xi, xo: xi + SWEEPS - xo),
    ]
    stacked = np.stack(blocks).astype(np.float32)
    high = stacked.astype(jnp.bfloat16)
    low = (stacked - high.astype(np.float32)).astype(jnp.bfloat16)
    return np.stack([high, low], axis=1)


def split_high_low(values):
    high = values.astype(BF16)
    return high, (values - high.astype(F32)).astype(BF16)


def mm(a, b):
    return jnp.dot(a, b, preferred_element_type=F32)


def mm_nt(a, b):
    return lax.dot_general(a, b, (((1,), (1,)), ((), ())), preferred_element_type=F32)


def in_hbm(x):
    return pltpu.with_memory_space_constraint(x, pltpu.HBM)


def params(**extra):
    return pltpu.CompilerParams(vmem_limit_bytes=24 * 1024 * 1024, **extra)


def cost(flops, bytes_accessed):
    return pl.CostEstimate(flops=flops, bytes_accessed=bytes_accessed, transcendentals=0)


def encode_kernel(x_hbm, low_ref, high_ref, x_ref, sems):
    members = x_hbm.shape[0]
    step = 4
    turns = members // step

    def load(turn):
        at = pl.ds(turn * step, step)
        return pltpu.make_async_copy(x_hbm.at[at], x_ref.at[at], sems.at[turn])

    for turn in range(turns):
        load(turn).start()

    def one(turn, carry):
        load(turn).wait()
        at = pl.ds(turn * step, step)
        coded = jnp.round(x_ref[at] * (1.0 / CONTROL_STEP)).astype(I32).astype(I16)
        low_ref[at] = coded[:, :, :HALF]
        high_ref[at] = coded[:, :, HALF:]
        return carry

    lax.fori_loop(0, turns, one, 0)


def encode(control):
    members, levels, _ = control.shape
    half = jax.ShapeDtypeStruct((members, levels, HALF), I16)
    return pl.pallas_call(
        encode_kernel,
        out_shape=(half, half),
        in_specs=[HBM],
        out_specs=(VMEM, VMEM),
        scratch_shapes=[
            pltpu.VMEM(control.shape, F32),
            pltpu.SemaphoreType.DMA((members // 4,)),
        ],
        compiler_params=params(),
        cost_estimate=cost(4 * control.size, 6 * control.size),
        name="encode",
    )(in_hbm(control))


def pack_kernel(count_ref, channel_ref, innovation_ref, weight_ref, o_ref):
    owners, slots, observed = channel_ref.shape
    slot_id = lax.broadcasted_iota(I32, (slots, observed), 0)
    for s in range(owners):
        filled = slot_id < count_ref[0, s]
        weight = jnp.where(filled, weight_ref[s] * (1.0 / WEIGHT_STEP), 0.0)
        innovation = innovation_ref[s] * (1.0 / INNOVATION_STEP)
        row = [channel_ref[s], jnp.round(innovation).astype(I32), jnp.round(weight).astype(I32)]
        for n, values in enumerate(row):
            o_ref[s, :, n * observed : (n + 1) * observed] = values.astype(I16)


def pack(counts, channel, innovation, weight):
    owners, slots, observed = channel.shape
    return pl.pallas_call(
        pack_kernel,
        out_shape=jax.ShapeDtypeStruct((owners, slots, 3 * observed), I16),
        in_specs=[SMEM, VMEM, VMEM, VMEM],
        out_specs=VMEM,
        compiler_params=params(),
        cost_estimate=cost(10 * channel.size, 18 * channel.size),
        name="pack",
    )(counts, channel, innovation, weight)


def depart_kernel(count_ref, evolved_ref, innovation_ref, o_ref):
    owners, slots, observed = evolved_ref.shape
    slot_id = lax.broadcasted_iota(I32, (slots, observed), 0)
    for s in range(owners):
        filled = slot_id < count_ref[0, s]
        o_ref[s] = jnp.where(filled, evolved_ref[s] - innovation_ref[s], 0.0)


def depart(counts, evolved, innovation):
    return pl.pallas_call(
        depart_kernel,
        out_shape=jax.ShapeDtypeStruct(evolved.shape, F32),
        in_specs=[SMEM, VMEM, VMEM],
        out_specs=VMEM,
        compiler_params=params(),
        cost_estimate=cost(2 * evolved.size, 12 * evolved.size),
        name="depart",
    )(counts, evolved, innovation)


def sweep_rows(edge_ref, x_ref, t_ref, o_ref, step, ready):
    def apply(high, low, index):
        t_high, t_low = t_ref[index, 0], t_ref[index, 1]
        return mm(high, t_high) + mm(low, t_high) + mm(high, t_low)

    def one(turn, carry):
        ready(turn)
        at = pl.ds(pl.multiple_of(turn * step, step), step)
        left_high, left_low = split_high_low(x_ref[at, :HALF])
        right_high, right_low = split_high_low(x_ref[at, HALF:])
        o_ref[at, :HALF] = apply(left_high, left_low, edge_ref[0]) + apply(
            right_high, right_low, 4
        )
        o_ref[at, HALF:] = apply(right_high, right_low, edge_ref[1]) + apply(
            left_high, left_low, 3
        )
        return carry

    lax.fori_loop(0, x_ref.shape[0] // step, one, 0)


def sweep_near_kernel(edge_ref, x_ref, t_ref, o_ref):
    sweep_rows(edge_ref, x_ref, t_ref, o_ref, 256, lambda turn: None)


def sweep_far_kernel(edge_ref, x_hbm, t_ref, o_ref, x_ref, sems):
    rows = x_hbm.shape[0]
    step = 256

    def load(turn):
        at = pl.ds(turn * step, step)
        return pltpu.make_async_copy(x_hbm.at[at], x_ref.at[at], sems.at[turn])

    for turn in range(rows // step):
        load(turn).start()
    sweep_rows(edge_ref, x_ref, t_ref, o_ref, step, lambda turn: load(turn).wait())


def sweep_own(edges, field, matrices, far):
    rows, columns = field.shape
    scratch = [pltpu.VMEM(field.shape, F32), pltpu.SemaphoreType.DMA((rows // 256,))]
    return pl.pallas_call(
        sweep_far_kernel if far else sweep_near_kernel,
        out_shape=jax.ShapeDtypeStruct((rows, columns), F32),
        in_specs=[SMEM, HBM if far else VMEM, VMEM],
        out_specs=VMEM,
        scratch_shapes=scratch if far else [],
        compiler_params=params(),
        cost_estimate=cost(2 * 6 * rows * columns * HALF, 10 * rows * columns),
        name="sweep_own",
    )(edges, in_hbm(field) if far else field, matrices)


LEVEL_STEP = 16


def level_copies(source, target, sems):
    def copy(turn):
        at = pl.ds(turn * LEVEL_STEP, LEVEL_STEP)
        return pltpu.make_async_copy(
            source.at[:, :, at, :], target.at[:, :, at, :], sems.at[turn]
        )

    return copy


def member_sum_kernel(
    scale, own_ref, low_ref, high_ref, ens_hbm, t_ref, o_hbm, ens_ref, o_ref, in_sems, out_sems
):
    members, variables, levels, _ = ens_ref.shape
    blocks, width = o_ref.shape[0], o_ref.shape[3]
    half_blocks = blocks // 2
    step = LEVEL_STEP
    load = level_copies(ens_hbm, ens_ref, in_sems)
    save = level_copies(o_ref, o_hbm, out_sems)
    for turn in range(levels // step):
        load(turn).start()

    def one(turn, carry):
        at = pl.ds(pl.multiple_of(turn * step, step), step)

        def from_halo(halo_ref, index):
            coded = halo_ref[:, at, :].astype(I32).reshape(members * step, HALF)
            upper = (coded >> 8).astype(F32).astype(BF16)
            lower = (coded & 255).astype(F32).astype(BF16)
            upper_part = mm(upper, t_ref[index, 0]) + mm(upper, t_ref[index, 1])
            lower_part = mm(lower, t_ref[index, 0])
            total = (upper_part * 256.0 + lower_part) * CONTROL_STEP
            return total.reshape(members, step, HALF)

        halos = [from_halo(low_ref, 3), from_halo(high_ref, 4)]
        load(turn).wait()
        for k in range(blocks):
            offset = (k % half_blocks) * width
            halo = halos[k // half_blocks][:, :, offset : offset + width]
            weights = own_ref[:, at, k * width : (k + 1) * width] + halo
            weights = weights.astype(BF16).astype(F32)
            for v in range(variables):
                total = None
                for m in range(members):
                    term = weights[m] * ens_ref[m, v, at, k * width : (k + 1) * width].astype(F32)
                    total = term if total is None else total + term
                o_ref[k, v, at, :] = (total * scale).astype(BF16)
        save(turn).start()
        return carry

    lax.fori_loop(0, levels // step, one, 0)
    for turn in range(levels // step):
        save(turn).wait()


def member_sum(own, from_low, from_high, ensemble, matrices, scale, blocks):
    members, variables, levels, columns = ensemble.shape
    width = columns // blocks
    turns = levels // LEVEL_STEP
    shape = (blocks, variables, levels, width)
    return pl.pallas_call(
        functools.partial(member_sum_kernel, scale),
        out_shape=pltpu.HBM(shape, BF16),
        in_specs=[VMEM, VMEM, VMEM, HBM, VMEM],
        out_specs=HBM,
        scratch_shapes=[
            pltpu.VMEM(ensemble.shape, BF16),
            pltpu.VMEM(shape, BF16),
            pltpu.SemaphoreType.DMA((turns,)),
            pltpu.SemaphoreType.DMA((turns,)),
        ],
        compiler_params=params(),
        cost_estimate=cost(
            2 * 3 * members * levels * columns * HALF, 2 * ensemble.size + 6 * own.size
        ),
        name="member_sum",
    )(own, from_low, from_high, in_hbm(ensemble), matrices)


def obs_tables_kernel(obs_ref, w_ref, b_ref, channel_ref):
    owners, slots, _ = obs_ref.shape
    groups, _, width = w_ref.shape
    group_id = lax.broadcasted_iota(I32, (8, width), 0)
    lane_id = lax.broadcasted_iota(I32, (width, width), 0)

    def one(owner, slot):
        row = obs_ref[owner].astype(I32)[slot : slot + 1]
        channel = row[:, :width]
        innovation = row[:, width : 2 * width].astype(F32) * INNOVATION_STEP
        weight = row[:, 2 * width :].astype(F32) * WEIGHT_STEP
        in_group = jnp.broadcast_to(channel >> 7, (8, width)) == group_id
        one_hot = jnp.where(
            jnp.broadcast_to(channel & 127, (width, width)) == lane_id, 1.0, 0.0
        ).astype(BF16)

        def spread(values):
            return [
                jnp.where(in_group, jnp.broadcast_to(part.astype(F32), (8, width)), 0.0)
                for part in split_high_low(values)
            ]

        left = jnp.concatenate(spread(weight) + spread(weight * innovation), axis=0)
        sums = mm_nt(left.astype(BF16), one_hot)
        w_sum = sums[0:8] + sums[8:16]
        b_sum = sums[16:24] + sums[24:32]
        at = pl.ds(owner * slots + slot, 1)
        channel_ref[at, :] = channel
        for g in range(groups):
            w_ref[g, at, :] = w_sum[g : g + 1]
            b_ref[g, at, :] = b_sum[g : g + 1]

    unroll = 4

    def several(turn, carry):
        for inner in range(unroll):
            for slot in range(slots):
                one(turn * unroll + inner, slot)
        return carry

    lax.fori_loop(0, owners // unroll, several, 0)


def obs_tables(obs, channels):
    owners, slots, packed = obs.shape
    width = packed // 3
    rows = owners * slots
    shape = jax.ShapeDtypeStruct((channels // width, rows, width), F32)
    return pl.pallas_call(
        obs_tables_kernel,
        out_shape=(shape, shape, jax.ShapeDtypeStruct((rows, width), I32)),
        compiler_params=params(),
        cost_estimate=cost(2 * 32 * rows * width * width, 10 * rows * channels),
        name="obs_tables",
    )(obs)


def observe_kernel(
    parts_ref, slots_ref, jac_ref, w_ref, b_ref, adj_hbm, model_ref, adj_ref, sems
):
    count, state, width = parts_ref.shape
    groups = w_ref.shape[0]
    total = parts_ref[0].astype(F32)
    for p in range(1, count):
        total = total + parts_ref[p].astype(F32)
    increment = total.astype(BF16)
    slots = slots_ref.shape[1]
    column_id = lax.broadcasted_iota(I32, (width, slots), 0)
    hits = jnp.where(column_id == jnp.broadcast_to(slots_ref[...], (width, slots)), 1.0, 0.0)
    hits = hits.astype(BF16)
    carried = mm(increment, hits).T.astype(BF16)
    column_adjoint = jnp.zeros((slots, state), F32)
    for g in range(groups):
        jac = jac_ref[g * width : (g + 1) * width, :]
        model = mm_nt(carried, jac)
        model_ref[g] = model
        channel_adjoint = (model * w_ref[g] - b_ref[g]).astype(BF16)
        column_adjoint = column_adjoint + mm(channel_adjoint, jac)
    rounded = column_adjoint.T.astype(BF16)
    adj_ref[...] = mm_nt(rounded, hits).astype(BF16)
    copies = [
        pltpu.make_async_copy(adj_ref, adj_hbm.at[p], sems.at[p]) for p in range(count)
    ]
    for copy in copies:
        copy.start()
    for copy in copies:
        copy.wait()


def observe(parts, slots, jacobian, w_table, b_table):
    count, state, width = parts.shape
    channels = jacobian.shape[0]
    rows = slots.shape[1]
    return pl.pallas_call(
        observe_kernel,
        out_shape=(
            pltpu.HBM((count, state, width), BF16),
            jax.ShapeDtypeStruct((channels // width, rows, width), F32),
        ),
        in_specs=[VMEM] * 5,
        out_specs=(HBM, VMEM),
        scratch_shapes=[
            pltpu.VMEM((state, width), BF16),
            pltpu.SemaphoreType.DMA((count,)),
        ],
        compiler_params=params(),
        cost_estimate=cost(4 * rows * state * channels, 12 * rows * channels),
        name="observe",
    )(parts, slots, jacobian, w_table, b_table)


def pick_kernel(model_ref, channel_ref, o_hbm, o_ref, sem):
    channel = channel_ref[...]
    group, lane = channel >> 7, channel & 127
    picked = jnp.zeros(channel.shape, F32)
    for g in range(model_ref.shape[0]):
        taken = jnp.take_along_axis(model_ref[g], lane, axis=1)
        picked = jnp.where(group == g, taken, picked)
    o_ref[...] = picked
    copy = pltpu.make_async_copy(o_ref, o_hbm, sem)
    copy.start()
    copy.wait()


def pick(model, channel):
    groups, slots, width = model.shape
    return pl.pallas_call(
        pick_kernel,
        out_shape=pltpu.HBM((slots, width), F32),
        in_specs=[VMEM, VMEM],
        out_specs=HBM,
        scratch_shapes=[pltpu.VMEM((slots, width), F32), pltpu.SemaphoreType.DMA],
        compiler_params=params(),
        cost_estimate=cost(slots * width * 16, 8 * groups * slots * width),
        name="pick",
    )(model, channel)


def member_adjoint_kernel(
    scale, ens_hbm, adj_ref, full_hbm, low_ref, high_ref, ens_ref, full_ref, sems, out_sems
):
    members, variables, levels, _ = ens_ref.shape
    blocks, width = adj_ref.shape[0], adj_ref.shape[3]
    half_blocks = blocks // 2
    step = LEVEL_STEP
    load = level_copies(ens_hbm, ens_ref, sems)
    for turn in range(levels // step):
        load(turn).start()

    def save(turn):
        at = pl.ds(turn * step, step)
        return pltpu.make_async_copy(
            full_ref.at[:, at, :], full_hbm.at[:, at, :], out_sems.at[turn]
        )

    def one(turn, carry):
        at = pl.ds(pl.multiple_of(turn * step, step), step)
        load(turn).wait()
        for k in range(blocks):
            adjoint = [adj_ref[k, v, at, :].astype(F32) * scale for v in range(variables)]
            half = low_ref if k < half_blocks else high_ref
            offset = (k % half_blocks) * width
            for m in range(members):
                total = None
                for v in range(variables):
                    term = ens_ref[m, v, at, k * width : (k + 1) * width].astype(F32) * adjoint[v]
                    total = term if total is None else total + term
                full_ref[m, at, k * width : (k + 1) * width] = total
                half[m, at, offset : offset + width] = total.astype(BF16)
        save(turn).start()
        return carry

    lax.fori_loop(0, levels // step, one, 0)
    for turn in range(levels // step):
        save(turn).wait()


def member_adjoint(ensemble, adjoint, scale):
    members, _, levels, columns = ensemble.shape
    half = jax.ShapeDtypeStruct((members, levels, HALF), BF16)
    return pl.pallas_call(
        functools.partial(member_adjoint_kernel, scale),
        out_shape=(pltpu.HBM((members, levels, columns), F32), half, half),
        in_specs=[HBM, VMEM],
        out_specs=(HBM, VMEM, VMEM),
        scratch_shapes=[
            pltpu.VMEM(ensemble.shape, BF16),
            pltpu.VMEM((members, levels, columns), F32),
            pltpu.SemaphoreType.DMA((levels // LEVEL_STEP,)),
            pltpu.SemaphoreType.DMA((levels // LEVEL_STEP,)),
        ],
        compiler_params=params(),
        cost_estimate=cost(2 * ensemble.size, 4 * ensemble.size),
        name="member_adjoint",
    )(in_hbm(ensemble), adjoint)


def add_halo_kernel(own_ref, low_ref, high_ref, t_ref, o_ref):
    i = pl.program_id(0)
    step = o_ref.shape[0]
    at = pl.ds(pl.multiple_of(i * step, step), step)

    def from_halo(halo_ref, index):
        halo = halo_ref[at, :]
        return mm(halo, t_ref[index, 0]) + mm(halo, t_ref[index, 1])

    o_ref[:, :HALF] = own_ref[at, :HALF] + from_halo(low_ref, 3)
    o_ref[:, HALF:] = own_ref[at, HALF:] + from_halo(high_ref, 4)


def add_halo(own, from_low, from_high, matrices):
    rows, columns = own.shape
    step = 256
    return pl.pallas_call(
        add_halo_kernel,
        out_shape=jax.ShapeDtypeStruct((rows, columns), F32),
        grid=(rows // step,),
        in_specs=[VMEM] * 4,
        out_specs=pl.BlockSpec((step, columns), lambda i: (i, 0)),
        compiler_params=params(),
        cost_estimate=cost(2 * 2 * rows * columns * HALF, 10 * rows * columns),
        name="add_halo",
    )(own, from_low, from_high, matrices)


def swap_halos(low_half, high_half):
    count = lax.axis_size("tile")
    forward = [(i, i + 1) for i in range(count - 1)]
    backward = [(i + 1, i) for i in range(count - 1)]
    from_low = lax.ppermute(high_half, "tile", forward)
    from_high = lax.ppermute(low_half, "tile", backward)
    return from_low, from_high


def body(
    control,
    ensemble,
    jacobian,
    send_columns,
    received_counts,
    observed_channel,
    innovation,
    error_weight,
):
    members, levels, columns = control.shape
    variables = ensemble.shape[1]
    state = variables * levels
    groups = lax.axis_size("mem")
    owners = lax.axis_size("tile")
    scale = 1.0 / math.sqrt(members * groups)
    width = columns // groups
    channels = jacobian.shape[0]
    observed = observed_channel.shape[-1]
    slots = send_columns.shape[-1]
    tile_index = lax.axis_index("tile")
    matrices = jnp.asarray(sweep_matrices())
    edges = jnp.stack(
        [jnp.where(tile_index == 0, 0, 1), jnp.where(tile_index == owners - 1, 2, 1)]
    ).astype(I32)

    counts = received_counts
    from_low, from_high = swap_halos(*encode(control))
    own = sweep_own(edges, control.reshape(members * levels, columns), matrices, True)
    packed = pack(counts, observed_channel[0], innovation[0], error_weight[0])
    packed, own = lax.optimization_barrier((packed, own))
    obs = lax.all_to_all(packed, "tile", split_axis=0, concat_axis=0, tiled=True)
    parts = member_sum(
        own.reshape(members, levels, columns),
        from_low,
        from_high,
        ensemble,
        matrices,
        scale,
        groups,
    )
    parts = lax.all_to_all(
        parts.reshape(groups, state, width), "mem", split_axis=0, concat_axis=0, tiled=True
    )
    w_table, b_table, channel = obs_tables(obs, channels)
    block_adjoint, model = observe(
        parts, send_columns.reshape(1, owners * slots), jacobian, w_table, b_table
    )
    adjoint = lax.all_to_all(
        block_adjoint, "mem", split_axis=0, concat_axis=0, tiled=True
    ).reshape(groups, variables, levels, width)
    evolved = pick(model, channel).reshape(owners, slots, observed)
    evolved = lax.all_to_all(evolved, "tile", split_axis=0, concat_axis=0, tiled=True)
    full, low_half, high_half = member_adjoint(ensemble, adjoint, scale)
    from_low, from_high = swap_halos(low_half, high_half)
    own = sweep_own(edges, full.reshape(members * levels, columns), matrices, True)
    departures = depart(counts, evolved, innovation[0])
    gradient = add_halo(
        own,
        from_low.reshape(members * levels, HALF),
        from_high.reshape(members * levels, HALF),
        matrices,
    )
    return gradient.reshape(members, levels, columns), departures[None]


def solution(mesh):
    in_specs = (
        P("mem", None, "tile"),
        P("mem", None, None, "tile"),
        P(),
        P(("tile", "mem"), None, None),
        P(("tile", "mem"), None),
        P(("tile", "mem"), None, None, None),
        P(("tile", "mem"), None, None, None),
        P(("tile", "mem"), None, None, None),
    )
    out_specs = (P("mem", None, "tile"), P(("tile", "mem"), None, None, None))
    return jax.shard_map(body, mesh=mesh, in_specs=in_specs, out_specs=out_specs, check_vma=False)
```

time: 95.3 us -> 99.5 us (1.044)
  Pallas kernels: 24 us -> 33.2 us
  other arithmetic: 5.6 us -> 0.07 us
  waiting for transfers between devices: 3.14 us -> 4.23 us
    pallas_call x6 -> x9, Pallas kernels: 17.6 us -> 27 us  [the longest x2 8.01 us: sweep_own(): pl.pallas_call(sweep_far_kernel if far else sweep_near_kernel, out_shape=...]
    convert_element_type x3 -> x0, other arithmetic: 4.76 us -> none  [the longest x2 3.91 us: coded(): jnp.clip(jnp.round(values * (1.0 / step)), -32767.0, 32767.0).astype(I16)]
    ppermute x2, starting transfers between devices: 7.02 us -> 4.19 us  [swap_halos(): from_high = lax.ppermute(low_half, 'tile', backward)]
    all_to_all x1, waiting for transfers between devices: 1.38 us -> 4.2 us  [body(): lax.all_to_all(packed, 'tile', split_axis=0, concat_axis=0, tiled=True)]
    all_to_all x1, blocking collectives: 20.5 us -> 17.9 us  [body(): lax.all_to_all(evolved, 'tile', split_axis=0, concat_axis=0, tiled=True)]
    ppermute x2, starting transfers between devices: 7.41 us -> 9.83 us  [swap_halos(): from_low = lax.ppermute(high_half, 'tile', forward)]
    all_to_all x1, blocking collectives: 8.25 us -> 10.2 us  [body(): lax.all_to_all(block_adjoint, 'mem', split_axis=0, concat_axis=0, tiled=T...]
    all_to_all x1, waiting for transfers between devices: 1.75 us -> 0.02 us  [body(): lax.all_to_all(parts.reshape(groups, state, width), 'mem', split_axis=0,...]
  transfers between devices with their start and end apart: 6 -> 6, of which waited for: 2 -> 1; matrix products, arithmetic and copies ran while one was open for 5% -> 2% of each run, Pallas kernels for 17% -> 23%
where the time goes in v2:
time: 99.5 us; the launch traced here: 98.9 us
  Pallas kernels  33.2 us (33%)
  starting transfers between devices  30.9 us (31%)
  blocking collectives  28.1 us (28%)
  waiting for transfers between devices  4.23 us (4%)
  local copies, waits for them, and re-layouts  1.52 us (2%)
    all_to_all x1, blocking collectives, body(): lax.all_to_all(evolved, 'tile', split_axis=0, concat_axis=0, tiled=True)  17.9 us
    all_to_all x1, starting transfers between devices, body(): lax.all_to_all(packed, 'tile', split_axis=0, concat_axis=0, tiled=True)  12.7 us
    all_to_all x1, blocking collectives, body(): lax.all_to_all(block_adjoint, 'mem', split_axis=0, concat_axis=0, tiled=T...  10.2 us
    ppermute x2, starting transfers between devices, swap_halos(): from_low = lax.ppermute(high_half, 'tile', forward)  9.83 us
    pallas_call x2, Pallas kernels, sweep_own(): pl.pallas_call(sweep_far_kernel if far else sweep_near_kernel, out_shape=...  8.01 us
    pallas_call x1, Pallas kernels, member_sum(): pl.pallas_call(functools.partial(member_sum_kernel, scale), out_shape=plt...  5.8 us
    pallas_call x1, Pallas kernels, obs_tables(): pl.pallas_call(obs_tables_kernel, out_shape=(shape, shape, jax.ShapeDtype...  5.06 us
    all_to_all x1, waiting for transfers between devices, body(): lax.all_to_all(packed, 'tile', split_axis=0, concat_axis=0, tiled=True)  4.2 us
  transfers between devices with their start and end apart: 6, of which 1 were waited for; matrix products, arithmetic and copies ran while one was open for 2% of the time, Pallas kernels for 23%

profile of v2, /device:TPU:1, one launch (start us, length us, event | category | flops | bytes accessed | tf_op | source)
XLA Modules:
  0.0 98.9 jit_solution(15464188798633247994)
XLA Ops:
  0.6 0.0 copy-start
  0.6 0.0 copy-start.4
  0.7 0.0 copy-start.3
  0.7 0.0 copy-start.1
  0.7 0.0 copy-start.2
  0.7 2.7 %encode.1 = (s16[16,64,256]{2,1,0:T(8,128)(2,1)}, s16[16,64,256]{2,1,0:T(8,128)(2,1)}) custom-call(f32[16,64,512]{2,1,0:T(8,128)} %x_hbm.1), custom_call_target="tpu_custom_call" | custom-call | flops 2097152 | bytes 3145728 | tf_op jit(solution)/shard_map/encode/pallas_call | solution.py:127
  3.3 4.9 %collective-permute-start = (s16[16,64,256]{2,1,0:T(8,128)(2,1)}, s16[16,64,256]{2,1,0:T(8,128)(2,1)}, u32[]{:S(2)}, u32[]{:S(2)}) collective-permute-start(s16[16,64,256]{2,1,0:T(8,128)(2,1)} %get-tuple-element.15), channel_id=1, source_target_pairs={{0,4},{4,8},{8,12},{12,16},{16,20},{20,24},{24,28},{28,32},{32,36}... | collective-permute-start | bytes 1572872 | tf_op jit(solution)/shard_map/ppermute | solution.py:551
  8.3 2.3 %collective-permute-start.1 = (s16[16,64,256]{2,1,0:T(8,128)(2,1)}, s16[16,64,256]{2,1,0:T(8,128)(2,1)}, u32[]{:S(2)}, u32[]{:S(2)}) collective-permute-start(s16[16,64,256]{2,1,0:T(8,128)(2,1)} %get-tuple-element.16), channel_id=1, source_target_pairs={{4,0},{8,4},{12,8},{16,12},{20,16},{24,20},{28,24},{32,28},{36,32}... | collective-permute-start | bytes 1572872 | tf_op jit(solution)/shard_map/ppermute | solution.py:552
  10.6 0.0 copy-done.4
  10.6 0.0 copy-done.3
  10.6 0.0 copy-done.1
  10.6 0.0 copy-done.2
  10.6 1.3 %pack.1 = s16[64,2,384]{2,1,0:T(2,128)(2,1)} custom-call(s32[1,64]{1,0:T(1,128)S(1)} %copy-done.4, s32[64,2,128]{2,1,0:T(2,128)S(1)} %bitcast.21, f32[64,2,128]{2,1,0:T(2,128)S(1)} %bitcast.19, f32[64,2,128]{2,1,0:T(2,128)S(1)} %bitcast.22), custom_call_target="tpu_custom_call" | custom-call | flops 163840 | bytes 294912 | tf_op jit(solution)/shard_map/pack/pallas_call | solution.py:156
  11.9 0.1 pad_add_fusion.edge_ref
  11.9 0.0 copy-done
  11.9 4.0 %sweep_own.2 = f32[1024,512]{1,0:T(8,128)S(1)} custom-call(s32[2]{0:T(128)S(1)} %pad_add_fusion.edge_ref, f32[1024,512]{1,0:T(8,128)} %bitcast.24, bf16[5,2,256,256]{3,2,1,0:T(8,128)(2,1)S(1)} %copy-done), custom_call_target="tpu_custom_call" | custom-call | flops 1610612736 | bytes 5242880 | tf_op jit(solution)/shard_map/sweep_own/pallas_call | solution.py:228
  16.0 12.7 %all-to-all-start.1 = ((s16[64,2,384]{2,1,0:T(2,128)(2,1)}), s16[64,2,384]{2,1,0:T(2,128)(2,1)}, u32[]{:S(2)}, u32[]{:S(2)}) async-start(s16[64,2,384]{2,1,0:T(2,128)(2,1)} %pack.1), calls=%async_computation.1 | async-start | bytes 196608 | tf_op jit(solution)/shard_map/all_to_all | solution.py:587
  28.7 0.0 collective-permute-done.low_ref
  28.7 0.0 collective-permute-done.1.high_ref
  28.7 0.0 copy-start.5
  28.7 5.8 %member_sum.1 = bf16[4,5,64,128]{3,2,1,0:T(8,128)(2,1)} custom-call(f32[16,64,512]{2,1,0:T(8,128)S(1)} %bitcast.15, s16[16,64,256]{2,1,0:T(8,128)(2,1)} %collective-permute-done.low_ref, s16[16,64,256]{2,1,0:T(8,128)(2,1)} %collective-permute-done.1.high_ref, bf16[16,5,64,512]{3,2,1,0:T(8,128)(2,1)} %ens_hbm.3, bf16[5,2,256,256]{3,2,1,0:T(8,128)(2,1)S(1)} %copy-done), custom_call_target="tpu_custom_call" | custom-call | flops 805306368 | bytes 8388608 | tf_op jit(solution)/shard_map/member_sum/pallas_call | solution.py:303
  34.5 4.2 %all-to-all-done.1.obs_ref = s16[64,2,384]{2,1,0:T(2,128)(2,1)} async-done(((s16[64,2,384]{2,1,0:T(2,128)(2,1)}), s16[64,2,384]{2,1,0:T(2,128)(2,1)}, u32[]{:S(2)}, u32[]{:S(2)}) %all-to-all-start.1) | async-done | bytes 98336 | tf_op jit(solution)/shard_map/all_to_all | solution.py:587
  38.7 4.2 %all-to-all-start = ((bf16[4,320,128]{2,1,0:T(8,128)(2,1)}), bf16[4,320,128]{2,1,0:T(8,128)(2,1)S(1)}, u32[]{:S(2)}, u32[]{:S(2)}) async-start(bf16[4,320,128]{2,1,0:T(8,128)(2,1)} %bitcast.25), calls=%async_computation | async-start | bytes 655360 | tf_op jit(solution)/shard_map/all_to_all | solution.py:597
  42.9 0.0 copy-done.5
  42.9 0.1 copy.13
  43.0 0.1 reshape.37.slots_ref
  43.2 1.3 %copy.14.jac_ref = bf16[640,320]{1,0:T(8,128)(2,1)S(1)} copy(bf16[640,320]{0,1:T(8,128)(2,1)} %param.11) | data formatting | bytes 819200 | tf_op args[2]
  44.4 5.1 %obs_tables.1 = (f32[5,128,128]{2,1,0:T(8,128)S(1)}, f32[5,128,128]{2,1,0:T(8,128)S(1)}, s32[128,128]{1,0:T(8,128)S(1)}) custom-call(s16[64,2,384]{2,1,0:T(2,128)(2,1)} %all-to-all-done.1.obs_ref), custom_call_target="tpu_custom_call" | custom-call | flops 134217728 | bytes 819200 | tf_op jit(solution)/shard_map/obs_tables/pallas_call | solution.py:370
  49.5 0.0 all-to-all-done.parts_ref
  49.5 2.1 %observe.1 = (bf16[4,320,128]{2,1,0:T(8,128)(2,1)}, f32[5,128,128]{2,1,0:T(8,128)S(1)}) custom-call(bf16[4,320,128]{2,1,0:T(8,128)(2,1)S(1)} %all-to-all-done.parts_ref, s32[1,128]{1,0:T(1,128)S(1)} %reshape.37.slots_ref, bf16[640,320]{1,0:T(8,128)(2,1)S(1)} %copy.14.jac_ref, f32[5,128,128]{2,1,0:T(8,128)S(1)} %get-tuple-element.18.w_ref, ...), custom_call_target="tpu_custom_call" | custom-call | flops 104857600 | bytes 983040 | tf_op jit(solution)/shard_map/observe/pallas_call | solution.py:415
  51.6 10.2 %all_to_all.20 = bf16[4,320,128]{2,1,0:T(8,128)(2,1)S(1)} all-to-all(bf16[4,320,128]{2,1,0:T(8,128)(2,1)} %get-tuple-element.20), channel_id=1, replica_groups=mesh['tile'=64,'mem'=4] {'mem'}, dimensions={0} | all-to-all | bytes 655360 | tf_op jit(solution)/shard_map/all_to_all | solution.py:604
  61.8 3.6 %member_adjoint.1 = (f32[16,64,512]{2,1,0:T(8,128)}, bf16[16,64,256]{2,1,0:T(8,128)(2,1)S(1)}, bf16[16,64,256]{2,1,0:T(8,128)(2,1)S(1)}) custom-call(bf16[16,5,64,512]{3,2,1,0:T(8,128)(2,1)} %ens_hbm.3, bf16[4,5,64,128]{3,2,1,0:T(8,128)(2,1)S(1)} %bitcast.16), custom_call_target="tpu_custom_call" | custom-call | flops 5242880 | bytes 10485760 | tf_op jit(solution)/shard_map/member_adjoint/pallas_call | solution.py:502
  65.5 4.9 %collective-permute-start.2 = (bf16[16,64,256]{2,1,0:T(8,128)(2,1)S(1)}, bf16[16,64,256]{2,1,0:T(8,128)(2,1)S(1)}, u32[]{:S(2)}, u32[]{:S(2)}) collective-permute-start(bf16[16,64,256]{2,1,0:T(8,128)(2,1)S(1)} %get-tuple-element.22), channel_id=1, source_target_pairs={{0,4},{4,8},{8,12},{12,16},{16,20},{20,24},{24,28},{28,32},{32,36}... | collective-permute-start | bytes 1572872 | tf_op jit(solution)/shard_map/ppermute | solution.py:551
  70.4 1.9 %collective-permute-start.3 = (bf16[16,64,256]{2,1,0:T(8,128)(2,1)S(1)}, bf16[16,64,256]{2,1,0:T(8,128)(2,1)S(1)}, u32[]{:S(2)}, u32[]{:S(2)}) collective-permute-start(bf16[16,64,256]{2,1,0:T(8,128)(2,1)S(1)} %get-tuple-element.23), channel_id=1, source_target_pairs={{4,0},{8,4},{12,8},{16,12},{20,16},{24,20},{28,24},{32,28},{36,32}... | collective-permute-start | bytes 1572872 | tf_op jit(solution)/shard_map/ppermute | solution.py:552
  72.3 0.9 pick.1
  73.2 17.9 %all_to_all.21.evolved_ref = f32[64,2,128]{2,1,0:T(2,128)S(1)} all-to-all(f32[64,2,128]{2,1,0:T(2,128)} %bitcast.26), channel_id=1, replica_groups=mesh['tile'=64,'mem'=4] {'tile'}, dimensions={0} | all-to-all | bytes 131072 | tf_op jit(solution)/shard_map/all_to_all | solution.py:608
  91.1 1.2 %depart.1 = f32[64,2,128]{2,1,0:T(2,128)} custom-call(s32[1,64]{1,0:T(1,128)S(1)} %copy-done.4, f32[64,2,128]{2,1,0:T(2,128)S(1)} %all_to_all.21.evolved_ref, f32[64,2,128]{2,1,0:T(2,128)S(1)} %bitcast.20), custom_call_target="tpu_custom_call" | custom-call | flops 32768 | bytes 196608 | tf_op jit(solution)/shard_map/depart/pallas_call | solution.py:176
  92.3 4.0 %sweep_own.3.own_ref = f32[1024,512]{1,0:T(8,128)S(1)} custom-call(s32[2]{0:T(128)S(1)} %pad_add_fusion.edge_ref, f32[1024,512]{1,0:T(8,128)} %bitcast.28, bf16[5,2,256,256]{3,2,1,0:T(8,128)(2,1)S(1)} %copy-done), custom_call_target="tpu_custom_call" | custom-call | flops 1610612736 | bytes 5242880 | tf_op jit(solution)/shard_map/sweep_own/pallas_call | solution.py:228
  96.3 0.0 collective-permute-done.2
  96.4 0.0 collective-permute-done.3
  96.4 2.5 %add_halo.1 = f32[1024,512]{1,0:T(8,128)} custom-call(f32[1024,512]{1,0:T(8,128)S(1)} %sweep_own.3.own_ref, bf16[1024,256]{1,0:T(8,128)(2,1)S(1)} %bitcast.17, bf16[1024,256]{1,0:T(8,128)(2,1)S(1)} %bitcast.18, bf16[5,2,256,256]{3,2,1,0:T(8,128)(2,1)S(1)} %copy-done), custom_call_target="tpu_custom_call" | custom-call | flops 536870912 | bytes 5242880 | tf_op jit(solution)/shard_map/add_halo/pallas_call | solution.py:535
Async XLA Ops:
  0.6 11.3 %copy-start = (bf16[5,2,256,256]{3,2,1,0:T(8,128)(2,1)S(1)}, bf16[5,2,256,256]{3,2,1,0:T(8,128)(2,1)}, u32[]{:S(2)}) copy-start(bf16[5,2,256,256]{3,2,1,0:T(8,128)(2,1)} %constant.16.clone.t_ref) | copy-start | bytes 3932164
  0.6 9.9 %copy-start.4 = (s32[1,64]{1,0:T(1,128)S(1)}, s32[1,64]{1,0:T(1,128)}, u32[]{:S(2)}) copy-start(s32[1,64]{1,0:T(1,128)} %count_ref.3) | copy-start | bytes 772
  0.7 9.9 %copy-start.3 = (f32[1,64,2,128]{3,2,1,0:T(2,128)S(1)}, f32[1,64,2,128]{3,2,1,0:T(2,128)}, u32[]{:S(2)}) copy-start(f32[1,64,2,128]{3,2,1,0:T(2,128)} %param.16) | copy-start | bytes 196612
  0.7 9.9 %copy-start.1 = (f32[1,64,2,128]{3,2,1,0:T(2,128)S(1)}, f32[1,64,2,128]{3,2,1,0:T(2,128)}, u32[]{:S(2)}) copy-start(f32[1,64,2,128]{3,2,1,0:T(2,128)} %param.15) | copy-start | bytes 196612
  0.7 9.9 %copy-start.2 = (s32[1,64,2,128]{3,2,1,0:T(2,128)S(1)}, s32[1,64,2,128]{3,2,1,0:T(2,128)}, u32[]{:S(2)}) copy-start(s32[1,64,2,128]{3,2,1,0:T(2,128)} %param.14) | copy-start | bytes 196612
  3.3 25.4 %collective-permute-start = (s16[16,64,256]{2,1,0:T(8,128)(2,1)}, s16[16,64,256]{2,1,0:T(8,128)(2,1)}, u32[]{:S(2)}, u32[]{:S(2)}) collective-permute-start(s16[16,64,256]{2,1,0:T(8,128)(2,1)} %get-tuple-element.15), channel_id=1, source_target_pairs={{0,4},{4,8},{8,12},{12,16},{16,20},{20,24},{24,28},{28,32},{32,36}... | collective-permute-start | bytes 1572872 | tf_op jit(solution)/shard_map/ppermute | solution.py:551
  8.3 20.4 %collective-permute-start.1 = (s16[16,64,256]{2,1,0:T(8,128)(2,1)}, s16[16,64,256]{2,1,0:T(8,128)(2,1)}, u32[]{:S(2)}, u32[]{:S(2)}) collective-permute-start(s16[16,64,256]{2,1,0:T(8,128)(2,1)} %get-tuple-element.16), channel_id=1, source_target_pairs={{4,0},{8,4},{12,8},{16,12},{20,16},{24,20},{28,24},{32,28},{36,32}... | collective-permute-start | bytes 1572872 | tf_op jit(solution)/shard_map/ppermute | solution.py:552
  16.0 22.8 %all-to-all-start.1 = ((s16[64,2,384]{2,1,0:T(2,128)(2,1)}), s16[64,2,384]{2,1,0:T(2,128)(2,1)}, u32[]{:S(2)}, u32[]{:S(2)}) async-start(s16[64,2,384]{2,1,0:T(2,128)(2,1)} %pack.1), calls=%async_computation.1 | async-start | bytes 196608 | tf_op jit(solution)/shard_map/all_to_all | solution.py:587
  28.7 14.2 %copy-start.5 = (s32[1,64,2]{1,2,0:T(2,128)S(1)}, s32[1,64,2]{1,2,0:T(2,128)}, u32[]{:S(2)}) copy-start(s32[1,64,2]{1,2,0:T(2,128)} %param.12) | copy-start | bytes 1540
  38.7 10.8 %all-to-all-start = ((bf16[4,320,128]{2,1,0:T(8,128)(2,1)}), bf16[4,320,128]{2,1,0:T(8,128)(2,1)S(1)}, u32[]{:S(2)}, u32[]{:S(2)}) async-start(bf16[4,320,128]{2,1,0:T(8,128)(2,1)} %bitcast.25), calls=%async_computation | async-start | bytes 655360 | tf_op jit(solution)/shard_map/all_to_all | solution.py:597
  65.5 30.9 %collective-permute-start.2 = (bf16[16,64,256]{2,1,0:T(8,128)(2,1)S(1)}, bf16[16,64,256]{2,1,0:T(8,128)(2,1)S(1)}, u32[]{:S(2)}, u32[]{:S(2)}) collective-permute-start(bf16[16,64,256]{2,1,0:T(8,128)(2,1)S(1)} %get-tuple-element.22), channel_id=1, source_target_pairs={{0,4},{4,8},{8,12},{12,16},{16,20},{20,24},{24,28},{28,32},{32,36}... | collective-permute-start | bytes 1572872 | tf_op jit(solution)/shard_map/ppermute | solution.py:551
  70.4 26.0 %collective-permute-start.3 = (bf16[16,64,256]{2,1,0:T(8,128)(2,1)S(1)}, bf16[16,64,256]{2,1,0:T(8,128)(2,1)S(1)}, u32[]{:S(2)}, u32[]{:S(2)}) collective-permute-start(bf16[16,64,256]{2,1,0:T(8,128)(2,1)S(1)} %get-tuple-element.23), channel_id=1, source_target_pairs={{4,0},{8,4},{12,8},{16,12},{20,16},{24,20},{28,24},{32,28},{36,32}... | collective-permute-start | bytes 1572872 | tf_op jit(solution)/shard_map/ppermute | solution.py:552

commit v3 on v2

v3 whole, which is shorter than its diff:
```python
import functools
import math

import jax
import jax.numpy as jnp
import numpy as np
from jax import lax
from jax.experimental import pallas as pl
from jax.experimental.pallas import tpu as pltpu
from jax.sharding import PartitionSpec as P


NY = 64
SWEEPS = 4
SWEEP_SCALE = 0.2**SWEEPS
HALF = SWEEPS * NY

CONTROL_STEP = 8.0 / 32704.0
INNOVATION_STEP = 1.5 / 32700.0
WEIGHT_STEP = 10.0 / 32700.0

F32 = jnp.float32
BF16 = jnp.bfloat16
I16 = jnp.int16
I32 = jnp.int32

VMEM = pl.BlockSpec(memory_space=pltpu.VMEM)
HBM = pl.BlockSpec(memory_space=pltpu.HBM)
SMEM = pl.BlockSpec(memory_space=pltpu.SMEM)


def sweep_matrices():
    y_part = np.eye(NY) + np.eye(NY, k=1) + np.eye(NY, k=-1)
    powers = [np.linalg.matrix_power(y_part, n) for n in range(SWEEPS + 1)]
    by_distance = [np.zeros((NY, NY)) for _ in range(SWEEPS + 1)]
    for k in range(SWEEPS + 1):
        for ups in range(k + 1):
            distance = 2 * ups - k
            if distance >= 0:
                by_distance[distance] = (
                    by_distance[distance]
                    + math.comb(SWEEPS, k) * math.comb(k, ups) * powers[SWEEPS - k]
                )

    def block(distance_of, image_of=None):
        full = np.zeros((HALF, HALF))
        for xi in range(SWEEPS):
            for xo in range(SWEEPS):
                piece = np.zeros((NY, NY))
                if distance_of(xi, xo) <= SWEEPS:
                    piece = piece + by_distance[distance_of(xi, xo)]
                if image_of is not None and image_of(xi, xo) <= SWEEPS:
                    piece = piece - by_distance[image_of(xi, xo)]
                full[xi * NY : (xi + 1) * NY, xo * NY : (xo + 1) * NY] = piece
        return full

    last = SWEEPS - 1
    same = lambda xi, xo: abs(xi - xo)
    blocks = [
        block(same, lambda xi, xo: xi + xo + 2),
        block(same),
        block(same, lambda xi, xo: (last - xi) + (last - xo) + 2),
        block(lambda xi, xo: xo + SWEEPS - xi),
        block(lambda xi, xo: xi + SWEEPS - xo),
    ]
    return np.stack(blocks).astype(jnp.bfloat16)


def split_high_low(values):
    high = values.astype(BF16)
    return high, (values - high.astype(F32)).astype(BF16)


def mm(a, b):
    return jnp.dot(a, b, preferred_element_type=F32)


def mm_nt(a, b):
    return lax.dot_general(a, b, (((1,), (1,)), ((), ())), preferred_element_type=F32)


def in_vmem(x):
    return pltpu.with_memory_space_constraint(x, pltpu.VMEM)


def in_hbm(x):
    return pltpu.with_memory_space_constraint(x, pltpu.HBM)


def params(**extra):
    return pltpu.CompilerParams(vmem_limit_bytes=24 * 1024 * 1024, **extra)


def cost(flops, bytes_accessed):
    return pl.CostEstimate(flops=flops, bytes_accessed=bytes_accessed, transcendentals=0)


ENCODE_STEP = 4


def encode_kernel(
    count_ref,
    x_hbm,
    channel_hbm,
    innovation_hbm,
    weight_hbm,
    low_hbm,
    high_hbm,
    packed_hbm,
    x_ref,
    channel_ref,
    innovation_ref,
    weight_ref,
    low_ref,
    high_ref,
    packed_ref,
    in_sems,
    obs_sems,
    low_sems,
    high_sems,
    packed_sem,
):
    turns = x_hbm.shape[0] // ENCODE_STEP
    owners, slots, observed = channel_hbm.shape

    def chunk(source, target, sems, turn):
        at = pl.ds(turn * ENCODE_STEP, ENCODE_STEP)
        return pltpu.make_async_copy(source.at[at], target.at[at], sems.at[turn])

    obs_loads = [
        pltpu.make_async_copy(channel_hbm, channel_ref, obs_sems.at[0]),
        pltpu.make_async_copy(innovation_hbm, innovation_ref, obs_sems.at[1]),
        pltpu.make_async_copy(weight_hbm, weight_ref, obs_sems.at[2]),
    ]
    for turn in range(turns - 1):
        chunk(x_hbm, x_ref, in_sems, turn).start()
    for copy in obs_loads:
        copy.start()
    chunk(x_hbm, x_ref, in_sems, turns - 1).start()
    saves = []

    def encode_chunk(turn):
        chunk(x_hbm, x_ref, in_sems, turn).wait()
        at = slice(turn * ENCODE_STEP, (turn + 1) * ENCODE_STEP)
        coded = jnp.round(x_ref[at] * (1.0 / CONTROL_STEP)).astype(I32).astype(I16)
        low_ref[at] = coded[:, :, :HALF]
        high_ref[at] = coded[:, :, HALF:]
        for source, target, sems in (
            (low_ref, low_hbm, low_sems),
            (high_ref, high_hbm, high_sems),
        ):
            saves.append(chunk(source, target, sems, turn))
            saves[-1].start()

    for turn in range(turns - 1):
        encode_chunk(turn)
    for copy in obs_loads:
        copy.wait()
    slot_id = lax.broadcasted_iota(I32, (slots, observed), 0)
    for s in range(owners):
        filled = slot_id < count_ref[0, s]
        weight = jnp.where(filled, weight_ref[s] * (1.0 / WEIGHT_STEP), 0.0)
        innovation = innovation_ref[s] * (1.0 / INNOVATION_STEP)
        row = [channel_ref[s], jnp.round(innovation).astype(I32), jnp.round(weight).astype(I32)]
        for n, values in enumerate(row):
            packed_ref[s, :, n * observed : (n + 1) * observed] = values.astype(I16)
    saves.append(pltpu.make_async_copy(packed_ref, packed_hbm, packed_sem))
    saves[-1].start()
    encode_chunk(turns - 1)
    for copy in saves:
        copy.wait()


def encode(counts, control, channel, innovation, weight):
    members, levels, _ = control.shape
    owners, slots, observed = channel.shape
    turns = members // ENCODE_STEP
    half = (members, levels, HALF)
    packed = (owners, slots, 3 * observed)
    return pl.pallas_call(
        encode_kernel,
        out_shape=(pltpu.HBM(half, I16), pltpu.HBM(half, I16), pltpu.HBM(packed, I16)),
        in_specs=[SMEM, HBM, HBM, HBM, HBM],
        out_specs=(HBM, HBM, HBM),
        scratch_shapes=[
            pltpu.VMEM(control.shape, F32),
            pltpu.VMEM(channel.shape, I32),
            pltpu.VMEM(channel.shape, F32),
            pltpu.VMEM(channel.shape, F32),
            pltpu.VMEM(half, I16),
            pltpu.VMEM(half, I16),
            pltpu.VMEM(packed, I16),
            pltpu.SemaphoreType.DMA((turns,)),
            pltpu.SemaphoreType.DMA((3,)),
            pltpu.SemaphoreType.DMA((turns,)),
            pltpu.SemaphoreType.DMA((turns,)),
            pltpu.SemaphoreType.DMA,
        ],
        compiler_params=params(),
        cost_estimate=cost(4 * control.size, 6 * control.size),
        name="encode",
    )(counts, *[in_hbm(x) for x in (control, channel, innovation, weight)])


def depart_kernel(count_ref, evolved_ref, innovation_ref, o_ref):
    owners, slots, observed = evolved_ref.shape
    slot_id = lax.broadcasted_iota(I32, (slots, observed), 0)
    for s in range(owners):
        filled = slot_id < count_ref[0, s]
        o_ref[s] = jnp.where(filled, evolved_ref[s], 0.0) - innovation_ref[s]


def depart(counts, evolved, innovation):
    return pl.pallas_call(
        depart_kernel,
        out_shape=jax.ShapeDtypeStruct(evolved.shape, F32),
        in_specs=[SMEM, VMEM, VMEM],
        out_specs=VMEM,
        compiler_params=params(),
        cost_estimate=cost(2 * evolved.size, 12 * evolved.size),
        name="depart",
    )(counts, evolved, innovation)


def sweep_rows(edge_ref, x_ref, t_ref, o_ref, step, ready):
    def apply(high, low, index):
        return mm(high, t_ref[index]) + mm(low, t_ref[index])

    def one(turn, carry):
        ready(turn)
        at = pl.ds(pl.multiple_of(turn * step, step), step)
        left_high, left_low = split_high_low(x_ref[at, :HALF] * SWEEP_SCALE)
        right_high, right_low = split_high_low(x_ref[at, HALF:] * SWEEP_SCALE)
        o_ref[at, :HALF] = apply(left_high, left_low, edge_ref[0]) + apply(
            right_high, right_low, 4
        )
        o_ref[at, HALF:] = apply(right_high, right_low, edge_ref[1]) + apply(
            left_high, left_low, 3
        )
        return carry

    lax.fori_loop(0, x_ref.shape[0] // step, one, 0)


def sweep_near_kernel(edge_ref, x_ref, t_ref, o_ref):
    sweep_rows(edge_ref, x_ref, t_ref, o_ref, 256, lambda turn: None)


def sweep_far_kernel(edge_ref, x_hbm, t_ref, o_ref, x_ref, sems):
    rows = x_hbm.shape[0]
    step = 256

    def load(turn):
        at = pl.ds(turn * step, step)
        return pltpu.make_async_copy(x_hbm.at[at], x_ref.at[at], sems.at[turn])

    for turn in range(rows // step):
        load(turn).start()
    sweep_rows(edge_ref, x_ref, t_ref, o_ref, step, lambda turn: load(turn).wait())


def sweep_own(edges, field, matrices, far):
    rows, columns = field.shape
    scratch = [pltpu.VMEM(field.shape, F32), pltpu.SemaphoreType.DMA((rows // 256,))]
    return pl.pallas_call(
        sweep_far_kernel if far else sweep_near_kernel,
        out_shape=jax.ShapeDtypeStruct((rows, columns), F32),
        in_specs=[SMEM, HBM if far else VMEM, VMEM],
        out_specs=VMEM,
        scratch_shapes=scratch if far else [],
        compiler_params=params(),
        cost_estimate=cost(2 * 6 * rows * columns * HALF, 10 * rows * columns),
        name="sweep_own",
    )(edges, in_hbm(field) if far else field, matrices)


LEVEL_STEP = 16


def level_copies(source, target, sems):
    def copy(turn):
        at = pl.ds(turn * LEVEL_STEP, LEVEL_STEP)
        return pltpu.make_async_copy(
            source.at[:, :, at, :], target.at[:, :, at, :], sems.at[turn]
        )

    return copy


def localize_sum_kernel(
    scale,
    place_ref,
    x_ref,
    low_ref,
    high_ref,
    ens_hbm,
    t_hbm,
    own_hbm,
    one_hbm,
    two_hbm,
    three_hbm,
    ens_ref,
    t_ref,
    w_even,
    w_odd,
    o_ref,
    in_sems,
    t_sem,
    out_sems,
):
    members, variables, levels, _ = ens_ref.shape
    blocks, width = o_ref.shape[0], o_ref.shape[3]
    step = LEVEL_STEP
    turns = levels // step
    load = level_copies(ens_hbm, ens_ref, in_sems)
    t_load = pltpu.make_async_copy(t_hbm, t_ref, t_sem)
    t_load.start()
    for turn in range(turns):
        load(turn).start()

    def apply(high, low, index):
        return mm(high, t_ref[index]) + mm(low, t_ref[index])

    def weigh(turn, w_ref):
        at = pl.ds(turn * step, step)
        rows = members * step
        left_high, left_low = split_high_low(x_ref[:, at, :HALF].reshape(rows, HALF))
        right_high, right_low = split_high_low(x_ref[:, at, HALF:].reshape(rows, HALF))

        def from_halo(halo_ref, index):
            coded = halo_ref[:, at, :].reshape(rows, HALF).astype(I32)
            upper = (coded >> 8).astype(F32).astype(BF16)
            lower = (coded & 255).astype(F32).astype(BF16)
            return (mm(upper, t_ref[index]) * 256.0 + mm(lower, t_ref[index])) * CONTROL_STEP

        left = (
            apply(left_high, left_low, place_ref[0])
            + apply(right_high, right_low, 4)
            + from_halo(low_ref, 3)
        )
        right = (
            apply(right_high, right_low, place_ref[1])
            + apply(left_high, left_low, 3)
            + from_halo(high_ref, 4)
        )
        left, right = left * SWEEP_SCALE, right * SWEEP_SCALE
        w_ref[:, :, :HALF] = left.astype(BF16).reshape(members, step, HALF)
        w_ref[:, :, HALF:] = right.astype(BF16).reshape(members, step, HALF)

    def total_up(turn, w_ref):
        at = pl.ds(turn * step, step)
        for k in range(blocks):
            across = slice(k * width, (k + 1) * width)
            totals = [None] * variables
            for m in range(members):
                weight = w_ref[m, :, across].astype(F32)
                for v in range(variables):
                    term = weight * ens_ref[m, v, at, across].astype(F32)
                    totals[v] = term if totals[v] is None else totals[v] + term
            for v in range(variables):
                o_ref[k, v, at, :] = (totals[v] * scale).astype(BF16)

    buffers = [w_even, w_odd]
    t_load.wait()
    weigh(0, buffers[0])
    for turn in range(turns):
        load(turn).wait()
        if turn + 1 < turns:
            weigh(turn + 1, buffers[(turn + 1) % 2])
        total_up(turn, buffers[turn % 2])
    mine = place_ref[2]
    copies = [
        pltpu.make_async_copy(o_ref.at[lax.rem(mine + s, blocks)], target, out_sems.at[s])
        for s, target in enumerate((own_hbm, one_hbm, two_hbm, three_hbm))
    ]
    for copy in copies:
        copy.start()
    for copy in copies:
        copy.wait()


def localize_sum(place, control, from_low, from_high, ensemble, matrices, scale, blocks):
    members, variables, levels, columns = ensemble.shape
    width = columns // blocks
    turns = levels // LEVEL_STEP
    piece = pltpu.HBM((variables, levels, width), BF16)
    return pl.pallas_call(
        functools.partial(localize_sum_kernel, scale),
        out_shape=(piece,) * blocks,
        in_specs=[SMEM, VMEM, VMEM, VMEM, HBM, HBM],
        out_specs=(HBM,) * blocks,
        scratch_shapes=[
            pltpu.VMEM(ensemble.shape, BF16),
            pltpu.VMEM(matrices.shape, BF16),
            pltpu.VMEM((members, LEVEL_STEP, columns), BF16),
            pltpu.VMEM((members, LEVEL_STEP, columns), BF16),
            pltpu.VMEM((blocks, variables, levels, width), BF16),
            pltpu.SemaphoreType.DMA((turns,)),
            pltpu.SemaphoreType.DMA,
            pltpu.SemaphoreType.DMA((blocks,)),
        ],
        compiler_params=params(),
        cost_estimate=cost(
            2 * 6 * members * levels * columns * HALF, 2 * ensemble.size + 8 * control.size
        ),
        name="localize_sum",
    )(
        place,
        in_vmem(control),
        in_vmem(from_low),
        in_vmem(from_high),
        in_hbm(ensemble),
        in_hbm(matrices),
    )


def obs_tables_kernel(
    obs_ref, own_hbm, slots_hbm, w_ref, b_ref, channel_ref, own_ref, slots_ref, sems
):
    copies = [
        pltpu.make_async_copy(own_hbm, own_ref, sems.at[0]),
        pltpu.make_async_copy(slots_hbm, slots_ref, sems.at[1]),
    ]
    for copy in copies:
        copy.start()
    owners, slots, _ = obs_ref.shape
    groups, _, width = w_ref.shape
    group_id = lax.broadcasted_iota(I32, (8, width), 0)
    lane_id = lax.broadcasted_iota(I32, (width, width), 0).astype(F32).astype(BF16)
    one_bf, zero_bf = jnp.ones((), BF16), jnp.zeros((), BF16)

    def one(owner, slot):
        row = obs_ref[owner].astype(I32)[slot : slot + 1]
        channel = row[:, :width]
        innovation = row[:, width : 2 * width].astype(F32) * INNOVATION_STEP
        weight = row[:, 2 * width :].astype(F32) * WEIGHT_STEP
        in_group = jnp.broadcast_to(channel >> 7, (8, width)) == group_id
        lane = (channel & 127).astype(F32).astype(BF16)
        one_hot = jnp.where(jnp.broadcast_to(lane, (width, width)) == lane_id, one_bf, zero_bf)

        def spread(values):
            return [
                jnp.where(in_group, jnp.broadcast_to(part.astype(F32), (8, width)), 0.0)
                for part in split_high_low(values)
            ]

        left = jnp.concatenate(spread(weight) + spread(weight * innovation), axis=0)
        sums = mm_nt(left.astype(BF16), one_hot)
        w_sum = sums[0:8] + sums[8:16]
        b_sum = sums[16:24] + sums[24:32]
        at = pl.ds(slot * owners + owner, 1)
        channel_ref[at, :] = channel
        for g in range(groups):
            w_ref[g, at, :] = w_sum[g : g + 1]
            b_ref[g, at, :] = b_sum[g : g + 1]

    unroll = 4

    def several(turn, carry):
        for inner in range(unroll):
            for slot in range(slots):
                one(turn * unroll + inner, slot)
        return carry

    lax.fori_loop(0, owners // unroll, several, 0)
    for copy in copies:
        copy.wait()


def obs_tables(obs, own, columns, channels):
    owners, slots, packed = obs.shape
    width = packed // 3
    rows = owners * slots
    shape = jax.ShapeDtypeStruct((channels // width, rows, width), F32)
    return pl.pallas_call(
        obs_tables_kernel,
        out_shape=(
            shape,
            shape,
            jax.ShapeDtypeStruct((rows, width), I32),
            jax.ShapeDtypeStruct(own.shape, own.dtype),
            jax.ShapeDtypeStruct(columns.shape, columns.dtype),
        ),
        in_specs=[VMEM, HBM, HBM],
        out_specs=(VMEM,) * 5,
        scratch_shapes=[pltpu.SemaphoreType.DMA((2,))],
        compiler_params=params(),
        cost_estimate=cost(2 * 32 * rows * width * width, 10 * rows * channels),
        name="obs_tables",
    )(obs, in_hbm(own), in_hbm(columns))


def observe_kernel(
    own_ref,
    one_ref,
    two_ref,
    three_ref,
    slots_ref,
    jac_ref,
    w_ref,
    b_ref,
    channel_ref,
    adj_ref,
    evolved_ref,
):
    groups, rows, width = w_ref.shape
    state = jac_ref.shape[0]
    slots, owners = slots_ref.shape
    total = own_ref[...].astype(F32)
    for part in (one_ref, two_ref, three_ref):
        total = total + part[...].astype(F32)
    increment = total.astype(BF16)
    columns = increment.shape[1]
    column_id = lax.broadcasted_iota(I32, (columns, rows), 0)
    table = jnp.concatenate([slots_ref[j : j + 1, :] for j in range(slots)], axis=1)
    hits = jnp.where(column_id == jnp.broadcast_to(table, (columns, rows)), 1.0, 0.0)
    hits = hits.astype(BF16)
    carried = mm(increment, hits).T.astype(BF16)
    column_adjoint = jnp.zeros((rows, state), F32)
    channel = channel_ref[...]
    group, lane = channel >> 7, channel & 127
    picked = jnp.zeros(channel.shape, F32)
    for g in range(groups):
        jac = jac_ref[:, g * width : (g + 1) * width]
        model = mm(carried, jac)
        channel_adjoint = (model * w_ref[g] - b_ref[g]).astype(BF16)
        column_adjoint = column_adjoint + mm_nt(channel_adjoint, jac)
        taken = jnp.take_along_axis(model, lane, axis=1)
        picked = jnp.where(group == g, taken, picked)
    rounded = column_adjoint.T.astype(BF16)
    adj_ref[...] = mm_nt(rounded, hits).astype(BF16)
    for j in range(slots):
        evolved_ref[:, j, :] = picked[j * owners : (j + 1) * owners]


def observe(pieces, slots, jacobian, w_table, b_table, channel):
    state, width = pieces[0].shape
    channels = jacobian.shape[1]
    rows = channel.shape[0]
    return pl.pallas_call(
        observe_kernel,
        out_shape=(
            jax.ShapeDtypeStruct((state, width), BF16),
            jax.ShapeDtypeStruct((slots.shape[1], slots.shape[0], width), F32),
        ),
        in_specs=[VMEM] * 9,
        out_specs=(VMEM, VMEM),
        compiler_params=params(),
        cost_estimate=cost(4 * rows * state * channels, 12 * rows * channels),
        name="observe",
    )(*pieces, slots, jacobian, w_table, b_table, channel)


def member_adjoint_kernel(
    scale,
    place_ref,
    ens_hbm,
    own_ref,
    one_ref,
    two_ref,
    three_ref,
    full_hbm,
    low_hbm,
    high_hbm,
    ens_ref,
    adj_ref,
    full_ref,
    low_ref,
    high_ref,
    sems,
    full_sems,
    low_sems,
    high_sems,
):
    members, variables, levels, _ = ens_ref.shape
    blocks, width = adj_ref.shape[0], adj_ref.shape[3]
    half_blocks = blocks // 2
    step = LEVEL_STEP
    load = level_copies(ens_hbm, ens_ref, sems)
    for turn in range(levels // step):
        load(turn).start()

    mine = place_ref[2]
    for back, part in enumerate((own_ref, one_ref, two_ref, three_ref)):
        adj_ref[lax.rem(mine + blocks - back, blocks)] = part[...]

    def saves(turn):
        at = pl.ds(turn * step, step)
        return [
            pltpu.make_async_copy(source.at[:, at, :], target.at[:, at, :], sem.at[turn])
            for source, target, sem in (
                (low_ref, low_hbm, low_sems),
                (high_ref, high_hbm, high_sems),
                (full_ref, full_hbm, full_sems),
            )
        ]

    def one(turn, carry):
        at = pl.ds(pl.multiple_of(turn * step, step), step)
        load(turn).wait()
        for k in range(blocks):
            adjoint = [adj_ref[k, v, at, :].astype(F32) * scale for v in range(variables)]
            half = low_ref if k < half_blocks else high_ref
            offset = (k % half_blocks) * width
            for m in range(members):
                total = None
                for v in range(variables):
                    term = ens_ref[m, v, at, k * width : (k + 1) * width].astype(F32) * adjoint[v]
                    total = term if total is None else total + term
                full_ref[m, at, k * width : (k + 1) * width] = total
                half[m, at, offset : offset + width] = total.astype(BF16)
        for copy in saves(turn):
            copy.start()
        return carry

    lax.fori_loop(0, levels // step, one, 0)
    for turn in range(levels // step):
        for copy in saves(turn):
            copy.wait()


def member_adjoint(place, ensemble, pieces, scale):
    members, variables, levels, columns = ensemble.shape
    width = pieces[0].shape[-1]
    half = pltpu.HBM((members, levels, HALF), BF16)
    turns = pltpu.SemaphoreType.DMA((levels // LEVEL_STEP,))
    return pl.pallas_call(
        functools.partial(member_adjoint_kernel, scale),
        out_shape=(pltpu.HBM((members, levels, columns), F32), half, half),
        in_specs=[SMEM, HBM, VMEM, VMEM, VMEM, VMEM],
        out_specs=(HBM, HBM, HBM),
        scratch_shapes=[
            pltpu.VMEM(ensemble.shape, BF16),
            pltpu.VMEM((columns // width, variables, levels, width), BF16),
            pltpu.VMEM((members, levels, columns), F32),
            pltpu.VMEM((members, levels, HALF), BF16),
            pltpu.VMEM((members, levels, HALF), BF16),
            turns,
            turns,
            turns,
            turns,
        ],
        compiler_params=params(),
        cost_estimate=cost(2 * ensemble.size, 4 * ensemble.size),
        name="member_adjoint",
    )(place, in_hbm(ensemble), *pieces)


def add_halo_kernel(own_ref, low_ref, high_ref, t_ref, o_ref):
    i = pl.program_id(0)
    members = o_ref.shape[0]
    levels = o_ref.shape[1]
    rows = members * levels
    at = pl.ds(i * members, members)

    def from_halo(halo_ref, index):
        halo = mm(halo_ref[at].reshape(rows, HALF), t_ref[index]) * SWEEP_SCALE
        return halo.reshape(members, levels, HALF)

    o_ref[:, :, :HALF] = own_ref[at, :, :HALF] + from_halo(low_ref, 3)
    o_ref[:, :, HALF:] = own_ref[at, :, HALF:] + from_halo(high_ref, 4)


def add_halo(own, from_low, from_high, matrices):
    members, levels, columns = own.shape
    step = 4
    return pl.pallas_call(
        add_halo_kernel,
        out_shape=jax.ShapeDtypeStruct(own.shape, F32),
        grid=(members // step,),
        in_specs=[VMEM] * 4,
        out_specs=pl.BlockSpec((step, levels, columns), lambda i: (i, 0, 0)),
        compiler_params=params(),
        cost_estimate=cost(2 * own.size * HALF, 10 * own.size),
        name="add_halo",
    )(own, in_vmem(from_low), in_vmem(from_high), matrices)


def to_members(pieces):
    count = lax.axis_size("mem")
    received = []
    for shift, piece in enumerate(pieces, 1):
        pairs = [(i, (i + shift) % count) for i in range(count)]
        received.append(lax.ppermute(piece, "mem", pairs))
    return received


def keep_kernel(count_ref, innovation_ref, o_ref):
    owners, slots, observed = innovation_ref.shape
    slot_id = lax.broadcasted_iota(I32, (slots, observed), 0)
    for s in range(owners):
        o_ref[s] = jnp.where(slot_id < count_ref[0, s], innovation_ref[s], 0.0)


def keep_filled(counts, innovation):
    return pl.pallas_call(
        keep_kernel,
        out_shape=jax.ShapeDtypeStruct(innovation.shape, F32),
        in_specs=[SMEM, VMEM],
        out_specs=VMEM,
        compiler_params=params(),
        cost_estimate=cost(innovation.size, 8 * innovation.size),
        name="keep_filled",
    )(counts, innovation)


def swap_halos(low_half, high_half):
    count = lax.axis_size("tile")
    forward = [(i, i + 1) for i in range(count - 1)]
    backward = [(i + 1, i) for i in range(count - 1)]
    from_low = lax.ppermute(high_half, "tile", forward)
    from_high = lax.ppermute(low_half, "tile", backward)
    return from_low, from_high


def body(
    control,
    ensemble,
    jacobian,
    send_columns,
    received_counts,
    observed_channel,
    innovation,
    error_weight,
):
    members, levels, columns = control.shape
    variables = ensemble.shape[1]
    state = variables * levels
    groups = lax.axis_size("mem")
    owners = lax.axis_size("tile")
    scale = 1.0 / math.sqrt(members * groups)
    width = columns // groups
    channels = jacobian.shape[0]
    tile_index = lax.axis_index("tile")
    matrices = jnp.asarray(sweep_matrices())
    place = jnp.stack(
        [
            jnp.where(tile_index == 0, 0, 1),
            jnp.where(tile_index == owners - 1, 2, 1),
            lax.axis_index("mem"),
        ]
    ).astype(I32)
    counts = received_counts
    low_half, high_half, packed = encode(
        counts, control, observed_channel[0], innovation[0], error_weight[0]
    )
    from_low, from_high = swap_halos(low_half, high_half)
    obs = lax.all_to_all(packed, "tile", split_axis=0, concat_axis=0, tiled=True)
    pieces = localize_sum(place, control, from_low, from_high, ensemble, matrices, scale, groups)
    pieces = [piece.reshape(state, width) for piece in pieces]
    received = to_members(pieces[1:])
    w_table, b_table, channel, own, carried = obs_tables(
        obs, pieces[0], jnp.transpose(send_columns[0]), channels
    )
    block_adjoint, evolved = observe(
        [own] + received,
        carried,
        jnp.transpose(jacobian),
        w_table,
        b_table,
        channel,
    )
    adjoint = [block_adjoint] + to_members([block_adjoint] * (groups - 1))
    adjoint = [piece.reshape(variables, levels, width) for piece in adjoint]
    evolved = lax.all_to_all(evolved, "tile", split_axis=0, concat_axis=0, tiled=True)
    kept = keep_filled(counts, innovation[0])
    full, low_half, high_half = member_adjoint(place, ensemble, adjoint, scale)
    from_low, from_high = swap_halos(low_half, high_half)
    own = sweep_own(place, full.reshape(members * levels, columns), matrices, True)
    departures = depart(counts, evolved, kept)
    gradient = add_halo(
        own.reshape(members, levels, columns), from_low, from_high, matrices
    )
    return gradient, departures[None]


def solution(mesh):
    in_specs = (
        P("mem", None, "tile"),
        P("mem", None, None, "tile"),
        P(),
        P(("tile", "mem"), None, None),
        P(("tile", "mem"), None),
        P(("tile", "mem"), None, None, None),
        P(("tile", "mem"), None, None, None),
        P(("tile", "mem"), None, None, None),
    )
    out_specs = (P("mem", None, "tile"), P(("tile", "mem"), None, None, None))
    return jax.shard_map(body, mesh=mesh, in_specs=in_specs, out_specs=out_specs, check_vma=False)
```

time: 99.5 us -> 90.8 us (0.913)
  blocking collectives: 28.1 us -> 0 us
  starting transfers between devices: 30.9 us -> 46.2 us
  waiting for transfers between devices: 4.23 us -> 11.5 us
  Pallas kernels: 33.2 us -> 30.3 us
    all_to_all x2 -> x0, blocking collectives: 28.1 us -> none  [the longest x1 17.9 us: body(): lax.all_to_all(evolved, 'tile', split_axis=0, concat_axis=0, tiled=True)]
    all_to_all x1, starting transfers between devices: 4.18 us -> 11.6 us  [body(): lax.all_to_all(evolved, 'tile', split_axis=0, concat_axis=0, tiled=True)]
    ppermute x0 -> x6, starting transfers between devices: none -> 7.25 us  [to_members(): received.append(lax.ppermute(piece, 'mem', pairs))]
    all_to_all x1, waiting for transfers between devices: 0.02 us -> 6.33 us  [body(): lax.all_to_all(evolved, 'tile', split_axis=0, concat_axis=0, tiled=True)]
    ppermute x0 -> x6, waiting for transfers between devices: none -> 5.13 us  [to_members(): received.append(lax.ppermute(piece, 'mem', pairs))]
    pallas_call x2 -> x1, Pallas kernels: 8.01 us -> 3.42 us  [sweep_own(): pl.pallas_call(sweep_far_kernel if far else sweep_near_kernel, out_shape=...]
    all_to_all x1, waiting for transfers between devices: 4.2 us -> 0.01 us  [body(): lax.all_to_all(packed, 'tile', split_axis=0, concat_axis=0, tiled=True)]
    pallas_call x6 -> x5, Pallas kernels: 15.3 us -> 16 us  [the longest x1 7.01 us: localize_sum(): pl.pallas_call(functools.partial(localize_sum_kernel, scale), out_shape=(...]
  transfers between devices with their start and end apart: 6 -> 12, of which waited for: 1 -> 4; matrix products, arithmetic and copies ran while one was open for 2% -> 0% of each run, Pallas kernels for 23% -> 19%
where the time goes in v3:
time: 90.8 us; the launch traced here: 90.4 us
  starting transfers between devices  46.2 us (51%)
  Pallas kernels  30.3 us (33%)
  waiting for transfers between devices  11.5 us (13%)
  local copies, waits for them, and re-layouts  1.48 us (2%)
    all_to_all x1, starting transfers between devices, body(): lax.all_to_all(packed, 'tile', split_axis=0, concat_axis=0, tiled=True)  13.1 us
    all_to_all x1, starting transfers between devices, body(): lax.all_to_all(evolved, 'tile', split_axis=0, concat_axis=0, tiled=True)  11.6 us
    ppermute x2, starting transfers between devices, swap_halos(): from_low = lax.ppermute(high_half, 'tile', forward)  10.4 us
    ppermute x6, starting transfers between devices, to_members(): received.append(lax.ppermute(piece, 'mem', pairs))  7.25 us
    pallas_call x1, Pallas kernels, localize_sum(): pl.pallas_call(functools.partial(localize_sum_kernel, scale), out_shape=(...  7.01 us
    all_to_all x1, waiting for transfers between devices, body(): lax.all_to_all(evolved, 'tile', split_axis=0, concat_axis=0, tiled=True)  6.33 us
    pallas_call x1, Pallas kernels, obs_tables(): pl.pallas_call(obs_tables_kernel, out_shape=(shape, shape, jax.ShapeDtype...  5.19 us
    ppermute x6, waiting for transfers between devices, to_members(): received.append(lax.ppermute(piece, 'mem', pairs))  5.13 us
  transfers between devices with their start and end apart: 12, of which 4 were waited for; matrix products, arithmetic and copies ran while one was open for 0% of the time, Pallas kernels for 19%

profile of v3, /device:TPU:1, one launch (start us, length us, event | category | flops | bytes accessed | tf_op | source)
XLA Modules:
  0.0 90.4 jit_solution(11634474697607068264)
XLA Ops:
  0.6 0.0 copy-start
  0.6 0.0 copy-start.4
  0.7 0.8 copy-done.4
  1.4 3.0 %encode.1 = (s16[16,64,256]{2,1,0:T(8,128)(2,1)}, s16[16,64,256]{2,1,0:T(8,128)(2,1)}, s16[64,2,384]{2,1,0:T(2,128)(2,1)}) custom-call(s32[1,64]{1,0:T(1,128)S(1)} %copy-done.4, f32[16,64,512]{2,1,0:T(8,128)} %x_ref.1, s32[64,2,128]{2,1,0:T(2,128)} %bitcast.29, f32[64,2,128]{2,1,0:T(2,128)} %bitcast.23, f32[64,2,128]{2,1,0:T(2,128)} %bitcast.30), custom_call_target="tpu_custom_call" | custom-call | flops 2097152 | bytes 3145728 | tf_op jit(solution)/shard_map/encode/pallas_call | solution.py:180
  4.4 4.9 %collective-permute-start = (s16[16,64,256]{2,1,0:T(8,128)(2,1)}, s16[16,64,256]{2,1,0:T(8,128)(2,1)S(1)}, u32[]{:S(2)}, u32[]{:S(2)}) collective-permute-start(s16[16,64,256]{2,1,0:T(8,128)(2,1)} %get-tuple-element.20), channel_id=1, source_target_pairs={{0,4},{4,8},{8,12},{12,16},{16,20},{20,24},{24,28},{28,32},{32,36}... | collective-permute-start | bytes 1572872 | tf_op jit(solution)/shard_map/ppermute | solution.py:711
  9.4 1.9 %collective-permute-start.1 = (s16[16,64,256]{2,1,0:T(8,128)(2,1)}, s16[16,64,256]{2,1,0:T(8,128)(2,1)S(1)}, u32[]{:S(2)}, u32[]{:S(2)}) collective-permute-start(s16[16,64,256]{2,1,0:T(8,128)(2,1)} %get-tuple-element.21), channel_id=1, source_target_pairs={{4,0},{8,4},{12,8},{16,12},{20,16},{24,20},{28,24},{32,28},{36,32}... | collective-permute-start | bytes 1572872 | tf_op jit(solution)/shard_map/ppermute | solution.py:712
  11.3 13.1 %all-to-all-start = ((s16[64,2,384]{2,1,0:T(2,128)(2,1)}), s16[64,2,384]{2,1,0:T(2,128)(2,1)}, u32[]{:S(2)}, u32[]{:S(2)}) async-start(s16[64,2,384]{2,1,0:T(2,128)(2,1)} %get-tuple-element.19), calls=%async_computation | async-start | bytes 196608 | tf_op jit(solution)/shard_map/all_to_all | solution.py:748
  24.4 0.1 pad_add_fusion.place_ref.edge_ref
  24.5 0.0 copy-start.6
  24.5 0.0 copy-start.2
  24.5 0.0 collective-permute-done.low_ref
  24.5 0.0 collective-permute-done.1.high_ref
  24.5 0.0 copy-done
  24.5 7.0 %localize_sum.1 = (bf16[5,64,128]{2,1,0:T(8,128)(2,1)}, bf16[5,64,128]{2,1,0:T(8,128)(2,1)}, bf16[5,64,128]{2,1,0:T(8,128)(2,1)}, bf16[5,64,128]{2,1,0:T(8,128)(2,1)}) custom-call(s32[3]{0:T(128)S(1)} %pad_add_fusion.place_ref.edge_ref, f32[16,64,512]{2,1,0:T(8,128)S(1)} %copy-done, s16[16,64,256]{2,1,0:T(8,128)(2,1)S(1)} %collective-permute-done.low_ref, ...), custom_call_target="tpu_custom_call" | custom-call | flops 1610612736 | bytes 9437184 | tf_op jit(solution)/shard_map/localize_sum/pallas_call | solution.py:387
  31.5 0.0 copy-done.6
  31.5 1.4 %collective-permute-start.2 = (bf16[320,128]{1,0:T(8,128)(2,1)}, bf16[320,128]{1,0:T(8,128)(2,1)S(1)}, u32[]{:S(2)}, u32[]{:S(2)}) collective-permute-start(bf16[320,128]{1,0:T(8,128)(2,1)} %bitcast.36), channel_id=1, source_target_pairs={{0,1},{1,2},{2,3},{3,0},{4,5},{5,6},{6,7},{7,4},{8,9},{9,10},{10,1... | collective-permute-start | bytes 245768 | tf_op jit(solution)/shard_map/ppermute | solution.py:684
  32.9 2.6 %collective-permute-start.3 = (bf16[320,128]{1,0:T(8,128)(2,1)}, bf16[320,128]{1,0:T(8,128)(2,1)S(1)}, u32[]{:S(2)}, u32[]{:S(2)}) collective-permute-start(bf16[320,128]{1,0:T(8,128)(2,1)} %bitcast.34), channel_id=1, source_target_pairs={{0,2},{1,3},{2,0},{3,1},{4,6},{5,7},{6,4},{7,5},{8,10},{9,11},{10,... | collective-permute-start | bytes 245768 | tf_op jit(solution)/shard_map/ppermute | solution.py:684
  35.5 1.1 %collective-permute-start.4 = (bf16[320,128]{1,0:T(8,128)(2,1)}, bf16[320,128]{1,0:T(8,128)(2,1)S(1)}, u32[]{:S(2)}, u32[]{:S(2)}) collective-permute-start(bf16[320,128]{1,0:T(8,128)(2,1)} %bitcast.33), channel_id=1, source_target_pairs={{0,3},{1,0},{2,1},{3,2},{4,7},{5,4},{6,5},{7,6},{8,11},{9,8},{10,9... | collective-permute-start | bytes 245768 | tf_op jit(solution)/shard_map/ppermute | solution.py:684
  36.6 0.0 all-to-all-done.obs_ref
  36.6 5.2 %obs_tables.1 = (f32[5,128,128]{2,1,0:T(8,128)S(1)}, f32[5,128,128]{2,1,0:T(8,128)S(1)}, s32[128,128]{1,0:T(8,128)S(1)}, bf16[320,128]{1,0:T(8,128)(2,1)S(1)}, s32[2,64]{1,0:T(2,128)S(1)}) custom-call(s16[64,2,384]{2,1,0:T(2,128)(2,1)} %all-to-all-done.obs_ref, bf16[320,128]{1,0:T(8,128)(2,1)} %bitcast.35, s32[2,64]{1,0:T(2,128)} %bitcast.37), custom_call_target="tpu_custom_call" | custom-call | flops 134217728 | bytes 819200 | tf_op jit(solution)/shard_map/obs_tables/pallas_call | solution.py:475
  41.8 0.0 collective-permute-done.2.one_ref
  41.8 0.0 collective-permute-done.3.two_ref
  41.8 0.0 collective-permute-done.4.three_ref
  41.8 0.0 copy-done.2
  41.8 2.1 %observe.1 = (bf16[320,128]{1,0:T(8,128)(2,1)S(1)}, f32[64,2,128]{2,1,0:T(2,128)}) custom-call(bf16[320,128]{1,0:T(8,128)(2,1)S(1)} %get-tuple-element.23.own_ref, bf16[320,128]{1,0:T(8,128)(2,1)S(1)} %collective-permute-done.2.one_ref, bf16[320,128]{1,0:T(8,128)(2,1)S(1)} %collective-permute-done.3.two_ref, ...), custom_call_target="tpu_custom_call" | custom-call | flops 104857600 | bytes 983040 | tf_op jit(solution)/shard_map/observe/pallas_call | solution.py:540
  43.9 0.6 collective-permute-start.7
  44.6 1.6 %collective-permute-start.6 = (bf16[320,128]{1,0:T(8,128)(2,1)S(1)}, bf16[320,128]{1,0:T(8,128)(2,1)S(1)}, u32[]{:S(2)}, u32[]{:S(2)}) collective-permute-start(bf16[320,128]{1,0:T(8,128)(2,1)S(1)} %get-tuple-element.31), channel_id=1, source_target_pairs={{0,2},{1,3},{2,0},{3,1},{4,6},{5,7},{6,4},{7,5},{8,10},{9,11},{10,... | collective-permute-start | bytes 245768 | tf_op jit(solution)/shard_map/ppermute | solution.py:684
  46.1 0.0 collective-permute-start.5
  46.1 1.1 %collective-permute-done.7 = bf16[320,128]{1,0:T(8,128)(2,1)S(1)} collective-permute-done((bf16[320,128]{1,0:T(8,128)(2,1)S(1)}, bf16[320,128]{1,0:T(8,128)(2,1)S(1)}, u32[]{:S(2)}, u32[]{:S(2)}) %collective-permute-start.7) | collective-permute-done | bytes 81952 | tf_op jit(solution)/shard_map/ppermute | solution.py:684
  47.2 2.1 %collective-permute-done.6 = bf16[320,128]{1,0:T(8,128)(2,1)S(1)} collective-permute-done((bf16[320,128]{1,0:T(8,128)(2,1)S(1)}, bf16[320,128]{1,0:T(8,128)(2,1)S(1)}, u32[]{:S(2)}, u32[]{:S(2)}) %collective-permute-start.6) | collective-permute-done | bytes 81952 | tf_op jit(solution)/shard_map/ppermute | solution.py:684
  49.4 1.9 %collective-permute-done.5 = bf16[320,128]{1,0:T(8,128)(2,1)S(1)} collective-permute-done((bf16[320,128]{1,0:T(8,128)(2,1)S(1)}, bf16[320,128]{1,0:T(8,128)(2,1)S(1)}, u32[]{:S(2)}, u32[]{:S(2)}) %collective-permute-start.5) | collective-permute-done | bytes 81952 | tf_op jit(solution)/shard_map/ppermute | solution.py:684
  51.2 0.0 copy-start.7
  51.2 0.7 copy-done.7
  51.9 0.0 copy-start.3
  51.9 0.0 copy-start.5
  51.9 0.0 copy-start.1
  51.9 0.0 copy-start.8
  51.9 4.4 %member_adjoint.1 = (f32[16,64,512]{2,1,0:T(8,128)}, bf16[16,64,256]{2,1,0:T(8,128)(2,1)}, bf16[16,64,256]{2,1,0:T(8,128)(2,1)}) custom-call(s32[3]{0:T(128)S(1)} %copy-done.7, bf16[16,5,64,512]{3,2,1,0:T(8,128)(2,1)} %ens_hbm.3, bf16[5,64,128]{2,1,0:T(8,128)(2,1)S(1)} %bitcast.25, bf16[5,64,128]{2,1,0:T(8,128)(2,1)S(1)} %bitcast.28, ...), custom_call_target="tpu_custom_call" | custom-call | flops 5242880 | bytes 10485760 | tf_op jit(solution)/shard_map/member_adjoint/pallas_call | solution.py:627
  56.4 5.5 %collective-permute-start.8 = (bf16[16,64,256]{2,1,0:T(8,128)(2,1)}, bf16[16,64,256]{2,1,0:T(8,128)(2,1)S(1)}, u32[]{:S(2)}, u32[]{:S(2)}) collective-permute-start(bf16[16,64,256]{2,1,0:T(8,128)(2,1)} %get-tuple-element.33), channel_id=1, source_target_pairs={{0,4},{4,8},{8,12},{12,16},{16,20},{20,24},{24,28},{28,32},{32,36}... | collective-permute-start | bytes 1572872 | tf_op jit(solution)/shard_map/ppermute | solution.py:711
  61.8 1.9 %collective-permute-start.9 = (bf16[16,64,256]{2,1,0:T(8,128)(2,1)}, bf16[16,64,256]{2,1,0:T(8,128)(2,1)}, u32[]{:S(2)}, u32[]{:S(2)}) collective-permute-start(bf16[16,64,256]{2,1,0:T(8,128)(2,1)} %get-tuple-element.34), channel_id=1, source_target_pairs={{4,0},{8,4},{12,8},{16,12},{20,16},{24,20},{28,24},{32,28},{36,32}... | collective-permute-start | bytes 1572872 | tf_op jit(solution)/shard_map/ppermute | solution.py:712
  63.8 0.0 copy-done.3
  63.8 0.0 copy-done.5
  63.8 0.6 keep_filled.1.innovation_ref
  64.4 11.6 %all-to-all-start.1 = ((f32[64,2,128]{2,1,0:T(2,128)}), f32[64,2,128]{2,1,0:T(2,128)S(1)}, u32[]{:S(2)}, u32[]{:S(2)}) async-start(f32[64,2,128]{2,1,0:T(2,128)} %get-tuple-element.35), calls=%async_computation.1 | async-start | bytes 131072 | tf_op jit(solution)/shard_map/all_to_all | solution.py:765
  76.0 0.0 copy-done.1
  76.0 0.0 copy-done.8
  76.0 3.4 %sweep_own.1 = f32[1024,512]{1,0:T(8,128)S(1)} custom-call(s32[3]{0:T(128)S(1)} %copy-done.8, f32[1024,512]{1,0:T(8,128)} %bitcast.32, bf16[5,256,256]{2,1,0:T(8,128)(2,1)S(1)} %copy-done.1), custom_call_target="tpu_custom_call" | custom-call | flops 1610612736 | bytes 5242880 | tf_op jit(solution)/shard_map/sweep_own/pallas_call | solution.py:265
  79.5 6.3 %all-to-all-done.1.evolved_ref = f32[64,2,128]{2,1,0:T(2,128)S(1)} async-done(((f32[64,2,128]{2,1,0:T(2,128)}), f32[64,2,128]{2,1,0:T(2,128)S(1)}, u32[]{:S(2)}, u32[]{:S(2)}) %all-to-all-start.1) | async-done | bytes 65568 | tf_op jit(solution)/shard_map/all_to_all | solution.py:765
  85.8 1.2 %depart.1 = f32[64,2,128]{2,1,0:T(2,128)} custom-call(s32[1,64]{1,0:T(1,128)S(1)} %copy-done.5, f32[64,2,128]{2,1,0:T(2,128)S(1)} %all-to-all-done.1.evolved_ref, f32[64,2,128]{2,1,0:T(2,128)S(1)} %keep_filled.1.innovation_ref), custom_call_target="tpu_custom_call" | custom-call | flops 32768 | bytes 196608 | tf_op jit(solution)/shard_map/depart/pallas_call | solution.py:214
  87.0 0.0 collective-permute-done.8.low_ref
  87.0 0.0 collective-permute-done.9.high_ref
  87.0 3.3 %add_halo.1 = f32[16,64,512]{2,1,0:T(8,128)} custom-call(f32[16,64,512]{2,1,0:T(8,128)S(1)} %bitcast.21, bf16[16,64,256]{2,1,0:T(8,128)(2,1)S(1)} %collective-permute-done.8.low_ref, bf16[16,64,256]{2,1,0:T(8,128)(2,1)} %collective-permute-done.9.high_ref, bf16[5,256,256]{2,1,0:T(8,128)(2,1)S(1)} %copy-done.1), custom_call_target="tpu_custom_call" | custom-call | flops 268435456 | bytes 5242880 | tf_op jit(solution)/shard_map/add_halo/pallas_call | solution.py:667
Async XLA Ops:
  0.6 23.8 %copy-start = (f32[16,64,512]{2,1,0:T(8,128)S(1)}, f32[16,64,512]{2,1,0:T(8,128)}, u32[]{:S(2)}) copy-start(f32[16,64,512]{2,1,0:T(8,128)} %x_ref.1) | copy-start | bytes 6291460
  0.6 0.8 copy-start.4
  4.4 20.0 %collective-permute-start = (s16[16,64,256]{2,1,0:T(8,128)(2,1)}, s16[16,64,256]{2,1,0:T(8,128)(2,1)S(1)}, u32[]{:S(2)}, u32[]{:S(2)}) collective-permute-start(s16[16,64,256]{2,1,0:T(8,128)(2,1)} %get-tuple-element.20), channel_id=1, source_target_pairs={{0,4},{4,8},{8,12},{12,16},{16,20},{20,24},{24,28},{28,32},{32,36}... | collective-permute-start | bytes 1572872 | tf_op jit(solution)/shard_map/ppermute | solution.py:711
  9.4 15.1 %collective-permute-start.1 = (s16[16,64,256]{2,1,0:T(8,128)(2,1)}, s16[16,64,256]{2,1,0:T(8,128)(2,1)S(1)}, u32[]{:S(2)}, u32[]{:S(2)}) collective-permute-start(s16[16,64,256]{2,1,0:T(8,128)(2,1)} %get-tuple-element.21), channel_id=1, source_target_pairs={{4,0},{8,4},{12,8},{16,12},{20,16},{24,20},{28,24},{32,28},{36,32}... | collective-permute-start | bytes 1572872 | tf_op jit(solution)/shard_map/ppermute | solution.py:712
  11.3 25.3 %all-to-all-start = ((s16[64,2,384]{2,1,0:T(2,128)(2,1)}), s16[64,2,384]{2,1,0:T(2,128)(2,1)}, u32[]{:S(2)}, u32[]{:S(2)}) async-start(s16[64,2,384]{2,1,0:T(2,128)(2,1)} %get-tuple-element.19), calls=%async_computation | async-start | bytes 196608 | tf_op jit(solution)/shard_map/all_to_all | solution.py:748
  24.5 7.1 %copy-start.6 = (s32[3]{0:T(128)}, s32[3]{0:T(128)S(1)}, u32[]{:S(2)}) copy-start(s32[3]{0:T(128)S(1)} %pad_add_fusion.place_ref.edge_ref) | copy-start | bytes 40
  24.5 17.4 %copy-start.2 = (bf16[640,320]{0,1:T(8,128)(2,1)S(1)}, bf16[640,320]{0,1:T(8,128)(2,1)}, u32[]{:S(2)}) copy-start(bf16[640,320]{0,1:T(8,128)(2,1)} %param.11) | copy-start | bytes 1228804
  31.5 10.3 %collective-permute-start.2 = (bf16[320,128]{1,0:T(8,128)(2,1)}, bf16[320,128]{1,0:T(8,128)(2,1)S(1)}, u32[]{:S(2)}, u32[]{:S(2)}) collective-permute-start(bf16[320,128]{1,0:T(8,128)(2,1)} %bitcast.36), channel_id=1, source_target_pairs={{0,1},{1,2},{2,3},{3,0},{4,5},{5,6},{6,7},{7,4},{8,9},{9,10},{10,1... | collective-permute-start | bytes 245768 | tf_op jit(solution)/shard_map/ppermute | solution.py:684
  32.9 8.9 %collective-permute-start.3 = (bf16[320,128]{1,0:T(8,128)(2,1)}, bf16[320,128]{1,0:T(8,128)(2,1)S(1)}, u32[]{:S(2)}, u32[]{:S(2)}) collective-permute-start(bf16[320,128]{1,0:T(8,128)(2,1)} %bitcast.34), channel_id=1, source_target_pairs={{0,2},{1,3},{2,0},{3,1},{4,6},{5,7},{6,4},{7,5},{8,10},{9,11},{10,... | collective-permute-start | bytes 245768 | tf_op jit(solution)/shard_map/ppermute | solution.py:684
  35.5 6.3 %collective-permute-start.4 = (bf16[320,128]{1,0:T(8,128)(2,1)}, bf16[320,128]{1,0:T(8,128)(2,1)S(1)}, u32[]{:S(2)}, u32[]{:S(2)}) collective-permute-start(bf16[320,128]{1,0:T(8,128)(2,1)} %bitcast.33), channel_id=1, source_target_pairs={{0,3},{1,0},{2,1},{3,2},{4,7},{5,4},{6,5},{7,6},{8,11},{9,8},{10,9... | collective-permute-start | bytes 245768 | tf_op jit(solution)/shard_map/ppermute | solution.py:684
  43.9 3.3 %collective-permute-start.7 = (bf16[320,128]{1,0:T(8,128)(2,1)S(1)}, bf16[320,128]{1,0:T(8,128)(2,1)S(1)}, u32[]{:S(2)}, u32[]{:S(2)}) collective-permute-start(bf16[320,128]{1,0:T(8,128)(2,1)S(1)} %get-tuple-element.31), channel_id=1, source_target_pairs={{0,3},{1,0},{2,1},{3,2},{4,7},{5,4},{6,5},{7,6},{8,11},{9,8},{10,9... | collective-permute-start | bytes 245768 | tf_op jit(solution)/shard_map/ppermute | solution.py:684
  44.6 4.8 %collective-permute-start.6 = (bf16[320,128]{1,0:T(8,128)(2,1)S(1)}, bf16[320,128]{1,0:T(8,128)(2,1)S(1)}, u32[]{:S(2)}, u32[]{:S(2)}) collective-permute-start(bf16[320,128]{1,0:T(8,128)(2,1)S(1)} %get-tuple-element.31), channel_id=1, source_target_pairs={{0,2},{1,3},{2,0},{3,1},{4,6},{5,7},{6,4},{7,5},{8,10},{9,11},{10,... | collective-permute-start | bytes 245768 | tf_op jit(solution)/shard_map/ppermute | solution.py:684
  46.1 5.1 %collective-permute-start.5 = (bf16[320,128]{1,0:T(8,128)(2,1)S(1)}, bf16[320,128]{1,0:T(8,128)(2,1)S(1)}, u32[]{:S(2)}, u32[]{:S(2)}) collective-permute-start(bf16[320,128]{1,0:T(8,128)(2,1)S(1)} %get-tuple-element.31), channel_id=1, source_target_pairs={{0,1},{1,2},{2,3},{3,0},{4,5},{5,6},{6,7},{7,4},{8,9},{9,10},{10,1... | collective-permute-start | bytes 245768 | tf_op jit(solution)/shard_map/ppermute | solution.py:684
  51.2 0.7 copy-start.7
  51.9 11.9 %copy-start.3 = (f32[1,64,2,128]{3,2,1,0:T(2,128)S(1)}, f32[1,64,2,128]{3,2,1,0:T(2,128)}, u32[]{:S(2)}) copy-start(f32[1,64,2,128]{3,2,1,0:T(2,128)} %param.15) | copy-start | bytes 196612
  51.9 11.9 %copy-start.5 = (s32[1,64]{1,0:T(1,128)S(1)}, s32[1,64]{1,0:T(1,128)}, u32[]{:S(2)}) copy-start(s32[1,64]{1,0:T(1,128)} %count_ref.5) | copy-start | bytes 772
  51.9 24.1 %copy-start.1 = (bf16[5,256,256]{2,1,0:T(8,128)(2,1)S(1)}, bf16[5,256,256]{2,1,0:T(8,128)(2,1)}, u32[]{:S(2)}) copy-start(bf16[5,256,256]{2,1,0:T(8,128)(2,1)} %constant.19.clone.t_hbm.t_ref) | copy-start | bytes 1966084
  51.9 24.1 %copy-start.8 = (s32[3]{0:T(128)S(1)}, s32[3]{0:T(128)}, u32[]{:S(2)}) copy-start(s32[3]{0:T(128)} %copy-done.6) | copy-start | bytes 40
  56.4 30.7 %collective-permute-start.8 = (bf16[16,64,256]{2,1,0:T(8,128)(2,1)}, bf16[16,64,256]{2,1,0:T(8,128)(2,1)S(1)}, u32[]{:S(2)}, u32[]{:S(2)}) collective-permute-start(bf16[16,64,256]{2,1,0:T(8,128)(2,1)} %get-tuple-element.33), channel_id=1, source_target_pairs={{0,4},{4,8},{8,12},{12,16},{16,20},{20,24},{24,28},{28,32},{32,36}... | collective-permute-start | bytes 1572872 | tf_op jit(solution)/shard_map/ppermute | solution.py:711
  61.8 25.2 %collective-permute-start.9 = (bf16[16,64,256]{2,1,0:T(8,128)(2,1)}, bf16[16,64,256]{2,1,0:T(8,128)(2,1)}, u32[]{:S(2)}, u32[]{:S(2)}) collective-permute-start(bf16[16,64,256]{2,1,0:T(8,128)(2,1)} %get-tuple-element.34), channel_id=1, source_target_pairs={{4,0},{8,4},{12,8},{16,12},{20,16},{24,20},{28,24},{32,28},{36,32}... | collective-permute-start | bytes 1572872 | tf_op jit(solution)/shard_map/ppermute | solution.py:712
  64.4 21.4 %all-to-all-start.1 = ((f32[64,2,128]{2,1,0:T(2,128)}), f32[64,2,128]{2,1,0:T(2,128)S(1)}, u32[]{:S(2)}, u32[]{:S(2)}) async-start(f32[64,2,128]{2,1,0:T(2,128)} %get-tuple-element.35), calls=%async_computation.1 | async-start | bytes 131072 | tf_op jit(solution)/shard_map/all_to_all | solution.py:765

commit v4 on v3

--- a/solution.py
+++ b/solution.py
@@ -15,7 +15,7 @@
 SWEEP_SCALE = 0.2**SWEEPS
 HALF = SWEEPS * NY
 
-CONTROL_STEP = 8.0 / 32704.0
+CONTROL_STEP = 2.0**-12
 INNOVATION_STEP = 1.5 / 32700.0
 WEIGHT_STEP = 10.0 / 32700.0
 
@@ -95,11 +95,11 @@
     return pl.CostEstimate(flops=flops, bytes_accessed=bytes_accessed, transcendentals=0)
 
 
-ENCODE_STEP = 4
+ENCODE_STEP = 2
 
 
 def encode_kernel(
-    count_ref,
+    count_hbm,
     x_hbm,
     channel_hbm,
     innovation_hbm,
@@ -107,6 +107,7 @@
     low_hbm,
     high_hbm,
     packed_hbm,
+    count_ref,
     x_ref,
     channel_ref,
     innovation_ref,
@@ -128,6 +129,7 @@
         return pltpu.make_async_copy(source.at[at], target.at[at], sems.at[turn])
 
     obs_loads = [
+        pltpu.make_async_copy(count_hbm, count_ref, obs_sems.at[3]),
         pltpu.make_async_copy(channel_hbm, channel_ref, obs_sems.at[0]),
         pltpu.make_async_copy(innovation_hbm, innovation_ref, obs_sems.at[1]),
         pltpu.make_async_copy(weight_hbm, weight_ref, obs_sems.at[2]),
@@ -142,7 +144,8 @@
     def encode_chunk(turn):
         chunk(x_hbm, x_ref, in_sems, turn).wait()
         at = slice(turn * ENCODE_STEP, (turn + 1) * ENCODE_STEP)
-        coded = jnp.round(x_ref[at] * (1.0 / CONTROL_STEP)).astype(I32).astype(I16)
+        coded = jnp.minimum(jnp.round(x_ref[at] * (1.0 / CONTROL_STEP)), 32767.0)
+        coded = coded.astype(I32).astype(I16)
         low_ref[at] = coded[:, :, :HALF]
         high_ref[at] = coded[:, :, HALF:]
         for source, target, sems in (
@@ -180,9 +183,10 @@
     return pl.pallas_call(
         encode_kernel,
         out_shape=(pltpu.HBM(half, I16), pltpu.HBM(half, I16), pltpu.HBM(packed, I16)),
-        in_specs=[SMEM, HBM, HBM, HBM, HBM],
+        in_specs=[HBM] * 5,
         out_specs=(HBM, HBM, HBM),
         scratch_shapes=[
+            pltpu.SMEM(counts.shape, I32),
             pltpu.VMEM(control.shape, F32),
             pltpu.VMEM(channel.shape, I32),
             pltpu.VMEM(channel.shape, F32),
@@ -191,7 +195,7 @@
             pltpu.VMEM(half, I16),
             pltpu.VMEM(packed, I16),
             pltpu.SemaphoreType.DMA((turns,)),
-            pltpu.SemaphoreType.DMA((3,)),
+            pltpu.SemaphoreType.DMA((4,)),
             pltpu.SemaphoreType.DMA((turns,)),
             pltpu.SemaphoreType.DMA((turns,)),
             pltpu.SemaphoreType.DMA,
@@ -199,7 +203,7 @@
         compiler_params=params(),
         cost_estimate=cost(4 * control.size, 6 * control.size),
         name="encode",
-    )(counts, *[in_hbm(x) for x in (control, channel, innovation, weight)])
+    )(*[in_hbm(x) for x in (counts, control, channel, innovation, weight)])
 
 
 def depart_kernel(count_ref, evolved_ref, innovation_ref, o_ref):
@@ -222,56 +226,39 @@
     )(counts, evolved, innovation)
 
 
-def sweep_rows(edge_ref, x_ref, t_ref, o_ref, step, ready):
-    def apply(high, low, index):
-        return mm(high, t_ref[index]) + mm(low, t_ref[index])
+def sweep_own_kernel(place_ref, x_ref, t_ref, o_ref):
+    members, levels, _ = x_ref.shape
+    step = 4
+    rows = step * levels
 
     def one(turn, carry):
-        ready(turn)
-        at = pl.ds(pl.multiple_of(turn * step, step), step)
-        left_high, left_low = split_high_low(x_ref[at, :HALF] * SWEEP_SCALE)
-        right_high, right_low = split_high_low(x_ref[at, HALF:] * SWEEP_SCALE)
-        o_ref[at, :HALF] = apply(left_high, left_low, edge_ref[0]) + apply(
-            right_high, right_low, 4
-        )
-        o_ref[at, HALF:] = apply(right_high, right_low, edge_ref[1]) + apply(
-            left_high, left_low, 3
-        )
+        at = pl.ds(turn * step, step)
+        left_high, left_low = split_high_low(x_ref[at, :, :HALF].reshape(rows, HALF))
+        right_high, right_low = split_high_low(x_ref[at, :, HALF:].reshape(rows, HALF))
+
+        def apply(high, low, index):
+            return mm(high, t_ref[index]) + mm(low, t_ref[index])
+
+        left = apply(left_high, left_low, place_ref[0]) + apply(right_high, right_low, 4)
+        right = apply(right_high, right_low, place_ref[1]) + apply(left_high, left_low, 3)
+        shape = (step, levels, HALF)
+        o_ref[at, :, :HALF] = (left * SWEEP_SCALE).reshape(shape)
+        o_ref[at, :, HALF:] = (right * SWEEP_SCALE).reshape(shape)
         return carry
 
-    lax.fori_loop(0, x_ref.shape[0] // step, one, 0)
-
-
-def sweep_near_kernel(edge_ref, x_ref, t_ref, o_ref):
-    sweep_rows(edge_ref, x_ref, t_ref, o_ref, 256, lambda turn: None)
-
-
-def sweep_far_kernel(edge_ref, x_hbm, t_ref, o_ref, x_ref, sems):
-    rows = x_hbm.shape[0]
-    step = 256
-
-    def load(turn):
-        at = pl.ds(turn * step, step)
-        return pltpu.make_async_copy(x_hbm.at[at], x_ref.at[at], sems.at[turn])
-
-    for turn in range(rows // step):
-        load(turn).start()
-    sweep_rows(edge_ref, x_ref, t_ref, o_ref, step, lambda turn: load(turn).wait())
-
-
-def sweep_own(edges, field, matrices, far):
-    rows, columns = field.shape
-    scratch = [pltpu.VMEM(field.shape, F32), pltpu.SemaphoreType.DMA((rows // 256,))]
+    lax.fori_loop(0, members // step, one, 0)
+
+
+def sweep_own(place, field, matrices):
     return pl.pallas_call(
-        sweep_far_kernel if far else sweep_near_kernel,
-        out_shape=jax.ShapeDtypeStruct((rows, columns), F32),
-        in_specs=[SMEM, HBM if far else VMEM, VMEM],
+        sweep_own_kernel,
+        out_shape=jax.ShapeDtypeStruct(field.shape, F32),
+        in_specs=[SMEM, VMEM, VMEM],
         out_specs=VMEM,
-        scratch_shapes=scratch if far else [],
         compiler_params=params(),
-        cost_estimate=cost(2 * 6 * rows * columns * HALF, 10 * rows * columns),
+        cost_estimate=cost(2 * 4 * field.size * HALF, 10 * field.size),
         name="sweep_own",
-    )(edges, in_hbm(field) if far else field, matrices)
+    )(place, in_vmem(field), matrices)
 
 
 LEVEL_STEP = 16
@@ -301,8 +288,10 @@
     three_hbm,
     ens_ref,
     t_ref,
-    w_even,
-    w_odd,
+    near_left,
+    near_right,
+    w_left,
+    w_right,
     o_ref,
     in_sems,
     t_sem,
@@ -318,56 +307,66 @@
     for turn in range(turns):
         load(turn).start()
 
-    def apply(high, low, index):
-        return mm(high, t_ref[index]) + mm(low, t_ref[index])
-
-    def weigh(turn, w_ref):
-        at = pl.ds(turn * step, step)
-        rows = members * step
-        left_high, left_low = split_high_low(x_ref[:, at, :HALF].reshape(rows, HALF))
-        right_high, right_low = split_high_low(x_ref[:, at, HALF:].reshape(rows, HALF))
-
-        def from_halo(halo_ref, index):
-            coded = halo_ref[:, at, :].reshape(rows, HALF).astype(I32)
-            upper = (coded >> 8).astype(F32).astype(BF16)
-            lower = (coded & 255).astype(F32).astype(BF16)
-            return (mm(upper, t_ref[index]) * 256.0 + mm(lower, t_ref[index])) * CONTROL_STEP
-
-        left = (
-            apply(left_high, left_low, place_ref[0])
-            + apply(right_high, right_low, 4)
-            + from_halo(low_ref, 3)
-        )
-        right = (
-            apply(right_high, right_low, place_ref[1])
-            + apply(left_high, left_low, 3)
-            + from_halo(high_ref, 4)
-        )
-        left, right = left * SWEEP_SCALE, right * SWEEP_SCALE
-        w_ref[:, :, :HALF] = left.astype(BF16).reshape(members, step, HALF)
-        w_ref[:, :, HALF:] = right.astype(BF16).reshape(members, step, HALF)
-
-    def total_up(turn, w_ref):
-        at = pl.ds(turn * step, step)
-        for k in range(blocks):
-            across = slice(k * width, (k + 1) * width)
-            totals = [None] * variables
-            for m in range(members):
-                weight = w_ref[m, :, across].astype(F32)
-                for v in range(variables):
-                    term = weight * ens_ref[m, v, at, across].astype(F32)
-                    totals[v] = term if totals[v] is None else totals[v] + term
+    def twice(index):
+        return jnp.concatenate([t_ref[index], t_ref[index]], axis=0)
+
+    rows = step * members
+    group = members // 2
+    half_rows = step * group
+
+    def pair_of(values):
+        return jnp.concatenate(split_high_low(values), axis=1)
+
+    def split_near(turn):
+        at = pl.ds(pl.multiple_of(turn * step, step), step)
+        near_left[...] = pair_of(x_ref[:, at, :HALF].reshape(rows, HALF))
+        near_right[...] = pair_of(x_ref[:, at, HALF:].reshape(rows, HALF))
+
+    def weigh(turn, right_side, piece):
+        at = pl.ds(pl.multiple_of(turn * step, step), step)
+        among = slice(piece * group, (piece + 1) * group)
+        these = slice(piece * half_rows, (piece + 1) * half_rows)
+        left, right = near_left[these], near_right[these]
+        halo_ref, w_ref = (high_ref, w_right) if right_side else (low_ref, w_left)
+        beyond = halo_ref[among, at, :].reshape(half_rows, HALF).astype(I32).astype(F32)
+        beyond = pair_of(beyond)
+        if right_side:
+            new = mm(right, twice(place_ref[1])) + mm(left, twice(3)) + mm(beyond, twice(6))
+        else:
+            new = mm(left, twice(place_ref[0])) + mm(right, twice(4)) + mm(beyond, twice(5))
+        w_ref[among] = (new * SWEEP_SCALE).astype(BF16).reshape(group, step, HALF)
+
+    def total_up(turn, w_ref, k):
+        at = pl.ds(pl.multiple_of(turn * step, step), step)
+        across = slice(k * width, (k + 1) * width)
+        within = slice(k * width % HALF, k * width % HALF + width)
+        totals = [None] * variables
+        for m in range(members):
+            weight = w_ref[m, :, within].astype(F32)
             for v in range(variables):
-                o_ref[k, v, at, :] = (totals[v] * scale).astype(BF16)
-
-    buffers = [w_even, w_odd]
+                term = weight * ens_ref[m, v, at, across].astype(F32)
+                totals[v] = term if totals[v] is None else totals[v] + term
+        for v in range(variables):
+            o_ref[k, v, at, :] = (totals[v] * scale).astype(BF16)
+
+    split_near(0)
     t_load.wait()
-    weigh(0, buffers[0])
-    for turn in range(turns):
+    for piece in range(2):
+        weigh(0, False, piece)
+
+    def one(turn, carry):
         load(turn).wait()
-        if turn + 1 < turns:
-            weigh(turn + 1, buffers[(turn + 1) % 2])
-        total_up(turn, buffers[turn % 2])
+        for piece in range(2):
+            weigh(turn, True, piece)
+            total_up(turn, w_left, piece)
+        later = jnp.minimum(turn + 1, turns - 1)
+        split_near(later)
+        for piece in range(2):
+            weigh(later, False, piece)
+            total_up(turn, w_right, blocks // 2 + piece)
+        return carry
+
+    lax.fori_loop(0, turns, one, 0)
     mine = place_ref[2]
     copies = [
         pltpu.make_async_copy(o_ref.at[lax.rem(mine + s, blocks)], target, out_sems.at[s])
@@ -392,8 +391,10 @@
         scratch_shapes=[
             pltpu.VMEM(ensemble.shape, BF16),
             pltpu.VMEM(matrices.shape, BF16),
-            pltpu.VMEM((members, LEVEL_STEP, columns), BF16),
-            pltpu.VMEM((members, LEVEL_STEP, columns), BF16),
+            pltpu.VMEM((members * LEVEL_STEP, 2 * HALF), BF16),
+            pltpu.VMEM((members * LEVEL_STEP, 2 * HALF), BF16),
+            pltpu.VMEM((members, LEVEL_STEP, HALF), BF16),
+            pltpu.VMEM((members, LEVEL_STEP, HALF), BF16),
             pltpu.VMEM((blocks, variables, levels, width), BF16),
             pltpu.SemaphoreType.DMA((turns,)),
             pltpu.SemaphoreType.DMA,
@@ -415,7 +416,7 @@
 
 
 def obs_tables_kernel(
-    obs_ref, own_hbm, slots_hbm, w_ref, b_ref, channel_ref, own_ref, slots_ref, sems
+    obs_ref, own_hbm, slots_hbm, w_ref, b_ref, channel_ref, own_ref, hits_ref, slots_ref, sems
 ):
     copies = [
         pltpu.make_async_copy(own_hbm, own_ref, sems.at[0]),
@@ -429,7 +430,9 @@
     lane_id = lax.broadcasted_iota(I32, (width, width), 0).astype(F32).astype(BF16)
     one_bf, zero_bf = jnp.ones((), BF16), jnp.zeros((), BF16)
 
-    def one(owner, slot):
+    zeros = jnp.zeros((32, width), BF16)
+
+    def prepare(owner, slot):
         row = obs_ref[owner].astype(I32)[slot : slot + 1]
         channel = row[:, :width]
         innovation = row[:, width : 2 * width].astype(F32) * INNOVATION_STEP
@@ -445,26 +448,45 @@
             ]
 
         left = jnp.concatenate(spread(weight) + spread(weight * innovation), axis=0)
-        sums = mm_nt(left.astype(BF16), one_hot)
-        w_sum = sums[0:8] + sums[8:16]
-        b_sum = sums[16:24] + sums[24:32]
-        at = pl.ds(slot * owners + owner, 1)
-        channel_ref[at, :] = channel
-        for g in range(groups):
-            w_ref[g, at, :] = w_sum[g : g + 1]
-            b_ref[g, at, :] = b_sum[g : g + 1]
-
-    unroll = 4
+        return channel, one_hot, left.astype(BF16)
+
+    def pair(owner):
+        first, second = prepare(owner, 0), prepare(owner, 1)
+        left = jnp.concatenate(
+            [
+                jnp.concatenate([first[2], zeros], axis=1),
+                jnp.concatenate([zeros, second[2]], axis=1),
+            ],
+            axis=0,
+        )
+        one_hot = jnp.concatenate([first[1], second[1]], axis=1)
+        both = mm_nt(left, one_hot)
+        for slot, channel in enumerate((first[0], second[0])):
+            sums = both[32 * slot : 32 * (slot + 1)]
+            w_sum = sums[0:8] + sums[8:16]
+            b_sum = sums[16:24] + sums[24:32]
+            at = pl.ds(slot * owners + owner, 1)
+            channel_ref[at, :] = channel
+            for g in range(groups):
+                w_ref[g, at, :] = w_sum[g : g + 1]
+                b_ref[g, at, :] = b_sum[g : g + 1]
+
+    unroll = 16
 
     def several(turn, carry):
         for inner in range(unroll):
-            for slot in range(slots):
-                one(turn * unroll + inner, slot)
+            pair(turn * unroll + inner)
         return carry
 
     lax.fori_loop(0, owners // unroll, several, 0)
     for copy in copies:
         copy.wait()
+    table = jnp.concatenate([slots_ref[j : j + 1, :] for j in range(slots)], axis=1)
+    columns, rows = hits_ref.shape[1:]
+    column_id = lax.broadcasted_iota(I32, (columns, rows), 0)
+    hits = jnp.where(column_id == jnp.broadcast_to(table, (columns, rows)), 1.0, 0.0)
+    hits_ref[0] = hits.astype(BF16)
+    hits_ref[1] = hits.T.astype(BF16)
 
 
 def obs_tables(obs, own, columns, channels):
@@ -479,11 +501,11 @@
             shape,
             jax.ShapeDtypeStruct((rows, width), I32),
             jax.ShapeDtypeStruct(own.shape, own.dtype),
-            jax.ShapeDtypeStruct(columns.shape, columns.dtype),
+            jax.ShapeDtypeStruct((2, own.shape[1], rows), BF16),
         ),
         in_specs=[VMEM, HBM, HBM],
         out_specs=(VMEM,) * 5,
-        scratch_shapes=[pltpu.SemaphoreType.DMA((2,))],
+        scratch_shapes=[pltpu.VMEM(columns.shape, I32), pltpu.SemaphoreType.DMA((2,))],
         compiler_params=params(),
         cost_estimate=cost(2 * 32 * rows * width * width, 10 * rows * channels),
         name="obs_tables",
@@ -495,7 +517,7 @@
     one_ref,
     two_ref,
     three_ref,
-    slots_ref,
+    hits_ref,
     jac_ref,
     w_ref,
     b_ref,
@@ -505,17 +527,12 @@
 ):
     groups, rows, width = w_ref.shape
     state = jac_ref.shape[0]
-    slots, owners = slots_ref.shape
+    owners, slots, _ = evolved_ref.shape
     total = own_ref[...].astype(F32)
     for part in (one_ref, two_ref, three_ref):
         total = total + part[...].astype(F32)
     increment = total.astype(BF16)
-    columns = increment.shape[1]
-    column_id = lax.broadcasted_iota(I32, (columns, rows), 0)
-    table = jnp.concatenate([slots_ref[j : j + 1, :] for j in range(slots)], axis=1)
-    hits = jnp.where(column_id == jnp.broadcast_to(table, (columns, rows)), 1.0, 0.0)
-    hits = hits.astype(BF16)
-    carried = mm(increment, hits).T.astype(BF16)
+    carried = mm_nt(hits_ref[1], increment).astype(BF16)
     column_adjoint = jnp.zeros((rows, state), F32)
     channel = channel_ref[...]
     group, lane = channel >> 7, channel & 127
@@ -528,12 +545,12 @@
         taken = jnp.take_along_axis(model, lane, axis=1)
         picked = jnp.where(group == g, taken, picked)
     rounded = column_adjoint.T.astype(BF16)
-    adj_ref[...] = mm_nt(rounded, hits).astype(BF16)
+    adj_ref[...] = mm_nt(rounded, hits_ref[0]).astype(BF16)
     for j in range(slots):
         evolved_ref[:, j, :] = picked[j * owners : (j + 1) * owners]
 
 
-def observe(pieces, slots, jacobian, w_table, b_table, channel):
+def observe(pieces, hits, jacobian, w_table, b_table, channel, owners):
     state, width = pieces[0].shape
     channels = jacobian.shape[1]
     rows = channel.shape[0]
@@ -541,14 +558,14 @@
         observe_kernel,
         out_shape=(
             jax.ShapeDtypeStruct((state, width), BF16),
-            jax.ShapeDtypeStruct((slots.shape[1], slots.shape[0], width), F32),
+            jax.ShapeDtypeStruct((owners, rows // owners, width), F32),
         ),
         in_specs=[VMEM] * 9,
         out_specs=(VMEM, VMEM),
         compiler_params=params(),
         cost_estimate=cost(4 * rows * state * channels, 12 * rows * channels),
         name="observe",
-    )(*pieces, slots, jacobian, w_table, b_table, channel)
+    )(*pieces, hits, jacobian, w_table, b_table, channel)
 
 
 def member_adjoint_kernel(
@@ -646,34 +663,59 @@
     )(place, in_hbm(ensemble), *pieces)
 
 
-def add_halo_kernel(own_ref, low_ref, high_ref, t_ref, o_ref):
-    i = pl.program_id(0)
-    members = o_ref.shape[0]
-    levels = o_ref.shape[1]
-    rows = members * levels
-    at = pl.ds(i * members, members)
-
-    def from_halo(halo_ref, index):
-        halo = mm(halo_ref[at].reshape(rows, HALF), t_ref[index]) * SWEEP_SCALE
-        return halo.reshape(members, levels, HALF)
-
-    o_ref[:, :, :HALF] = own_ref[at, :, :HALF] + from_halo(low_ref, 3)
-    o_ref[:, :, HALF:] = own_ref[at, :, HALF:] + from_halo(high_ref, 4)
+def add_halo_kernel(
+    own_ref, low_ref, high_hbm, t_ref, o_hbm, high_ref, o_ref, high_sem, low_sems, high_sems
+):
+    members, levels, _ = own_ref.shape
+    step = 4
+    rows = step * levels
+    turns = members // step
+    load = pltpu.make_async_copy(high_hbm, high_ref, high_sem)
+    load.start()
+
+    def save(turn, across, sems):
+        at = pl.ds(turn * step, step)
+        return pltpu.make_async_copy(
+            o_ref.at[at, :, across], o_hbm.at[at, :, across], sems.at[turn]
+        )
+
+    def half(halo_ref, across, index, sems):
+        def one(turn, carry):
+            at = pl.ds(turn * step, step)
+            halo = mm(halo_ref[at].reshape(rows, HALF), t_ref[index]) * SWEEP_SCALE
+            o_ref[at, :, across] = own_ref[at, :, across] + halo.reshape(step, levels, HALF)
+            save(turn, across, sems).start()
+            return carry
+
+        lax.fori_loop(0, turns, one, 0)
+
+    lower, upper = pl.ds(0, HALF), pl.ds(HALF, HALF)
+    half(low_ref, lower, 3, low_sems)
+    load.wait()
+    half(high_ref, upper, 4, high_sems)
+    for turn in range(turns):
+        save(turn, lower, low_sems).wait()
+        save(turn, upper, high_sems).wait()
 
 
 def add_halo(own, from_low, from_high, matrices):
-    members, levels, columns = own.shape
-    step = 4
+    members = own.shape[0]
     return pl.pallas_call(
         add_halo_kernel,
-        out_shape=jax.ShapeDtypeStruct(own.shape, F32),
-        grid=(members // step,),
-        in_specs=[VMEM] * 4,
-        out_specs=pl.BlockSpec((step, levels, columns), lambda i: (i, 0, 0)),
+        out_shape=pltpu.HBM(own.shape, F32),
+        in_specs=[VMEM, VMEM, HBM, VMEM],
+        out_specs=HBM,
+        scratch_shapes=[
+            pltpu.VMEM(from_high.shape, BF16),
+            pltpu.VMEM(own.shape, F32),
+            pltpu.SemaphoreType.DMA,
+            pltpu.SemaphoreType.DMA((members // 4,)),
+            pltpu.SemaphoreType.DMA((members // 4,)),
+        ],
         compiler_params=params(),
         cost_estimate=cost(2 * own.size * HALF, 10 * own.size),
         name="add_halo",
-    )(own, in_vmem(from_low), in_vmem(from_high), matrices)
+    )(own, in_vmem(from_low), in_hbm(from_high), matrices)
 
 
 def to_members(pieces):
@@ -732,7 +774,10 @@
     width = columns // groups
     channels = jacobian.shape[0]
     tile_index = lax.axis_index("tile")
-    matrices = jnp.asarray(sweep_matrices())
+    near = sweep_matrices()
+    matrices = jnp.asarray(near)
+    scaled = np.concatenate([near, (near[3:].astype(np.float32) * CONTROL_STEP).astype(near.dtype)])
+    matrices_with_halo = jnp.asarray(scaled)
     place = jnp.stack(
         [
             jnp.where(tile_index == 0, 0, 1),
@@ -746,19 +791,22 @@
     )
     from_low, from_high = swap_halos(low_half, high_half)
     obs = lax.all_to_all(packed, "tile", split_axis=0, concat_axis=0, tiled=True)
-    pieces = localize_sum(place, control, from_low, from_high, ensemble, matrices, scale, groups)
+    pieces = localize_sum(
+        place, control, from_low, from_high, ensemble, matrices_with_halo, scale, groups
+    )
     pieces = [piece.reshape(state, width) for piece in pieces]
     received = to_members(pieces[1:])
-    w_table, b_table, channel, own, carried = obs_tables(
+    w_table, b_table, channel, own, hits = obs_tables(
         obs, pieces[0], jnp.transpose(send_columns[0]), channels
     )
     block_adjoint, evolved = observe(
         [own] + received,
-        carried,
+        hits,
         jnp.transpose(jacobian),
         w_table,
         b_table,
         channel,
+        owners,
     )
     adjoint = [block_adjoint] + to_members([block_adjoint] * (groups - 1))
     adjoint = [piece.reshape(variables, levels, width) for piece in adjoint]
@@ -766,10 +814,10 @@
     kept = keep_filled(counts, innovation[0])
     full, low_half, high_half = member_adjoint(place, ensemble, adjoint, scale)
     from_low, from_high = swap_halos(low_half, high_half)
-    own = sweep_own(place, full.reshape(members * levels, columns), matrices, True)
+    own = sweep_own(place, full, matrices)
     departures = depart(counts, evolved, kept)
     gradient = add_halo(
-        own.reshape(members, levels, columns), from_low, from_high, matrices
+        own, from_low, from_high, matrices
     )
     return gradient, departures[None]
 

time: 90.8 us -> 87.6 us (0.965)
  Pallas kernels: 30.3 us -> 26.3 us
  starting transfers between devices: 46.2 us -> 47.7 us
  waiting for transfers between devices: 11.5 us -> 10 us
    pallas_call x1, Pallas kernels: 5.19 us -> 3.06 us  [obs_tables(): pl.pallas_call(obs_tables_kernel, out_shape=(shape, shape, jax.ShapeDtype...]
    pallas_call x2, Pallas kernels: 6.77 us -> 4.93 us  [the longest x1 2.59 us: add_halo(): pl.pallas_call(add_halo_kernel, out_shape=pltpu.HBM(own.shape, F32), in_s...]
    ppermute x2, starting transfers between devices: 10.4 us -> 11.5 us  [swap_halos(): from_low = lax.ppermute(high_half, 'tile', forward)]
    all_to_all x1, waiting for transfers between devices: 6.33 us -> 5.22 us  [body(): lax.all_to_all(evolved, 'tile', split_axis=0, concat_axis=0, tiled=True)]
  transfers between devices with their start and end apart: 12 -> 12, of which waited for: 4 -> 4; matrix products, arithmetic and copies ran while one was open for 0% -> 0% of each run, Pallas kernels for 19% -> 17%
where the time goes in v4:
time: 87.6 us; the launch traced here: 87.2 us
  starting transfers between devices  47.7 us (54%)
  Pallas kernels  26.3 us (30%)
  waiting for transfers between devices  10 us (11%)
  local copies, waits for them, and re-layouts  2.27 us (3%)
    all_to_all x1, starting transfers between devices, body(): lax.all_to_all(packed, 'tile', split_axis=0, concat_axis=0, tiled=True)  13.1 us
    all_to_all x1, starting transfers between devices, body(): lax.all_to_all(evolved, 'tile', split_axis=0, concat_axis=0, tiled=True)  11.6 us
    ppermute x2, starting transfers between devices, swap_halos(): from_low = lax.ppermute(high_half, 'tile', forward)  11.5 us
    ppermute x6, starting transfers between devices, to_members(): received.append(lax.ppermute(piece, 'mem', pairs))  7.69 us
    pallas_call x1, Pallas kernels, localize_sum(): pl.pallas_call(functools.partial(localize_sum_kernel, scale), out_shape=(...  7.34 us
    all_to_all x1, waiting for transfers between devices, body(): lax.all_to_all(evolved, 'tile', split_axis=0, concat_axis=0, tiled=True)  5.22 us
    ppermute x6, waiting for transfers between devices, to_members(): received.append(lax.ppermute(piece, 'mem', pairs))  4.77 us
    pallas_call x1, Pallas kernels, member_adjoint(): pl.pallas_call(functools.partial(member_adjoint_kernel, scale), out_shape...  4.44 us
  transfers between devices with their start and end apart: 12, of which 4 were waited for; matrix products, arithmetic and copies ran while one was open for 0% of the time, Pallas kernels for 17%

profile of v4, /device:TPU:1, one launch (start us, length us, event | category | flops | bytes accessed | tf_op | source)
XLA Modules:
  0.0 87.2 jit_solution(5121586486122661637)
XLA Ops:
  0.6 0.0 copy-start
  0.6 2.7 %encode.1 = (s16[16,64,256]{2,1,0:T(8,128)(2,1)}, s16[16,64,256]{2,1,0:T(8,128)(2,1)}, s16[64,2,384]{2,1,0:T(2,128)(2,1)}) custom-call(s32[1,64]{1,0:T(1,128)} %count_ref.3, f32[16,64,512]{2,1,0:T(8,128)} %x_ref.1, s32[64,2,128]{2,1,0:T(2,128)} %bitcast.26, f32[64,2,128]{2,1,0:T(2,128)} %bitcast.20, f32[64,2,128]{2,1,0:T(2,128)} %bitcast.27), custom_call_target="tpu_custom_call" | custom-call | flops 2097152 | bytes 3145728 | tf_op jit(solution)/shard_map/encode/pallas_call | solution.py:183
  3.3 4.9 %collective-permute-start = (s16[16,64,256]{2,1,0:T(8,128)(2,1)}, s16[16,64,256]{2,1,0:T(8,128)(2,1)S(1)}, u32[]{:S(2)}, u32[]{:S(2)}) collective-permute-start(s16[16,64,256]{2,1,0:T(8,128)(2,1)} %get-tuple-element.20), channel_id=1, source_target_pairs={{0,4},{4,8},{8,12},{12,16},{16,20},{20,24},{24,28},{28,32},{32,36}... | collective-permute-start | bytes 1572872 | tf_op jit(solution)/shard_map/ppermute | solution.py:753
  8.3 1.9 %collective-permute-start.1 = (s16[16,64,256]{2,1,0:T(8,128)(2,1)}, s16[16,64,256]{2,1,0:T(8,128)(2,1)S(1)}, u32[]{:S(2)}, u32[]{:S(2)}) collective-permute-start(s16[16,64,256]{2,1,0:T(8,128)(2,1)} %get-tuple-element.21), channel_id=1, source_target_pairs={{4,0},{8,4},{12,8},{16,12},{20,16},{24,20},{28,24},{32,28},{36,32}... | collective-permute-start | bytes 1572872 | tf_op jit(solution)/shard_map/ppermute | solution.py:754
  10.2 13.1 %all-to-all-start = ((s16[64,2,384]{2,1,0:T(2,128)(2,1)}), s16[64,2,384]{2,1,0:T(2,128)(2,1)}, u32[]{:S(2)}, u32[]{:S(2)}) async-start(s16[64,2,384]{2,1,0:T(2,128)(2,1)} %get-tuple-element.19), calls=%async_computation | async-start | bytes 196608 | tf_op jit(solution)/shard_map/all_to_all | solution.py:793
  23.3 0.1 pad_add_fusion.place_ref
  23.4 0.0 copy-start.5
  23.4 0.0 copy-start.3
  23.4 0.0 collective-permute-done.low_ref
  23.4 0.0 collective-permute-done.1.high_ref
  23.4 0.0 copy-done
  23.4 7.3 %localize_sum.1 = (bf16[5,64,128]{2,1,0:T(8,128)(2,1)}, bf16[5,64,128]{2,1,0:T(8,128)(2,1)}, bf16[5,64,128]{2,1,0:T(8,128)(2,1)}, bf16[5,64,128]{2,1,0:T(8,128)(2,1)}) custom-call(s32[3]{0:T(128)S(1)} %pad_add_fusion.place_ref, f32[16,64,512]{2,1,0:T(8,128)S(1)} %copy-done, s16[16,64,256]{2,1,0:T(8,128)(2,1)S(1)} %collective-permute-done.low_ref, ...), custom_call_target="tpu_custom_call" | custom-call | flops 1610612736 | bytes 9437184 | tf_op jit(solution)/shard_map/localize_sum/pallas_call | solution.py:386
  30.7 0.0 copy-done.5
  30.8 1.4 %collective-permute-start.2 = (bf16[320,128]{1,0:T(8,128)(2,1)}, bf16[320,128]{1,0:T(8,128)(2,1)S(1)}, u32[]{:S(2)}, u32[]{:S(2)}) collective-permute-start(bf16[320,128]{1,0:T(8,128)(2,1)} %bitcast.32), channel_id=1, source_target_pairs={{0,1},{1,2},{2,3},{3,0},{4,5},{5,6},{6,7},{7,4},{8,9},{9,10},{10,1... | collective-permute-start | bytes 245768 | tf_op jit(solution)/shard_map/ppermute | solution.py:726
  32.1 2.6 %collective-permute-start.3 = (bf16[320,128]{1,0:T(8,128)(2,1)}, bf16[320,128]{1,0:T(8,128)(2,1)S(1)}, u32[]{:S(2)}, u32[]{:S(2)}) collective-permute-start(bf16[320,128]{1,0:T(8,128)(2,1)} %bitcast.30), channel_id=1, source_target_pairs={{0,2},{1,3},{2,0},{3,1},{4,6},{5,7},{6,4},{7,5},{8,10},{9,11},{10,... | collective-permute-start | bytes 245768 | tf_op jit(solution)/shard_map/ppermute | solution.py:726
  34.8 1.1 %collective-permute-start.4 = (bf16[320,128]{1,0:T(8,128)(2,1)}, bf16[320,128]{1,0:T(8,128)(2,1)S(1)}, u32[]{:S(2)}, u32[]{:S(2)}) collective-permute-start(bf16[320,128]{1,0:T(8,128)(2,1)} %bitcast.29), channel_id=1, source_target_pairs={{0,3},{1,0},{2,1},{3,2},{4,7},{5,4},{6,5},{7,6},{8,11},{9,8},{10,9... | collective-permute-start | bytes 245768 | tf_op jit(solution)/shard_map/ppermute | solution.py:726
  35.8 0.0 all-to-all-done.obs_ref
  35.8 3.1 %obs_tables.1 = (f32[5,128,128]{2,1,0:T(8,128)S(1)}, f32[5,128,128]{2,1,0:T(8,128)S(1)}, s32[128,128]{1,0:T(8,128)S(1)}, bf16[320,128]{1,0:T(8,128)(2,1)S(1)}, bf16[2,128,128]{2,1,0:T(8,128)(2,1)S(1)}) custom-call(s16[64,2,384]{2,1,0:T(2,128)(2,1)} %all-to-all-done.obs_ref, bf16[320,128]{1,0:T(8,128)(2,1)} %bitcast.31, s32[2,64]{1,0:T(2,128)} %bitcast.33), custom_call_target="tpu_custom_call" | custom-call | flops 134217728 | bytes 819200 | tf_op jit(solution)/shard_map/obs_tables/pallas_call | solution.py:497
  38.9 0.0 collective-permute-done.2.one_ref
  38.9 0.0 collective-permute-done.3.two_ref
  38.9 0.0 collective-permute-done.4.three_ref
  38.9 0.0 copy-done.3
  38.9 2.0 %observe.1 = (bf16[320,128]{1,0:T(8,128)(2,1)S(1)}, f32[64,2,128]{2,1,0:T(2,128)}) custom-call(bf16[320,128]{1,0:T(8,128)(2,1)S(1)} %get-tuple-element.23.own_ref, bf16[320,128]{1,0:T(8,128)(2,1)S(1)} %collective-permute-done.2.one_ref, bf16[320,128]{1,0:T(8,128)(2,1)S(1)} %collective-permute-done.3.two_ref, ...), custom_call_target="tpu_custom_call" | custom-call | flops 104857600 | bytes 983040 | tf_op jit(solution)/shard_map/observe/pallas_call | solution.py:557
  41.0 1.7 %collective-permute-start.7 = (bf16[320,128]{1,0:T(8,128)(2,1)S(1)}, bf16[320,128]{1,0:T(8,128)(2,1)S(1)}, u32[]{:S(2)}, u32[]{:S(2)}) collective-permute-start(bf16[320,128]{1,0:T(8,128)(2,1)S(1)} %get-tuple-element.31), channel_id=1, source_target_pairs={{0,3},{1,0},{2,1},{3,2},{4,7},{5,4},{6,5},{7,6},{8,11},{9,8},{10,9... | collective-permute-start | bytes 245768 | tf_op jit(solution)/shard_map/ppermute | solution.py:726
  42.7 0.5 collective-permute-start.6
  43.1 0.4 collective-permute-start.5
  43.6 0.7 collective-permute-done.7
  44.2 3.3 %collective-permute-done.6 = bf16[320,128]{1,0:T(8,128)(2,1)S(1)} collective-permute-done((bf16[320,128]{1,0:T(8,128)(2,1)S(1)}, bf16[320,128]{1,0:T(8,128)(2,1)S(1)}, u32[]{:S(2)}, u32[]{:S(2)}) %collective-permute-start.6) | collective-permute-done | bytes 81952 | tf_op jit(solution)/shard_map/ppermute | solution.py:726
  47.5 0.8 collective-permute-done.5
  48.3 0.0 copy-start.6
  48.3 0.7 copy-done.6
  49.0 0.0 copy-start.4
  49.0 0.0 copy-start.8
  49.0 0.0 copy-start.1
  49.0 0.0 copy-start.7
  49.0 4.4 %member_adjoint.1 = (f32[16,64,512]{2,1,0:T(8,128)}, bf16[16,64,256]{2,1,0:T(8,128)(2,1)}, bf16[16,64,256]{2,1,0:T(8,128)(2,1)}) custom-call(s32[3]{0:T(128)S(1)} %copy-done.6, bf16[16,5,64,512]{3,2,1,0:T(8,128)(2,1)} %ens_hbm.3, bf16[5,64,128]{2,1,0:T(8,128)(2,1)S(1)} %bitcast.22, bf16[5,64,128]{2,1,0:T(8,128)(2,1)S(1)} %bitcast.25, ...), custom_call_target="tpu_custom_call" | custom-call | flops 5242880 | bytes 10485760 | tf_op jit(solution)/shard_map/member_adjoint/pallas_call | solution.py:644
  53.5 6.6 %collective-permute-start.8 = (bf16[16,64,256]{2,1,0:T(8,128)(2,1)}, bf16[16,64,256]{2,1,0:T(8,128)(2,1)S(1)}, u32[]{:S(2)}, u32[]{:S(2)}) collective-permute-start(bf16[16,64,256]{2,1,0:T(8,128)(2,1)} %get-tuple-element.33), channel_id=1, source_target_pairs={{0,4},{4,8},{8,12},{12,16},{16,20},{20,24},{24,28},{28,32},{32,36}... | collective-permute-start | bytes 1572872 | tf_op jit(solution)/shard_map/ppermute | solution.py:753
  60.1 1.9 %collective-permute-start.9 = (bf16[16,64,256]{2,1,0:T(8,128)(2,1)}, bf16[16,64,256]{2,1,0:T(8,128)(2,1)}, u32[]{:S(2)}, u32[]{:S(2)}) collective-permute-start(bf16[16,64,256]{2,1,0:T(8,128)(2,1)} %get-tuple-element.34), channel_id=1, source_target_pairs={{4,0},{8,4},{12,8},{16,12},{20,16},{24,20},{28,24},{32,28},{36,32}... | collective-permute-start | bytes 1572872 | tf_op jit(solution)/shard_map/ppermute | solution.py:754
  62.0 11.6 %all-to-all-start.1 = ((f32[64,2,128]{2,1,0:T(2,128)}), f32[64,2,128]{2,1,0:T(2,128)S(1)}, u32[]{:S(2)}, u32[]{:S(2)}) async-start(f32[64,2,128]{2,1,0:T(2,128)} %get-tuple-element.35), calls=%async_computation.1 | async-start | bytes 131072 | tf_op jit(solution)/shard_map/all_to_all | solution.py:813
  73.6 0.0 copy-done.4
  73.6 0.0 copy-done.8
  73.6 0.6 keep_filled.1.innovation_ref
  74.2 0.0 copy-done.1
  74.2 0.0 copy-done.7
  74.3 0.0 copy-start.2
  74.3 1.6 %copy-done.2 = f32[16,64,512]{2,1,0:T(8,128)S(1)} copy-done((f32[16,64,512]{2,1,0:T(8,128)S(1)}, f32[16,64,512]{2,1,0:T(8,128)}, u32[]{:S(2)}) %copy-start.2) | copy-done | bytes 2097176
  75.8 2.3 %sweep_own.1.own_ref = f32[16,64,512]{2,1,0:T(8,128)S(1)} custom-call(s32[3]{0:T(128)S(1)} %copy-done.7, f32[16,64,512]{2,1,0:T(8,128)S(1)} %copy-done.2, bf16[5,256,256]{2,1,0:T(8,128)(2,1)S(1)} %copy-done.1), custom_call_target="tpu_custom_call" | custom-call | flops 1073741824 | bytes 5242880 | tf_op jit(solution)/shard_map/sweep_own/pallas_call | solution.py:253
  78.2 5.2 %all-to-all-done.1.evolved_ref = f32[64,2,128]{2,1,0:T(2,128)S(1)} async-done(((f32[64,2,128]{2,1,0:T(2,128)}), f32[64,2,128]{2,1,0:T(2,128)S(1)}, u32[]{:S(2)}, u32[]{:S(2)}) %all-to-all-start.1) | async-done | bytes 65568 | tf_op jit(solution)/shard_map/all_to_all | solution.py:813
  83.4 1.2 %depart.1 = f32[64,2,128]{2,1,0:T(2,128)} custom-call(s32[1,64]{1,0:T(1,128)S(1)} %copy-done.8, f32[64,2,128]{2,1,0:T(2,128)S(1)} %all-to-all-done.1.evolved_ref, f32[64,2,128]{2,1,0:T(2,128)S(1)} %keep_filled.1.innovation_ref), custom_call_target="tpu_custom_call" | custom-call | flops 32768 | bytes 196608 | tf_op jit(solution)/shard_map/depart/pallas_call | solution.py:218
  84.6 0.0 collective-permute-done.8.low_ref
  84.6 0.0 collective-permute-done.9.high_hbm
  84.6 2.6 %add_halo.1 = f32[16,64,512]{2,1,0:T(8,128)} custom-call(f32[16,64,512]{2,1,0:T(8,128)S(1)} %sweep_own.1.own_ref, bf16[16,64,256]{2,1,0:T(8,128)(2,1)S(1)} %collective-permute-done.8.low_ref, bf16[16,64,256]{2,1,0:T(8,128)(2,1)} %collective-permute-done.9.high_hbm, bf16[5,256,256]{2,1,0:T(8,128)(2,1)S(1)} %copy-done.1), custom_call_target="tpu_custom_call" | custom-call | flops 268435456 | bytes 5242880 | tf_op jit(solution)/shard_map/add_halo/pallas_call | solution.py:703
Async XLA Ops:
  0.6 22.8 %copy-start = (f32[16,64,512]{2,1,0:T(8,128)S(1)}, f32[16,64,512]{2,1,0:T(8,128)}, u32[]{:S(2)}) copy-start(f32[16,64,512]{2,1,0:T(8,128)} %x_ref.1) | copy-start | bytes 6291460
  3.3 20.0 %collective-permute-start = (s16[16,64,256]{2,1,0:T(8,128)(2,1)}, s16[16,64,256]{2,1,0:T(8,128)(2,1)S(1)}, u32[]{:S(2)}, u32[]{:S(2)}) collective-permute-start(s16[16,64,256]{2,1,0:T(8,128)(2,1)} %get-tuple-element.20), channel_id=1, source_target_pairs={{0,4},{4,8},{8,12},{12,16},{16,20},{20,24},{24,28},{28,32},{32,36}... | collective-permute-start | bytes 1572872 | tf_op jit(solution)/shard_map/ppermute | solution.py:753
  8.3 15.1 %collective-permute-start.1 = (s16[16,64,256]{2,1,0:T(8,128)(2,1)}, s16[16,64,256]{2,1,0:T(8,128)(2,1)S(1)}, u32[]{:S(2)}, u32[]{:S(2)}) collective-permute-start(s16[16,64,256]{2,1,0:T(8,128)(2,1)} %get-tuple-element.21), channel_id=1, source_target_pairs={{4,0},{8,4},{12,8},{16,12},{20,16},{24,20},{28,24},{32,28},{36,32}... | collective-permute-start | bytes 1572872 | tf_op jit(solution)/shard_map/ppermute | solution.py:754
  10.2 25.6 %all-to-all-start = ((s16[64,2,384]{2,1,0:T(2,128)(2,1)}), s16[64,2,384]{2,1,0:T(2,128)(2,1)}, u32[]{:S(2)}, u32[]{:S(2)}) async-start(s16[64,2,384]{2,1,0:T(2,128)(2,1)} %get-tuple-element.19), calls=%async_computation | async-start | bytes 196608 | tf_op jit(solution)/shard_map/all_to_all | solution.py:793
  23.4 7.4 %copy-start.5 = (s32[3]{0:T(128)}, s32[3]{0:T(128)S(1)}, u32[]{:S(2)}) copy-start(s32[3]{0:T(128)S(1)} %pad_add_fusion.place_ref) | copy-start | bytes 40
  23.4 15.6 %copy-start.3 = (bf16[640,320]{0,1:T(8,128)(2,1)S(1)}, bf16[640,320]{0,1:T(8,128)(2,1)}, u32[]{:S(2)}) copy-start(bf16[640,320]{0,1:T(8,128)(2,1)} %param.12) | copy-start | bytes 1228804
  30.8 8.1 %collective-permute-start.2 = (bf16[320,128]{1,0:T(8,128)(2,1)}, bf16[320,128]{1,0:T(8,128)(2,1)S(1)}, u32[]{:S(2)}, u32[]{:S(2)}) collective-permute-start(bf16[320,128]{1,0:T(8,128)(2,1)} %bitcast.32), channel_id=1, source_target_pairs={{0,1},{1,2},{2,3},{3,0},{4,5},{5,6},{6,7},{7,4},{8,9},{9,10},{10,1... | collective-permute-start | bytes 245768 | tf_op jit(solution)/shard_map/ppermute | solution.py:726
  32.1 6.8 %collective-permute-start.3 = (bf16[320,128]{1,0:T(8,128)(2,1)}, bf16[320,128]{1,0:T(8,128)(2,1)S(1)}, u32[]{:S(2)}, u32[]{:S(2)}) collective-permute-start(bf16[320,128]{1,0:T(8,128)(2,1)} %bitcast.30), channel_id=1, source_target_pairs={{0,2},{1,3},{2,0},{3,1},{4,6},{5,7},{6,4},{7,5},{8,10},{9,11},{10,... | collective-permute-start | bytes 245768 | tf_op jit(solution)/shard_map/ppermute | solution.py:726
  34.8 4.2 %collective-permute-start.4 = (bf16[320,128]{1,0:T(8,128)(2,1)}, bf16[320,128]{1,0:T(8,128)(2,1)S(1)}, u32[]{:S(2)}, u32[]{:S(2)}) collective-permute-start(bf16[320,128]{1,0:T(8,128)(2,1)} %bitcast.29), channel_id=1, source_target_pairs={{0,3},{1,0},{2,1},{3,2},{4,7},{5,4},{6,5},{7,6},{8,11},{9,8},{10,9... | collective-permute-start | bytes 245768 | tf_op jit(solution)/shard_map/ppermute | solution.py:726
  41.0 3.3 %collective-permute-start.7 = (bf16[320,128]{1,0:T(8,128)(2,1)S(1)}, bf16[320,128]{1,0:T(8,128)(2,1)S(1)}, u32[]{:S(2)}, u32[]{:S(2)}) collective-permute-start(bf16[320,128]{1,0:T(8,128)(2,1)S(1)} %get-tuple-element.31), channel_id=1, source_target_pairs={{0,3},{1,0},{2,1},{3,2},{4,7},{5,4},{6,5},{7,6},{8,11},{9,8},{10,9... | collective-permute-start | bytes 245768 | tf_op jit(solution)/shard_map/ppermute | solution.py:726
  42.7 4.9 %collective-permute-start.6 = (bf16[320,128]{1,0:T(8,128)(2,1)S(1)}, bf16[320,128]{1,0:T(8,128)(2,1)S(1)}, u32[]{:S(2)}, u32[]{:S(2)}) collective-permute-start(bf16[320,128]{1,0:T(8,128)(2,1)S(1)} %get-tuple-element.31), channel_id=1, source_target_pairs={{0,2},{1,3},{2,0},{3,1},{4,6},{5,7},{6,4},{7,5},{8,10},{9,11},{10,... | collective-permute-start | bytes 245768 | tf_op jit(solution)/shard_map/ppermute | solution.py:726
  43.1 5.2 %collective-permute-start.5 = (bf16[320,128]{1,0:T(8,128)(2,1)S(1)}, bf16[320,128]{1,0:T(8,128)(2,1)S(1)}, u32[]{:S(2)}, u32[]{:S(2)}) collective-permute-start(bf16[320,128]{1,0:T(8,128)(2,1)S(1)} %get-tuple-element.31), channel_id=1, source_target_pairs={{0,1},{1,2},{2,3},{3,0},{4,5},{5,6},{6,7},{7,4},{8,9},{9,10},{10,1... | collective-permute-start | bytes 245768 | tf_op jit(solution)/shard_map/ppermute | solution.py:726
  48.3 0.7 copy-start.6
  49.0 24.6 %copy-start.4 = (f32[1,64,2,128]{3,2,1,0:T(2,128)S(1)}, f32[1,64,2,128]{3,2,1,0:T(2,128)}, u32[]{:S(2)}) copy-start(f32[1,64,2,128]{3,2,1,0:T(2,128)} %param.16) | copy-start | bytes 196612
  49.0 24.6 %copy-start.8 = (s32[1,64]{1,0:T(1,128)S(1)}, s32[1,64]{1,0:T(1,128)}, u32[]{:S(2)}) copy-start(s32[1,64]{1,0:T(1,128)} %count_ref.3) | copy-start | bytes 772
  49.0 25.2 %copy-start.1 = (bf16[5,256,256]{2,1,0:T(8,128)(2,1)S(1)}, bf16[5,256,256]{2,1,0:T(8,128)(2,1)}, u32[]{:S(2)}) copy-start(bf16[5,256,256]{2,1,0:T(8,128)(2,1)} %constant.21.clone.t_ref) | copy-start | bytes 1966084
  49.0 25.2 %copy-start.7 = (s32[3]{0:T(128)S(1)}, s32[3]{0:T(128)}, u32[]{:S(2)}) copy-start(s32[3]{0:T(128)} %copy-done.5) | copy-start | bytes 40
  53.5 31.2 %collective-permute-start.8 = (bf16[16,64,256]{2,1,0:T(8,128)(2,1)}, bf16[16,64,256]{2,1,0:T(8,128)(2,1)S(1)}, u32[]{:S(2)}, u32[]{:S(2)}) collective-permute-start(bf16[16,64,256]{2,1,0:T(8,128)(2,1)} %get-tuple-element.33), channel_id=1, source_target_pairs={{0,4},{4,8},{8,12},{12,16},{16,20},{20,24},{24,28},{28,32},{32,36}... | collective-permute-start | bytes 1572872 | tf_op jit(solution)/shard_map/ppermute | solution.py:753
  60.1 24.6 %collective-permute-start.9 = (bf16[16,64,256]{2,1,0:T(8,128)(2,1)}, bf16[16,64,256]{2,1,0:T(8,128)(2,1)}, u32[]{:S(2)}, u32[]{:S(2)}) collective-permute-start(bf16[16,64,256]{2,1,0:T(8,128)(2,1)} %get-tuple-element.34), channel_id=1, source_target_pairs={{4,0},{8,4},{12,8},{16,12},{20,16},{24,20},{28,24},{32,28},{36,32}... | collective-permute-start | bytes 1572872 | tf_op jit(solution)/shard_map/ppermute | solution.py:754
  62.0 21.4 %all-to-all-start.1 = ((f32[64,2,128]{2,1,0:T(2,128)}), f32[64,2,128]{2,1,0:T(2,128)S(1)}, u32[]{:S(2)}, u32[]{:S(2)}) async-start(f32[64,2,128]{2,1,0:T(2,128)} %get-tuple-element.35), calls=%async_computation.1 | async-start | bytes 131072 | tf_op jit(solution)/shard_map/all_to_all | solution.py:813
  74.3 1.6 %copy-start.2 = (f32[16,64,512]{2,1,0:T(8,128)S(1)}, f32[16,64,512]{2,1,0:T(8,128)}, u32[]{:S(2)}) copy-start(f32[16,64,512]{2,1,0:T(8,128)} %get-tuple-element.32.x_ref) | copy-start | bytes 6291460
